TPU v7x, 32 devices: a whole 2x2x4 slice. The times are simulated.
32 devices in a mesh: grp: 2 (over x), seq: 16 (over z, y, core).
Axes of the slice: x: 2, y: 2, z: 4, core: 2. Of those that a mesh axis runs over, the one named last changes fastest.
Arguments:
- feats: bfloat16 [32, 128, 384], P('seq', None, 'grp'), may hold values from -6 to 6
- conv_weight: bfloat16 [3, 128, 128], replicated, may hold values from -0.3125 to 0.3125
- conv_bias: float32 [128], replicated, may hold values from -3 to 3
- latent_projection_weight: bfloat16 [16, 128], replicated, may hold values from -0.75 to 0.75
- noise: bfloat16 [32, 16, 384], P('seq', None, 'grp'), may hold values from -6 to 6
- step_index: int32 [1], replicated, may hold values from 0 to 49
- hist: bfloat16 [128, 64], P('seq'), may hold values from -6 to 6
- hist_level: int32 [128], P('seq'), may hold values from 0 to 2
- hist_count: int32 [16], replicated, may hold values from 1 to 8, 96 in all
- w_in: bfloat16 [64, 3072], replicated, may hold values from -2 to 2
- w_hist: bfloat16 [3, 64, 3072], replicated, may hold values from -0.75 to 0.75
- norm_gain: float32 [3072], replicated, may hold values from 0.5 to 2
- w_query: bfloat16 [3072, 1536], P(None, 'grp'), may hold values from -2 to 2
- w_key: bfloat16 [3072, 1536], P(None, 'grp'), may hold values from -2 to 2
- w_value: bfloat16 [3072, 1536], P(None, 'grp'), may hold values from -0.109375 to 0.109375
- q_gain: float32 [128], replicated, may hold values from 0.5 to 6
- k_gain: float32 [128], replicated, may hold values from 0.5 to 6
- w_out: bfloat16 [1536, 3072], P('grp'), may hold values from -0.5 to 0.5
Outputs:
- attention_out: bfloat16 [3072, 3072], P('seq', 'grp')
Inputs may be any that keep to these rules, and one draw needn't show every extreme that they name: hist_count[s] of the 8 history slots of seq index s are live; the largest count is exactly 8.
All inputs are finite; a program needn't handle non-finite values.
Results may differ from a plain program's by a relative error of at most 0.0095.
The roundings to bfloat16 on the way count: a program that leaves them out, or rounds other values in their place, can miss the bound.
Values may be sent and summed in bfloat16 or wider, within the bound.
No kernel may reach another device: no remote copies, remote signals or barrier semaphores. Data moves between devices by JAX's collectives and lax.ppermute only.
A program may use at most 256 MiB of HBM per device.

v0:
```python
import math

import jax
import jax.numpy as jnp
from jax import lax
from jax.sharding import PartitionSpec as P

STEPS = 50


EPSILON = 1e-06


def from_behind(value, axis, steps):
    count = lax.axis_size(axis)
    initial, last = (max(0, -steps), min(count, count - steps))
    return lax.ppermute(value, axis, [(source, source + steps) for source in range(initial, last)])


def time_embed(step_index, width):
    half_width = width // 2
    frequency = jnp.exp(-math.log(10000.0) * jnp.arange(half_width, dtype=jnp.float32) / half_width)
    angles = step_index[0].astype(jnp.float32) * frequency
    return jnp.concatenate([jnp.cos(angles), jnp.sin(angles)])


def rms_scale(values, gain):
    return values * lax.rsqrt(jnp.mean(values * values, axis=-1, keepdims=True) + EPSILON) * gain


def local(
    feats,
    conv_weight,
    conv_bias,
    latent_projection_weight,
    noise,
    step_index,
    hist,
    hist_level,
    hist_count,
    w_in,
    w_hist,
    norm_gain,
    w_query,
    w_key,
    w_value,
    q_gain,
    k_gain,
    w_out,
):
    frame_count, channels, pixels = feats.shape
    earlier = from_behind(feats, "seq", 1)
    padded = jnp.concatenate([earlier, feats], axis=0)
    total = jnp.zeros(feats.shape, jnp.float32)
    for tap_index in range(3):
        window = padded[2 - tap_index : 2 - tap_index + frame_count]
        total = total + jnp.einsum(
            "oc,tcp->top", conv_weight[tap_index], window, preferred_element_type=jnp.float32
        )
    hidden_state = jax.nn.silu(total + conv_bias[None, :, None]).astype(jnp.bfloat16)
    sigma = (STEPS - step_index[0].astype(jnp.float32)) / STEPS
    latent_input = jnp.einsum(
        "qb,zby->zqy", latent_projection_weight, hidden_state, preferred_element_type=jnp.float32
    )
    noisy = ((1.0 - sigma) * latent_input + sigma * noise.astype(jnp.float32)).astype(jnp.bfloat16)
    lat_channels = noisy.shape[1]
    patches = (
        noisy.reshape(frame_count, lat_channels, pixels // 4, 4)
        .transpose(0, 2, 1, 3)
        .reshape(frame_count, pixels // 4, lat_channels * 4)
    )
    width = w_in.shape[1]
    embed = time_embed(step_index, width)
    all_patches = lax.all_gather(patches, "grp", axis=1, tiled=True)
    block_rows = all_patches.shape[1]
    summed = (
        jnp.dot(
            all_patches.reshape(-1, all_patches.shape[2]), w_in, preferred_element_type=jnp.float32
        )
        + embed
    )
    tokens = (
        rms_scale(summed, norm_gain)
        .astype(jnp.bfloat16)
        .reshape(frame_count, block_rows, width)
        .reshape(-1, width)
    )
    history = jnp.zeros((hist.shape[0], width), jnp.float32)
    for level in range(3):
        history = (
            history
            + jnp.dot(hist, w_hist[level], preferred_element_type=jnp.float32)
            * (hist_level == level).astype(jnp.float32)[:, None]
        )
    history = rms_scale(history, norm_gain).astype(jnp.bfloat16)
    both_rows = jnp.concatenate([tokens, history], axis=0)
    sec_rows = tokens.shape[0]
    key_rows = both_rows.shape[0]
    head_size = q_gain.shape[0]
    heads_local = w_query.shape[1] // head_size
    query = rms_scale(
        jnp.dot(tokens, w_query, preferred_element_type=jnp.float32).reshape(
            sec_rows, heads_local, head_size
        ),
        q_gain,
    ).astype(jnp.bfloat16)
    flattened_keys = (
        rms_scale(
            jnp.dot(both_rows, w_key, preferred_element_type=jnp.float32).reshape(
                key_rows, heads_local, head_size
            ),
            k_gain,
        )
        .astype(jnp.bfloat16)
        .reshape(key_rows, heads_local * head_size)
    )
    values_flat = jnp.dot(both_rows, w_value, preferred_element_type=jnp.float32).astype(
        jnp.bfloat16
    )
    seq_count = lax.axis_size("seq")
    shard_ids = jnp.arange(seq_count, dtype=jnp.int32)
    scale = 1.0 / math.sqrt(head_size)
    run_max = jnp.full((heads_local, sec_rows), -1e30, jnp.float32)
    key_piece = lax.all_gather(flattened_keys, "seq", axis=0, tiled=True)
    value_piece = lax.all_gather(values_flat, "seq", axis=0, tiled=True)
    count_rows = key_piece.shape[0]
    row_index = jnp.arange(count_rows, dtype=jnp.int32)
    owner = row_index // key_rows
    local_index = row_index - owner * key_rows
    owner_count = jnp.sum(
        jnp.where(owner[:, None] == shard_ids[None, :], hist_count[None, :], 0), axis=1
    )
    alive = (local_index < sec_rows) | (local_index - sec_rows < owner_count)
    key_heads = key_piece.reshape(count_rows, heads_local, head_size)
    value_heads = value_piece.reshape(count_rows, heads_local, head_size)
    scores = (
        jnp.einsum("qhd,khd->hqk", query, key_heads, preferred_element_type=jnp.float32) * scale
    )
    scores = jnp.where(alive[None, None, :], scores, -1e30)
    new_max = jnp.maximum(run_max, jnp.max(scores, axis=-1))
    soft = jnp.where(alive[None, None, :], jnp.exp(scores - new_max[..., None]), 0.0)
    new_sum = jnp.sum(soft, axis=-1)
    new_weighted = jnp.einsum(
        "hqk,khd->hqd", soft.astype(jnp.bfloat16), value_heads, preferred_element_type=jnp.float32
    )
    attended = new_weighted / new_sum[..., None]
    heads_out = (
        attended.astype(jnp.bfloat16).transpose(1, 0, 2).reshape(sec_rows, heads_local * head_size)
    )
    partial_out = jnp.dot(heads_out, w_out, preferred_element_type=jnp.float32)
    return lax.psum_scatter(
        partial_out.astype(jnp.bfloat16), "grp", scatter_dimension=1, tiled=True
    )


def solution(mesh):
    placed = (
        P("seq", None, "grp"),
        P(),
        P(),
        P(),
        P("seq", None, "grp"),
        P(),
        P("seq", None),
        P("seq"),
        P(),
        P(),
        P(),
        P(),
        P(None, "grp"),
        P(None, "grp"),
        P(None, "grp"),
        P(),
        P(),
        P("grp", None),
    )
    return jax.shard_map(
        local, mesh=mesh, in_specs=placed, out_specs=P("seq", "grp"), check_vma=False
    )
```

profile of v0, /device:TPU:0, one launch (start us, length us, event | category | flops | bytes accessed | tf_op | source)
XLA Modules:
  0.0 191.2 jit_solution(1770931649743177877)
XLA Ops:
  6.5 2.5 %collective-permute-start = (bf16[2,128,192]{1,2,0:T(8,128)(2,1)}, bf16[2,128,192]{1,2,0:T(8,128)(2,1)S(1)}, u32[]{:S(2)}, u32[]{:S(2)}) collective-permute-start(bf16[2,128,192]{1,2,0:T(8,128)(2,1)} %param.18), channel_id=1, source_target_pairs={{0,1},{1,2},{2,3},{3,4},{4,5},{5,6},{6,7},{7,8},{8,9},{9,10},{10,1... | collective-permute-start | bytes 294920 | tf_op jit(solution)/shard_map/ppermute | solution.py:17
  9.7 0.1 fusion.56
  9.8 1.1 fusion.46
  10.9 0.7 compare_convert_fusion
  11.5 1.2 convolution_multiply_fusion.2
  12.7 1.2 fusion.7
  13.9 1.3 multiply_reduce_fusion.2
  15.2 0.7 broadcast_bitcast_fusion
  15.9 0.8 multiply_convert_fusion.3
  16.7 1.0 convolution_add_fusion.2
  17.7 1.1 fusion.15
  18.8 0.1 copy.71
  18.9 0.1 copy.72
  19.0 0.1 copy.73
  19.1 4.8 %all_gather.9 = bf16[2,96,64]{2,0,1:T(2,128)(2,1)S(1)} all-gather(bf16[2,48,64]{2,0,1:T(2,128)(2,1)S(1)} %copy.73), channel_id=1, replica_groups=mesh['grp'=2,'seq'=16] {'grp'}, dimensions={1}, use_global_device_ids=true | all-gather | bytes 36864 | tf_op jit(solution)/shard_map/all_gather | solution.py:74
  23.9 0.1 copy.74
  24.0 0.1 reshape.109
  24.1 0.6 multiply_reduce_fusion
  24.7 0.3 multiply_convert_fusion
  25.1 1.4 copy-done.5
  26.5 2.0 %fusion.66 = (f32[200,768]{1,0:T(8,128)}, f32[200,768]{1,0:T(8,128)S(1)}) fusion(bf16[3072,768]{1,0:T(8,128)(2,1)S(1)} %copy-done.5, bf16[8,3072]{1,0:T(8,128)(2,1)S(1)} %multiply_convert_fusion.3, bf16[192,3072]{1,0:T(8,128)(2,1)S(1)} %multiply_convert_fusion), kind=kOutput, calls=%fused_computation.94 | convolution fusion | flops 946329600 | bytes 7176192 | tf_op jit(solution)/shard_map/dot_general | solution.py:109
  28.5 1.2 mul.185
  29.7 0.3 reduce_sum.58
  30.0 0.1 copy.77
  30.0 0.1 copy.78
  30.2 0.3 mul.186
  30.5 0.9 fusion.27
  31.4 0.0 all-gather.3.cloned.1.call-update
  31.4 0.0 all-gather.5.cloned.1.call-start
  31.4 4.2 %convolution_convert_fusion.1 = bf16[200,768]{1,0:T(8,128)(2,1)} fusion(bf16[3072,768]{1,0:T(8,128)(2,1)} %param.32, bf16[8,3072]{1,0:T(8,128)(2,1)S(1)} %multiply_convert_fusion.3, bf16[192,3072]{1,0:T(8,128)(2,1)S(1)} %multiply_convert_fusion), kind=kOutput, calls=%fused_computation.18 | convolution fusion | flops 946329600 | bytes 6254592 | tf_op jit(solution)/shard_map/dot_general | solution.py:117
  35.7 0.0 reduce-scatter.2.cloned.1.call-start
  35.7 0.1 select_reduce_fusion
  35.9 3.4 %fusion.67 = f32[192,768]{1,0:T(8,128)S(1)} fusion(bf16[192,3072]{1,0:T(8,128)(2,1)S(1)} %multiply_convert_fusion, bf16[3072,768]{1,0:T(8,128)(2,1)} %param.30), kind=kOutput, calls=%fused_computation.95 | convolution fusion | flops 905969664 | bytes 6488064 | tf_op jit(solution)/shard_map/dot_general | solution.py:102
  39.3 0.1 reshape.110
  39.4 0.3 multiply_reduce_fusion.1
  39.7 0.1 copy.75
  39.8 0.1 copy.76
  39.9 0.3 multiply_convert_fusion.1
  40.2 47.4 %all-gather.3.cloned.1.call-done = bf16[3200,768]{1,0:T(8,128)(2,1)} async-done(((bf16[200,768]{1,0:T(8,128)(2,1)}), bf16[3200,768]{1,0:T(8,128)(2,1)}) %all-gather.3.cloned.1.call-update) | async-done | bytes 4915216 | tf_op jit(solution)/shard_map/all_gather | solution.py:124
  87.6 7.4 %copy.79 = bf16[3200,768]{0,1:T(8,128)(2,1)} copy(bf16[3200,768]{1,0:T(8,128)(2,1)} %all-gather.3.cloned.1.call-done) | data formatting | bytes 9830400 | tf_op jit(solution)/shard_map/all_gather | solution.py:124
  95.1 10.4 %fusion = (f32[6,192]{1,0:T(8,128)S(1)}, f32[6,192,3200]{2,1,0:T(8,128)}) fusion(pred[3200]{0:T(1024)(128)(4,1)S(1)} %fusion.54, bf16[3200,6,128]{0,2,1:T(8,128)(2,1)} %bitcast.85, bf16[192,6,128]{2,1,0:T(8,128)(2,1)S(1)} %multiply_convert_fusion.1), kind=kOutput, calls=%fused_computation.2 | convolution fusion | flops 954776448 | bytes 19963520 | tf_op jit(solution)/shard_map/qhd,khd->hqk/dot_general | solution.py:137
  105.4 9.1 %fusion.1 = f32[6,192]{1,0:T(8,128)S(1)} fusion(f32[6,192,3200]{2,1,0:T(8,128)} %get-tuple-element.15, f32[6,192]{1,0:T(8,128)S(1)} %broadcast_maximum_fusion, pred[3200]{0:T(1024)(128)(4,1)S(1)} %fusion.54), kind=kLoop, calls=%fused_computation.3 | loop fusion | flops 18430848 | bytes 14758016 | tf_op jit(solution)/shard_map/reduce_sum | solution.py:142
  114.5 28.0 %all-gather.5.cloned.1.call-done = bf16[3200,768]{1,0:T(8,128)(2,1)} async-done(((bf16[200,768]{1,0:T(8,128)(2,1)}), bf16[3200,768]{1,0:T(8,128)(2,1)}) %all-gather.5.cloned.1.call-update) | async-done | bytes 4915216 | tf_op jit(solution)/shard_map/all_gather | solution.py:125
  142.5 7.4 %copy.82 = bf16[3200,768]{0,1:T(8,128)(2,1)} copy(bf16[3200,768]{1,0:T(8,128)(2,1)} %all-gather.5.cloned.1.call-done) | data formatting | bytes 9830400 | tf_op jit(solution)/shard_map/all_gather | solution.py:125
  149.9 9.7 %fusion.22 = bf16[6,24,8,128]{3,2,1,0:T(8,128)(2,1)S(1)} fusion(bf16[3200,6,128]{0,2,1:T(8,128)(2,1)} %bitcast.86, f32[6,192,3200]{2,1,0:T(8,128)} %get-tuple-element.15, f32[6,192]{1,0:T(8,128)S(1)} %broadcast_maximum_fusion, pred[3200]{0:T(1024)(128)(4,1)S(1)} %fusion.54, f32[192,6]{0,1:T(8,128)S(1)} %bitcast.90), kind=kOutput, calls=%fused_computation.29 | convolution fusion | flops 962445312 | bytes 19968128 | tf_op jit(solution)/shard_map/hqk,khd->hqd/dot_general | solution.py:143
  159.6 4.4 %convolution_convert_fusion = bf16[192,3072]{1,0:T(8,128)(2,1)} fusion(bf16[768,3072]{1,0:T(8,128)(2,1)} %param.35, bf16[6,24,8,128]{3,2,1,0:T(8,128)(2,1)S(1)} %fusion.22), kind=kOutput, calls=%fused_computation.8 | convolution fusion | flops 906559488 | bytes 6193152 | tf_op jit(solution)/shard_map/dot_general | solution.py:150
  164.1 0.0 reduce-scatter.2.cloned.1.call-update
  164.1 20.5 %reduce-scatter.2.cloned.1.call-done = bf16[192,1536]{1,0:T(8,128)(2,1)} async-done(((bf16[192,3072]{1,0:T(8,128)(2,1)}), bf16[192,1536]{1,0:T(8,128)(2,1)}) %reduce-scatter.2.cloned.1.call-update) | async-done | bytes 589840 | tf_op jit(solution)/shard_map/reduce_scatter | solution.py:151
  (22 shorter events, 0.1 us)
Async XLA Ops:
  6.5 17.6 %copy-start = (bf16[64,3072]{1,0:T(8,128)(2,1)S(1)}, bf16[64,3072]{1,0:T(8,128)(2,1)}, u32[]{:S(2)}) copy-start(bf16[64,3072]{1,0:T(8,128)(2,1)} %param.27) | copy-start | bytes 1179652
  6.5 18.2 %copy-start.2 = (f32[3072]{0:T(1024)S(1)}, f32[3072]{0:T(1024)}, u32[]{:S(2)}) copy-start(f32[3072]{0:T(1024)} %param.29) | copy-start | bytes 36868
  6.5 81.1 %all-gather.3.cloned.1.call-start = ((), (), s32[]{:S(2)}) async-start(), calls=%async_computation.1 | async-start | bytes 5222400 | tf_op jit(solution)/shard_map/all_gather | solution.py:124
  6.5 10.1 %collective-permute-start = (bf16[2,128,192]{1,2,0:T(8,128)(2,1)}, bf16[2,128,192]{1,2,0:T(8,128)(2,1)S(1)}, u32[]{:S(2)}, u32[]{:S(2)}) collective-permute-start(bf16[2,128,192]{1,2,0:T(8,128)(2,1)} %param.18), channel_id=1, source_target_pairs={{0,1},{1,2},{2,3},{3,4},{4,5},{5,6},{6,7},{7,8},{8,9},{9,10},{10,1... | collective-permute-start | bytes 294920 | tf_op jit(solution)/shard_map/ppermute | solution.py:17
  24.1 2.3 %copy-start.5 = (bf16[3072,768]{1,0:T(8,128)(2,1)S(1)}, bf16[3072,768]{1,0:T(8,128)(2,1)}, u32[]{:S(2)}) copy-start(bf16[3072,768]{1,0:T(8,128)(2,1)} %param.31) | copy-start | bytes 14155780
  30.5 5.3 %copy-start.3 = (s32[16]{0:T(128)S(1)}, s32[16]{0:T(128)}, u32[]{:S(2)}) copy-start(s32[16]{0:T(128)} %param.26) | copy-start | bytes 196
  31.4 111.1 %all-gather.5.cloned.1.call-start = ((), (), s32[]{:S(2)}) async-start(), calls=%async_computation.2 | async-start | bytes 5222400 | tf_op jit(solution)/shard_map/all_gather | solution.py:125
  35.6 4.3 %copy-start.4 = (f32[128]{0:T(128)S(1)}, f32[128]{0:T(128)}, u32[]{:S(2)}) copy-start(f32[128]{0:T(128)} %param.33) | copy-start | bytes 1540
  35.7 149.0 %reduce-scatter.2.cloned.1.call-start = ((), (), s32[]{:S(2)}) async-start(), calls=%async_computation.3 | async-start | bytes 1769472 | tf_op jit(solution)/shard_map/reduce_scatter | solution.py:151
  149.9 34.7 %copy-start.1 = (bf16[64,3072]{1,0:T(8,128)(2,1)S(1)}, bf16[64,3072]{1,0:T(8,128)(2,1)}, u32[]{:S(2)}) copy-start(bf16[64,3072]{1,0:T(8,128)(2,1)} %param.27) | copy-start | bytes 1179652
Sparse Core Ops, SparseCore 0:
  31.5 56.0 all-gather.2
  89.8 52.6 all-gather.4
  164.2 20.3 reduce-scatter.1
where the time goes:
time: 192 us; the launch traced here: 191 us
  waiting for transfers between devices  96 us (50%)
  matrix products  41.5 us (22%)
  local copies, waits for them, and re-layouts  19.5 us (10%)
  between operations  14 us (7%)
  other arithmetic  12.8 us (7%)
  blocking collectives  4.77 us (2%)
  starting transfers between devices  2.61 us (1%)
    all_gather x1, waiting for transfers between devices, local(): key_piece = lax.all_gather(flattened_keys, 'seq', axis=0, tiled=True)  47.4 us
    all_gather x1, waiting for transfers between devices, local(): value_piece = lax.all_gather(values_flat, 'seq', axis=0, tiled=True)  28 us
    reduce_scatter x1, waiting for transfers between devices, local(): lax.psum_scatter(partial_out.astype(jnp.bfloat16), 'grp', scatter_dimensi...  20.5 us
    dot_general x1, matrix products, local(): jnp.einsum('qhd,khd->hqk', query, key_heads, preferred_element_type=jnp.f...  10.4 us
    dot_general x1, matrix products, local(): jnp.einsum('hqk,khd->hqd', soft.astype(jnp.bfloat16), value_heads, prefer...  9.68 us
    reduce_sum x1, other arithmetic, local(): new_sum = jnp.sum(soft, axis=-1)  9.09 us
    all_gather x1, local copies, waits for them, and re-layouts, local(): key_piece = lax.all_gather(flattened_keys, 'seq', axis=0, tiled=True)  7.44 us
    all_gather x1, local copies, waits for them, and re-layouts, local(): value_piece = lax.all_gather(values_flat, 'seq', axis=0, tiled=True)  7.44 us
  transfers between devices with their start and end apart: 4, of which 3 were waited for; matrix products, arithmetic and copies ran while one was open for 22% of the time, Pallas kernels for 0%

commit v1 on v0

v1 whole, which is shorter than its diff:
```python
import functools
import math

import jax
import jax.numpy as jnp
from jax import lax
from jax.experimental import pallas as pl
from jax.experimental.pallas import tpu as pltpu
from jax.sharding import PartitionSpec as P

STEPS = 50
EPSILON = 1e-06
F32 = jnp.float32
BF16 = jnp.bfloat16
VMEM = pl.BlockSpec(memory_space=pltpu.VMEM)
SMEM = pl.BlockSpec(memory_space=pltpu.SMEM)


def dot(a, b):
    return jnp.dot(a, b, preferred_element_type=F32)


def time_embed(step_index, width):
    half_width = width // 2
    frequency = jnp.exp(-math.log(10000.0) * jnp.arange(half_width, dtype=F32) / half_width)
    angles = step_index[0].astype(F32) * frequency
    return jnp.concatenate([jnp.cos(angles), jnp.sin(angles)])


def encode_kernel(
    step_ref, feats_ref, earlier_ref, weight_ref, bias_ref, latent_ref, noise_ref, hist_ref,
    level_ref, out_ref,
):
    frames, channels, pixels = feats_ref.shape
    lat = noise_ref.shape[1]
    patch = lat * 4
    cells = pixels // 4
    diagonal = lax.broadcasted_iota(jnp.int32, (channels, channels), 0) == lax.broadcasted_iota(
        jnp.int32, (channels, channels), 1
    )
    bias = jnp.sum(jnp.where(diagonal, bias_ref[...], 0.0), axis=1, keepdims=True)
    step = jnp.full((lat, pixels), step_ref[0].astype(F32), F32)
    sigma = (STEPS - step) / STEPS
    row = lax.broadcasted_iota(jnp.int32, (lat, frames * patch), 0)
    lane = lax.broadcasted_iota(jnp.int32, (lat, frames * patch), 1)
    pixel = lax.broadcasted_iota(jnp.int32, (pixels, frames * patch), 0)
    feature = lax.broadcasted_iota(jnp.int32, (pixels, frames * patch), 1)
    keep = (pixel % 4) == (feature % 4)
    collect = (
        lax.broadcasted_iota(jnp.int32, (cells, pixels), 1) // 4
        == lax.broadcasted_iota(jnp.int32, (cells, pixels), 0)
    ).astype(BF16)
    patches = jnp.zeros((cells, frames * patch), F32)
    for t in range(frames):
        total = jnp.zeros((channels, pixels), F32)
        for tap in range(3):
            source = t - tap
            window = feats_ref[source] if source >= 0 else earlier_ref[frames + source]
            total = total + dot(weight_ref[tap], window)
        total = total + bias
        hidden = (total / (1.0 + jnp.exp(-total))).astype(BF16)
        mixed = dot(latent_ref[...], hidden)
        noisy = ((1.0 - sigma) * mixed + sigma * noise_ref[t].astype(F32)).astype(BF16)
        spread = (lane // 4 == row + t * lat).astype(BF16)
        wide = lax.dot_general(noisy, spread, (((0,), (0,)), ((), ())), preferred_element_type=F32)
        wide = jnp.where(keep, wide, 0.0).astype(BF16)
        patches = patches + dot(collect, wide)
    out_ref[0:cells, :] = patches.astype(BF16)
    slots = hist_ref.shape[0]
    level = jnp.broadcast_to(level_ref[...], (slots, patch)).astype(F32)
    tail = jnp.concatenate([hist_ref[...].astype(F32), level], axis=1)
    tail = jnp.concatenate([tail, jnp.zeros((out_ref.shape[0] - cells - slots, 2 * patch), F32)], axis=0)
    out_ref[cells:, :] = tail.astype(BF16)


def joint_kernel(
    info_ref, near_ref, far_ref, w_in_ref, w_hist_ref, embed_ref, gain_ref, w_q_ref, w_kv_ref,
    q_gain_ref, k_gain_ref, bias_ref, own_ref, sib_ref,
    patch_ref, hist_ref, x_ref, tok_ref, q_ref, k_ref, v_ref, s_ref,
    *, cells, slots, block, group_at, query_rows,
):
    heads, keys, size = k_ref.shape
    width = w_in_ref.shape[1]
    lanes = near_ref.shape[1]
    patch = w_in_ref.shape[0]
    half = near_ref.shape[0] // block
    tile = 4 * cells
    group = info_ref[0]
    hist_rows = hist_ref.shape[0]

    spot = 0
    for source in (near_ref, far_ref):
        for side in range(2):
            at = jnp.where(group == side, 0, group_at)
            patch_ref[spot * cells : (spot + 1) * cells, :] = source[
                pl.ds(pl.multiple_of(at * block, block), cells), :
            ]
            spot += 1
    for number, source in enumerate((near_ref, far_ref)):
        for p in range(half):
            if p != 0 and p != group_at:
                patch_ref[spot * cells : (spot + 1) * cells, :] = source[p * block : p * block + cells, :]
                spot += 1
        owners = group_at
        for p in range(owners):
            r = (number * owners + p) * slots
            hist_ref[r : r + slots, :] = source[p * block + cells : p * block + cells + slots, :].astype(F32)

    step = 512
    fold = 128

    def normalise(rows, with_embed, products):
        squares = jnp.zeros((rows, fold), F32)
        for n in range(0, width, step):
            x = products(n)
            if with_embed:
                x = x + embed_ref[:, n : n + step]
            x_ref[0:rows, n : n + step] = x
            for m in range(0, step, fold):
                part = x[:, m : m + fold]
                squares = squares + part * part
        mean = jnp.sum(squares, axis=1, keepdims=True) / width
        inverse = lax.rsqrt(mean + EPSILON)
        return inverse

    def emit(rows, at, inverse):
        for n in range(0, width, step):
            tok_ref[at : at + rows, n : n + step] = (
                x_ref[0:rows, n : n + step] * inverse * gain_ref[:, n : n + step]
            ).astype(BF16)

    def head_norm(values, gain):
        mean = jnp.mean(values * values, axis=1, keepdims=True)
        return (values * lax.rsqrt(mean + EPSILON) * gain).astype(BF16)

    def project(rows, at):
        both = dot(tok_ref[0:rows, :], w_kv_ref[...])
        for h in range(heads):
            k_ref[h, pl.ds(at, rows), :] = head_norm(both[:, h * size : (h + 1) * size], k_gain_ref[...])
            v_ref[h, pl.ds(at, rows), :] = both[:, (heads + h) * size : (heads + h + 1) * size].astype(BF16)

    tiles = patch_ref.shape[0] // tile
    frames = lanes // patch

    def token_tile(i, carry):
        source = patch_ref[pl.ds(pl.multiple_of(i * tile, tile), tile), :]
        for t in range(frames):
            part = source[:, t * patch : (t + 1) * patch]
            inverse = normalise(tile, True, lambda n: dot(part, w_in_ref[:, n : n + step]))
            emit(tile, t * tile, inverse)
        project(frames * tile, pl.multiple_of(i * (frames * tile), frames * tile))

        @pl.when(i == 0)
        def _():
            q = dot(tok_ref[...], w_q_ref[...])
            for h in range(heads):
                q_ref[h] = head_norm(q[:, h * size : (h + 1) * size], q_gain_ref[...])

        return carry

    lax.fori_loop(0, tiles, token_tile, 0)

    section = tiles * frames * tile
    for r in range(0, hist_rows, 128):
        rows = min(128, hist_rows - r)
        source = hist_ref[r : r + rows, :]
        values = source[:, 0:patch]
        level = source[:, patch : 2 * patch]
        parts = [jnp.where(level == v, values, 0.0).astype(BF16) for v in range(w_hist_ref.shape[0])]

        def products(n):
            total = dot(parts[0], w_hist_ref[0, :, n : n + step])
            for v in range(1, len(parts)):
                total = total + dot(parts[v], w_hist_ref[v, :, n : n + step])
            return total

        inverse = normalise(rows, False, products)
        emit(rows, 0, inverse)
        project(rows, section + r)

    scale = math.log2(math.e) / math.sqrt(size)
    chunk = 512
    pieces = [(a, chunk, False) for a in range(0, section, chunk)]
    pieces += [(section + r, min(128, hist_rows - r), True) for r in range(0, hist_rows, 128)]

    def attend(h, carry):
        for a in range(0, q_ref.shape[1], query_rows):
            q = q_ref[h, a : a + query_rows, :]
            top = jnp.full((query_rows, fold), -3e38, F32)
            for at, length, masked in pieces:
                s = lax.dot_general(
                    q, k_ref[h, at : at + length, :], (((1,), (1,)), ((), ())), preferred_element_type=F32
                )
                if masked:
                    s = s + bias_ref[:, at - section : at - section + length]
                s_ref[:, at : at + length] = s
                for m in range(0, length, fold):
                    top = jnp.maximum(top, s[:, m : m + fold])
            top = jnp.max(top, axis=1, keepdims=True)
            total = jnp.zeros((query_rows, fold), F32)
            weighted = jnp.zeros((query_rows, size), F32)
            for at, length, masked in pieces:
                soft = jnp.exp2((s_ref[:, at : at + length] - top) * scale)
                for m in range(0, length, fold):
                    total = total + soft[:, m : m + fold]
                weighted = weighted + dot(soft.astype(BF16), v_ref[h, at : at + length, :])
            out = (weighted / jnp.sum(total, axis=1, keepdims=True)).astype(BF16)
            q_ref[h, a : a + query_rows, :] = out
        return carry

    lax.fori_loop(0, heads, attend, 0)
    part = 2 * cells
    for h in range(heads):
        for t in range(frames):
            base = t * tile
            own_ref[t * part : (t + 1) * part, h * size : (h + 1) * size] = q_ref[h, base : base + part, :]
            sib_ref[t * part : (t + 1) * part, h * size : (h + 1) * size] = q_ref[
                h, base + part : base + tile, :
            ]


def combine_kernel(
    info_ref, own_ref, sib_ref, across_ref, corner_ref, w_local_ref, w_across_ref, w_corner_ref, out_ref
):
    core = info_ref[1]
    depth = own_ref.shape[1]
    mine = pl.ds(pl.multiple_of(core * depth, depth), depth)
    other = pl.ds(pl.multiple_of((1 - core) * depth, depth), depth)
    step = 512
    for n in range(0, out_ref.shape[1], step):
        columns = slice(n, n + step)
        total = dot(own_ref[...], w_local_ref[mine, columns])
        total = total + dot(sib_ref[...], w_local_ref[other, columns])
        total = total + dot(across_ref[...], w_across_ref[:, columns])
        total = total + dot(corner_ref[...], w_corner_ref[:, columns])
        out_ref[:, columns] = total.astype(BF16)


def flip(value, mask, seq_count):
    pairs = [(i, i ^ mask) for i in range(2 * seq_count)]
    return lax.ppermute(value, ("grp", "seq"), pairs)


def local(
    feats, conv_weight, conv_bias, latent_projection_weight, noise, step_index, hist, hist_level,
    hist_count, w_in, w_hist, norm_gain, w_query, w_key, w_value, q_gain, k_gain, w_out,
):
    frame_count, channels, pixels = feats.shape
    seq_count = lax.axis_size("seq")
    group = lax.axis_index("grp")
    place = lax.axis_index("seq")
    core = place % 2
    width = w_in.shape[1]
    patch = w_in.shape[0]
    cells = pixels // 4
    slots = hist.shape[0]
    block = cells + 16
    lanes = frame_count * patch
    size = q_gain.shape[0]
    heads = w_query.shape[1] // size // 2
    depth = heads * size

    earlier = lax.ppermute(feats, "seq", [(i, i + 1) for i in range(seq_count - 1)])
    gathered = pl.pallas_call(
        encode_kernel,
        out_shape=jax.ShapeDtypeStruct((block, lanes), BF16),
        in_specs=[SMEM] + [VMEM] * 8,
        out_specs=VMEM,
        name="encode",
    )(
        step_index, feats, earlier, conv_weight, conv_bias.reshape(1, channels),
        latent_projection_weight, noise, hist, hist_level.reshape(slots, 1),
    )

    masks = []
    bit = seq_count // 2
    while bit > 1:
        masks.append(bit)
        bit //= 2
    owner_masks = [0]
    for mask in masks:
        owner_masks = owner_masks + [m ^ mask for m in owner_masks]
    for mask in masks + [seq_count]:
        gathered = jnp.concatenate([gathered, flip(gathered, mask, seq_count)], axis=0)
    far = flip(gathered, 1, seq_count)
    group_at = len(owner_masks)

    owner = place ^ jnp.array(owner_masks + [m ^ 1 for m in owner_masks], jnp.int32)
    shards = jnp.arange(seq_count, dtype=jnp.int32)
    live = jnp.sum(jnp.where(owner[:, None] == shards[None, :], hist_count[None, :], 0), axis=1)
    slot = jnp.arange(slots, dtype=jnp.int32)
    bias = jnp.where(slot[None, :] < live[:, None], 0.0, -1e30).astype(F32).reshape(1, -1)

    w_q = lax.dynamic_slice_in_dim(w_query, core * depth, depth, axis=1)
    w_kv = jnp.concatenate(
        [
            lax.dynamic_slice_in_dim(w_key, core * depth, depth, axis=1),
            lax.dynamic_slice_in_dim(w_value, core * depth, depth, axis=1),
        ],
        axis=1,
    )
    columns = w_out.shape[1] // 2
    w_send = lax.dynamic_slice(w_out, (core * depth, (1 - group) * columns), (depth, columns))
    w_send, near = lax.optimization_barrier((w_send, gathered))
    w_across = flip(w_send, seq_count, seq_count)
    w_corner = flip(w_across, 1, seq_count)
    w_local = lax.dynamic_slice_in_dim(w_out, group * columns, columns, axis=1)

    info = jnp.stack([group, core]).astype(jnp.int32)
    hist_rows = slots * seq_count
    tokens = 2 * seq_count * frame_count * cells
    keys = tokens + hist_rows
    rows = frame_count * 4 * cells
    query_rows = rows if rows * keys * 4 <= 6 * 2**20 else rows // 2
    own, sib = pl.pallas_call(
        functools.partial(
            joint_kernel, cells=cells, slots=slots, block=block, group_at=group_at,
            query_rows=query_rows,
        ),
        out_shape=[jax.ShapeDtypeStruct((rows // 2, depth), BF16)] * 2,
        in_specs=[SMEM] + [VMEM] * 11,
        out_specs=[VMEM] * 2,
        scratch_shapes=[
            pltpu.VMEM((tokens // frame_count, lanes), BF16),
            pltpu.VMEM((hist_rows, lanes), F32),
            pltpu.VMEM((4 * cells, width), F32),
            pltpu.VMEM((rows, width), BF16),
            pltpu.VMEM((heads, rows, size), BF16),
            pltpu.VMEM((heads, keys, size), BF16),
            pltpu.VMEM((heads, keys, size), BF16),
            pltpu.VMEM((query_rows, keys), F32),
        ],
        compiler_params=pltpu.CompilerParams(vmem_limit_bytes=60 * 2**20),
        cost_estimate=pl.CostEstimate(
            flops=2 * keys * width * 3 * depth + 4 * rows * keys * depth,
            bytes_accessed=6 * width * depth,
            transcendentals=rows * keys * heads,
        ),
        name="joint",
    )(
        info, near, far, w_in, w_hist, time_embed(step_index, width).reshape(1, width),
        norm_gain.reshape(1, width), w_q, w_kv, q_gain.reshape(1, size), k_gain.reshape(1, size), bias,
    )
    from_sib = flip(sib, 1, seq_count)
    across = flip(own, seq_count, seq_count)
    corner = flip(sib, seq_count + 1, seq_count)
    return pl.pallas_call(
        combine_kernel,
        out_shape=jax.ShapeDtypeStruct((rows // 2, columns), BF16),
        in_specs=[SMEM] + [VMEM] * 7,
        out_specs=VMEM,
        compiler_params=pltpu.CompilerParams(vmem_limit_bytes=24 * 2**20),
        name="combine",
    )(info, own, from_sib, across, corner, w_local, w_across, w_corner)


def solution(mesh):
    placed = (
        P("seq", None, "grp"), P(), P(), P(), P("seq", None, "grp"), P(), P("seq", None), P("seq"),
        P(), P(), P(), P(), P(None, "grp"), P(None, "grp"), P(None, "grp"), P(), P(), P("grp", None),
    )
    return jax.shard_map(local, mesh=mesh, in_specs=placed, out_specs=P("seq", "grp"), check_vma=False)
```

time: 192 us -> 115 us (0.60)
  waiting for transfers between devices: 96 us -> 31 us
  Pallas kernels: 0 us -> 47.8 us
  matrix products: 41.5 us -> 0 us
  between operations: 14 us -> 0.79 us
  starting transfers between devices: 2.61 us -> 14.7 us
  local copies, waits for them, and re-layouts: 19.5 us -> 12.9 us
  other arithmetic: 12.8 us -> 7.58 us
  blocking collectives: 4.77 us -> 0 us
    all_gather x2 -> x0, waiting for transfers between devices: 75.4 us -> none  [the longest x1 47.4 us: local(): key_piece = lax.all_gather(flattened_keys, 'seq', axis=0, tiled=True)]
    pallas_call x0 -> x3, Pallas kernels: none -> 47.8 us  [the longest x1 42.3 us: local(): pl.pallas_call(functools.partial(joint_kernel, cells=cells, slots=slots,...]
    dot_general x13 -> x0, matrix products: 41.5 us -> none  [the longest x1 10.4 us: local(): jnp.einsum('qhd,khd->hqk', query, key_heads, preferred_element_type=jnp.f...]
    ppermute x1 -> x11, waiting for transfers between devices: 0.01 us -> 31 us  [the longest x10 31 us: flip(): return lax.ppermute(value, ('grp', 'seq'), pairs)]
    reduce_scatter x1 -> x0, waiting for transfers between devices: 20.5 us -> none  [local(): lax.psum_scatter(partial_out.astype(jnp.bfloat16), 'grp', scatter_dimensi...]
    all_gather x3 -> x0, local copies, waits for them, and re-layouts: 15 us -> none  [the longest x1 7.44 us: local(): key_piece = lax.all_gather(flattened_keys, 'seq', axis=0, tiled=True)]
    ppermute x1 -> x11, starting transfers between devices: 2.52 us -> 14.7 us  [the longest x10 12.3 us: flip(): return lax.ppermute(value, ('grp', 'seq'), pairs)]
    reduce_sum x4 -> x1, other arithmetic: 9.76 us -> 0.84 us  [local(): jnp.sum(jnp.where(owner[:, None] == shards[None, :], hist_count[None, :],...]
  transfers between devices with their start and end apart: 4 -> 11, of which waited for: 3 -> 5; matrix products, arithmetic and copies ran while one was open for 22% -> 14% of each run, Pallas kernels for 0% -> 37%
where the time goes in v1:
time: 115 us
  Pallas kernels  47.8 us (42%)
  waiting for transfers between devices  31 us (27%)
  starting transfers between devices  14.7 us (13%)
  local copies, waits for them, and re-layouts  12.9 us (11%)
  other arithmetic  7.58 us (7%)
    pallas_call x1, Pallas kernels, local(): pl.pallas_call(functools.partial(joint_kernel, cells=cells, slots=slots,...  42.3 us
    ppermute x10, waiting for transfers between devices, flip(): return lax.ppermute(value, ('grp', 'seq'), pairs)  31 us
    ppermute x10, starting transfers between devices, flip(): return lax.ppermute(value, ('grp', 'seq'), pairs)  12.3 us
    unnamed x21, local copies, waits for them, and re-layouts  3.11 us
    dynamic_slice x1, local copies, waits for them, and re-layouts, local(): lax.dynamic_slice_in_dim(w_value, core * depth, depth, axis=1)  3 us
    pallas_call x1, Pallas kernels, local(): pl.pallas_call(encode_kernel, out_shape=jax.ShapeDtypeStruct((block, lane...  2.79 us
    pallas_call x1, Pallas kernels, local(): pl.pallas_call(combine_kernel, out_shape=jax.ShapeDtypeStruct((rows // 2,...  2.77 us
    concatenate x1, other arithmetic, local(): jnp.concatenate([lax.dynamic_slice_in_dim(w_key, core * depth, depth, axi...  2.5 us
  transfers between devices with their start and end apart: 11, of which 5 were waited for; matrix products, arithmetic and copies ran while one was open for 14% of the time, Pallas kernels for 37%

profile of v1, /device:TPU:0, one launch (start us, length us, event | category | flops | bytes accessed | tf_op | source)
XLA Modules:
  0.0 114.9 jit_solution(9016934163228053238)
XLA Ops:
  0.0 1.0 copy.27.feats_ref
  1.0 0.0 copy-start.2
  1.0 2.4 %collective-permute-start = (bf16[2,128,192]{2,1,0:T(8,128)(2,1)S(1)}, bf16[2,128,192]{2,1,0:T(8,128)(2,1)S(1)}, u32[]{:S(2)}, u32[]{:S(2)}) collective-permute-start(bf16[2,128,192]{2,1,0:T(8,128)(2,1)S(1)} %copy.27.feats_ref), channel_id=1, source_target_pairs={{0,1},{1,2},{2,3},{3,4},{4,5},{5,6},{6,7},{7,8},{8,9},{9,10},{10,1... | collective-permute-start | bytes 294920 | tf_op jit(solution)/shard_map/ppermute | solution.py:263
  4.1 1.3 %copy.28.level_ref = s32[8,1]{1,0:T(8,128)} copy(s32[8,1]{0,1:T(1,128)} %bitcast.13) | data formatting | bytes 64 | tf_op jit(solution)/shard_map/reshape | solution.py:272
  5.4 0.1 fusion
  5.5 0.7 broadcast_xor_fusion
  6.1 0.8 select_reduce_fusion
  7.0 0.1 fusion.2
  7.0 0.6 pad_maximum_fusion.4
  7.6 0.0 collective-permute-done.earlier_ref
  7.7 0.6 copy-done.3
  8.3 2.8 %encode.1 = bf16[64,128]{1,0:T(8,128)(2,1)} custom-call(s32[1]{0:T(128)S(6)} %copy.33.step_ref, bf16[2,128,192]{2,1,0:T(8,128)(2,1)} %copy-done.2, bf16[2,128,192]{2,1,0:T(8,128)(2,1)} %copy-done.3, bf16[3,128,128]{2,1,0:T(8,128)(2,1)} %weight_ref.1, f32[1,128]{1,0:T(1,128)} %bitcast.12, bf16[16,128]{1,0:T(8,128)(2,1)} %latent_ref.1, ...), custom_call_target="tpu_custom_call" | custom-call | tf_op jit(solution)/shard_map/encode/pallas_call | solution.py:264
  11.1 4.6 %collective-permute-start.1 = (bf16[64,128]{1,0:T(8,128)(2,1)}, bf16[64,128]{1,0:T(8,128)(2,1)S(1)}, u32[]{:S(2)}, u32[]{:S(2)}) collective-permute-start(bf16[64,128]{1,0:T(8,128)(2,1)} %encode.1), channel_id=1, source_target_pairs={{0,8},{1,9},{2,10},{3,11},{4,12},{5,13},{6,14},{7,15},{8,0},{9,1},... | collective-permute-start | bytes 49160 | tf_op jit(solution)/shard_map/ppermute | solution.py:241
  15.7 0.7 pad_add_fusion.info_ref
  16.4 0.6 select_n.42.bias_ref
  17.0 1.3 %dynamic_slice.15 = bf16[384,1536]{1,0:T(8,128)(2,1)S(1)} dynamic-slice(bf16[768,3072]{1,0:T(8,128)(2,1)} %param.36, s32[]{:T(128)S(6)} %select_n.38, s32[]{:T(128)S(6)} %select_n.39), dynamic_slice_sizes={384,1536} | dynamic-slice | bytes 2359300 | tf_op jit(solution)/shard_map/dynamic_slice | solution.py:303
  18.3 0.0 collective-permute-done.1
  18.3 0.7 pad_maximum_fusion.3
  19.1 1.6 %collective-permute-start.2 = (bf16[128,128]{1,0:T(8,128)(2,1)S(1)}, bf16[128,128]{1,0:T(8,128)(2,1)S(1)}, u32[]{:S(2)}, u32[]{:S(2)}) collective-permute-start(bf16[128,128]{1,0:T(8,128)(2,1)S(1)} %pad_maximum_fusion.3), channel_id=1, source_target_pairs={{0,4},{1,5},{2,6},{3,7},{4,0},{5,1},{6,2},{7,3},{8,12},{9,13},{10,... | collective-permute-start | bytes 98312 | tf_op jit(solution)/shard_map/ppermute | solution.py:241
  20.6 0.7 constant_dynamic-update-slice_fusion.4
  21.4 1.6 %collective-permute-done.2 = bf16[128,128]{1,0:T(8,128)(2,1)S(1)} collective-permute-done((bf16[128,128]{1,0:T(8,128)(2,1)S(1)}, bf16[128,128]{1,0:T(8,128)(2,1)S(1)}, u32[]{:S(2)}, u32[]{:S(2)}) %collective-permute-start.2) | collective-permute-done | bytes 32800 | tf_op jit(solution)/shard_map/ppermute | solution.py:241
  23.0 0.7 pad_maximum_fusion.2
  23.7 0.7 collective-permute-start.3
  24.4 3.5 %collective-permute-done.3 = bf16[256,128]{1,0:T(8,128)(2,1)S(1)} collective-permute-done((bf16[256,128]{1,0:T(8,128)(2,1)S(1)}, bf16[256,128]{1,0:T(8,128)(2,1)S(1)}, u32[]{:S(2)}, u32[]{:S(2)}) %collective-permute-start.3) | collective-permute-done | bytes 65568 | tf_op jit(solution)/shard_map/ppermute | solution.py:241
  28.0 0.7 pad_maximum_fusion.1
  28.7 1.6 %collective-permute-start.4 = (bf16[512,128]{1,0:T(8,128)(2,1)S(1)}, bf16[512,128]{1,0:T(8,128)(2,1)S(1)}, u32[]{:S(2)}, u32[]{:S(2)}) collective-permute-start(bf16[512,128]{1,0:T(8,128)(2,1)S(1)} %pad_maximum_fusion.1), channel_id=1, source_target_pairs={{0,16},{1,17},{2,18},{3,19},{4,20},{5,21},{6,22},{7,23},{8,24},{9,... | collective-permute-start | bytes 393224 | tf_op jit(solution)/shard_map/ppermute | solution.py:241
  30.3 3.9 %collective-permute-done.4 = bf16[512,128]{1,0:T(8,128)(2,1)S(1)} collective-permute-done((bf16[512,128]{1,0:T(8,128)(2,1)S(1)}, bf16[512,128]{1,0:T(8,128)(2,1)S(1)}, u32[]{:S(2)}, u32[]{:S(2)}) %collective-permute-start.4) | collective-permute-done | bytes 131104 | tf_op jit(solution)/shard_map/ppermute | solution.py:241
  34.2 0.0 copy-start.4
  34.2 1.6 %collective-permute-start.9 = (bf16[384,1536]{1,0:T(8,128)(2,1)S(1)}, bf16[384,1536]{1,0:T(8,128)(2,1)S(1)}, u32[]{:S(2)}, u32[]{:S(2)}) collective-permute-start(bf16[384,1536]{1,0:T(8,128)(2,1)S(1)} %dynamic_slice.15), channel_id=1, source_target_pairs={{0,16},{1,17},{2,18},{3,19},{4,20},{5,21},{6,22},{7,23},{8,24},{9,... | collective-permute-start | bytes 3538952 | tf_op jit(solution)/shard_map/ppermute | solution.py:241
  35.8 3.0 %constant_dynamic-slice_fusion.1 = (bf16[3072,384]{1,0:T(8,128)(2,1)S(1)}, bf16[3072,384]{1,0:T(8,128)(2,1)S(1)}) fusion(bf16[3072,768]{1,0:T(8,128)(2,1)} %param.33, s32[]{:T(128)S(6)} %select_n.38, bf16[3072,768]{1,0:T(8,128)(2,1)} %param.32), kind=kLoop, calls=%fused_computation.18 | loop fusion | bytes 9437188 | tf_op jit(solution)/shard_map/dynamic_slice | solution.py:298
  38.8 0.0 slice-start.1
  38.8 2.5 %pad_maximum_fusion.w_kv_ref = bf16[3072,768]{1,0:T(8,128)(2,1)} fusion(bf16[3072,384]{1,0:T(8,128)(2,1)S(1)} %get-tuple-element.13, bf16[3072,384]{1,0:T(8,128)(2,1)S(1)} %get-tuple-element.14), kind=kLoop, calls=%fused_computation | loop fusion | flops 9437184 | bytes 9437184 | tf_op jit(solution)/shard_map/concatenate | solution.py:295
  41.3 0.0 collective-permute-start.5
  41.3 1.7 %constant_dynamic-slice_fusion.3.w_q_ref = bf16[3072,384]{1,0:T(8,128)(2,1)} fusion(bf16[3072,768]{1,0:T(8,128)(2,1)S(1)} %bitcast.10, s32[]{:T(128)S(6)} %select_n.38), kind=kLoop, calls=%fused_computation.20 | loop fusion | bytes 4718596 | tf_op jit(solution)/shard_map/dynamic_slice | solution.py:294
  43.0 16.0 %collective-permute-done.9.w_across_ref = bf16[384,1536]{1,0:T(8,128)(2,1)S(1)} collective-permute-done((bf16[384,1536]{1,0:T(8,128)(2,1)S(1)}, bf16[384,1536]{1,0:T(8,128)(2,1)S(1)}, u32[]{:S(2)}, u32[]{:S(2)}) %collective-permute-start.9) | collective-permute-done | bytes 1179680 | tf_op jit(solution)/shard_map/ppermute | solution.py:241
  59.0 0.0 collective-permute-start.10
  59.0 0.0 collective-permute-done.5.far_ref
  59.0 0.7 copy-done.5
  59.7 42.3 %joint.1 = (bf16[192,384]{1,0:T(8,128)(2,1)}, bf16[192,384]{1,0:T(8,128)(2,1)}) custom-call(s32[2]{0:T(128)} %pad_add_fusion.info_ref, bf16[1024,128]{1,0:T(8,128)(2,1)} %copy-done.4, bf16[1024,128]{1,0:T(8,128)(2,1)} %copy-done.5, bf16[64,3072]{1,0:T(8,128)(2,1)} %w_in_ref.1, bf16[3,64,3072]{2,1,0:T(8,128)(2,1)} %w_hist_ref.1, f32[1,3072]{1,0:T(1,128)} %bitcast.11, ...), custom_call_target="tpu_custom_call" | custom-call | flops 24536678400 | bytes 7077888 | tf_op jit(solution)/shard_map/joint/pallas_call | solution.py:315
  102.0 0.6 collective-permute-start.6
  102.6 1.2 %collective-permute-start.8 = (bf16[192,384]{1,0:T(8,128)(2,1)}, bf16[192,384]{1,0:T(8,128)(2,1)S(1)}, u32[]{:S(2)}, u32[]{:S(2)}) collective-permute-start(bf16[192,384]{1,0:T(8,128)(2,1)} %get-tuple-element.11), channel_id=1, source_target_pairs={{0,17},{1,16},{2,19},{3,18},{4,21},{5,20},{6,23},{7,22},{8,25},{9,... | collective-permute-start | bytes 442376 | tf_op jit(solution)/shard_map/ppermute | solution.py:241
  103.8 0.5 collective-permute-start.7
  104.3 1.8 %constant_dynamic-slice_fusion.w_local_ref = bf16[768,1536]{1,0:T(8,128)(2,1)S(1)} fusion(bf16[768,3072]{1,0:T(8,128)(2,1)} %param.36, s32[]{:T(128)S(6)} %select_n.43), kind=kLoop, calls=%fused_computation.17 | loop fusion | bytes 4718596 | tf_op jit(solution)/shard_map/dynamic_slice | solution.py:307
  106.1 0.0 collective-permute-done.6.sib_ref
  106.1 6.0 %collective-permute-done.7.across_ref = bf16[192,384]{1,0:T(8,128)(2,1)S(1)} collective-permute-done((bf16[192,384]{1,0:T(8,128)(2,1)}, bf16[192,384]{1,0:T(8,128)(2,1)S(1)}, u32[]{:S(2)}, u32[]{:S(2)}) %collective-permute-start.7) | collective-permute-done | bytes 147488 | tf_op jit(solution)/shard_map/ppermute | solution.py:241
  112.1 0.0 collective-permute-done.8.corner_ref
  112.1 0.0 collective-permute-done.10.w_corner_ref
  112.1 2.8 %combine.1 = bf16[192,1536]{1,0:T(8,128)(2,1)} custom-call(s32[2]{0:T(128)S(1)} %copy-done.1, bf16[192,384]{1,0:T(8,128)(2,1)S(1)} %copy-done, bf16[192,384]{1,0:T(8,128)(2,1)S(1)} %collective-permute-done.6.sib_ref, bf16[192,384]{1,0:T(8,128)(2,1)S(1)} %collective-permute-done.7.across_ref, bf16[192,384]{1,0:T(8,128)(2,1)S(1)} %collective-permute-done.8.corner_ref, ...), custom_call_target="tpu_custom_call" | custom-call | tf_op jit(solution)/shard_map/combine/pallas_call | solution.py:347
  (16 shorter events, 0.1 us)
Async XLA Ops:
  1.0 6.7 %copy-start.2 = (bf16[2,128,192]{2,1,0:T(8,128)(2,1)}, bf16[2,128,192]{2,1,0:T(8,128)(2,1)S(1)}, u32[]{:S(2)}) copy-start(bf16[2,128,192]{2,1,0:T(8,128)(2,1)S(1)} %copy.27.feats_ref) | copy-start | bytes 294916
  1.0 6.6 %collective-permute-start = (bf16[2,128,192]{2,1,0:T(8,128)(2,1)S(1)}, bf16[2,128,192]{2,1,0:T(8,128)(2,1)S(1)}, u32[]{:S(2)}, u32[]{:S(2)}) collective-permute-start(bf16[2,128,192]{2,1,0:T(8,128)(2,1)S(1)} %copy.27.feats_ref), channel_id=1, source_target_pairs={{0,1},{1,2},{2,3},{3,4},{4,5},{5,6},{6,7},{7,8},{8,9},{9,10},{10,1... | collective-permute-start | bytes 294920 | tf_op jit(solution)/shard_map/ppermute | solution.py:263
  7.6 0.6 copy-start.3
  11.1 7.3 %collective-permute-start.1 = (bf16[64,128]{1,0:T(8,128)(2,1)}, bf16[64,128]{1,0:T(8,128)(2,1)S(1)}, u32[]{:S(2)}, u32[]{:S(2)}) collective-permute-start(bf16[64,128]{1,0:T(8,128)(2,1)} %encode.1), channel_id=1, source_target_pairs={{0,8},{1,9},{2,10},{3,11},{4,12},{5,13},{6,14},{7,15},{8,0},{9,1},... | collective-permute-start | bytes 49160 | tf_op jit(solution)/shard_map/ppermute | solution.py:241
  19.1 3.9 %collective-permute-start.2 = (bf16[128,128]{1,0:T(8,128)(2,1)S(1)}, bf16[128,128]{1,0:T(8,128)(2,1)S(1)}, u32[]{:S(2)}, u32[]{:S(2)}) collective-permute-start(bf16[128,128]{1,0:T(8,128)(2,1)S(1)} %pad_maximum_fusion.3), channel_id=1, source_target_pairs={{0,4},{1,5},{2,6},{3,7},{4,0},{5,1},{6,2},{7,3},{8,12},{9,13},{10,... | collective-permute-start | bytes 98312 | tf_op jit(solution)/shard_map/ppermute | solution.py:241
  23.7 4.3 %collective-permute-start.3 = (bf16[256,128]{1,0:T(8,128)(2,1)S(1)}, bf16[256,128]{1,0:T(8,128)(2,1)S(1)}, u32[]{:S(2)}, u32[]{:S(2)}) collective-permute-start(bf16[256,128]{1,0:T(8,128)(2,1)S(1)} %pad_maximum_fusion.2), channel_id=1, source_target_pairs={{0,2},{1,3},{2,0},{3,1},{4,6},{5,7},{6,4},{7,5},{8,10},{9,11},{10,... | collective-permute-start | bytes 196616 | tf_op jit(solution)/shard_map/ppermute | solution.py:241
  28.7 5.5 %collective-permute-start.4 = (bf16[512,128]{1,0:T(8,128)(2,1)S(1)}, bf16[512,128]{1,0:T(8,128)(2,1)S(1)}, u32[]{:S(2)}, u32[]{:S(2)}) collective-permute-start(bf16[512,128]{1,0:T(8,128)(2,1)S(1)} %pad_maximum_fusion.1), channel_id=1, source_target_pairs={{0,16},{1,17},{2,18},{3,19},{4,20},{5,21},{6,22},{7,23},{8,24},{9,... | collective-permute-start | bytes 393224 | tf_op jit(solution)/shard_map/ppermute | solution.py:241
  34.2 7.1 %copy-start.4 = (bf16[1024,128]{1,0:T(8,128)(2,1)}, bf16[1024,128]{1,0:T(8,128)(2,1)S(1)}, u32[]{:S(2)}) copy-start(bf16[1024,128]{1,0:T(8,128)(2,1)S(1)} %constant_dynamic-update-slice_fusion.near_ref) | copy-start | bytes 786436
  34.2 24.8 %collective-permute-start.9 = (bf16[384,1536]{1,0:T(8,128)(2,1)S(1)}, bf16[384,1536]{1,0:T(8,128)(2,1)S(1)}, u32[]{:S(2)}, u32[]{:S(2)}) collective-permute-start(bf16[384,1536]{1,0:T(8,128)(2,1)S(1)} %dynamic_slice.15), channel_id=1, source_target_pairs={{0,16},{1,17},{2,18},{3,19},{4,20},{5,21},{6,22},{7,23},{8,24},{9,... | collective-permute-start | bytes 3538952 | tf_op jit(solution)/shard_map/ppermute | solution.py:241
  35.8 5.5 %slice-start = ((s8[4718592]{0:T(1024)(128)(4,1)}), s8[4194304]{0:T(1024)(128)(4,1)S(1)}, s32[]{:S(2)}) async-start(s8[4718592]{0:T(1024)(128)(4,1)} %bitcast.9), calls=%async_computation | async-start | bytes 8388608
  38.8 2.5 %slice-start.1 = ((s8[4718592]{0:T(1024)(128)(4,1)}), s8[524288]{0:T(1024)(128)(4,1)S(1)}, s32[]{:S(2)}) async-start(s8[4718592]{0:T(1024)(128)(4,1)} %bitcast.9), calls=%async_computation.1 | async-start | bytes 1048576
  41.3 17.7 %collective-permute-start.5 = (bf16[1024,128]{1,0:T(8,128)(2,1)S(1)}, bf16[1024,128]{1,0:T(8,128)(2,1)S(1)}, u32[]{:S(2)}, u32[]{:S(2)}) collective-permute-start(bf16[1024,128]{1,0:T(8,128)(2,1)S(1)} %constant_dynamic-update-slice_fusion.near_ref), channel_id=1, source_target_pairs={{0,1},{1,0},{2,3},{3,2},{4,5},{5,4},{6,7},{7,6},{8,9},{9,8},{10,11... | collective-permute-start | bytes 786440 | tf_op jit(solution)/shard_map/ppermute | solution.py:241
  59.0 53.1 %collective-permute-start.10 = (bf16[384,1536]{1,0:T(8,128)(2,1)S(1)}, bf16[384,1536]{1,0:T(8,128)(2,1)S(1)}, u32[]{:S(2)}, u32[]{:S(2)}) collective-permute-start(bf16[384,1536]{1,0:T(8,128)(2,1)S(1)} %collective-permute-done.9.w_across_ref), channel_id=1, source_target_pairs={{0,1},{1,0},{2,3},{3,2},{4,5},{5,4},{6,7},{7,6},{8,9},{9,8},{10,11... | collective-permute-start | bytes 3538952 | tf_op jit(solution)/shard_map/ppermute | solution.py:241
  59.0 0.7 copy-start.5
  102.0 10.1 %copy-start = (bf16[192,384]{1,0:T(8,128)(2,1)S(1)}, bf16[192,384]{1,0:T(8,128)(2,1)}, u32[]{:S(2)}) copy-start(bf16[192,384]{1,0:T(8,128)(2,1)} %get-tuple-element.10.own_ref) | copy-start | bytes 442372
  102.0 10.1 %copy-start.1 = (s32[2]{0:T(128)S(1)}, s32[2]{0:T(128)}, u32[]{:S(2)}) copy-start(s32[2]{0:T(128)} %pad_add_fusion.info_ref) | copy-start | bytes 28
  102.0 4.1 %collective-permute-start.6 = (bf16[192,384]{1,0:T(8,128)(2,1)}, bf16[192,384]{1,0:T(8,128)(2,1)S(1)}, u32[]{:S(2)}, u32[]{:S(2)}) collective-permute-start(bf16[192,384]{1,0:T(8,128)(2,1)} %get-tuple-element.11), channel_id=1, source_target_pairs={{0,1},{1,0},{2,3},{3,2},{4,5},{5,4},{6,7},{7,6},{8,9},{9,8},{10,11... | collective-permute-start | bytes 442376 | tf_op jit(solution)/shard_map/ppermute | solution.py:241
  102.6 9.5 %collective-permute-start.8 = (bf16[192,384]{1,0:T(8,128)(2,1)}, bf16[192,384]{1,0:T(8,128)(2,1)S(1)}, u32[]{:S(2)}, u32[]{:S(2)}) collective-permute-start(bf16[192,384]{1,0:T(8,128)(2,1)} %get-tuple-element.11), channel_id=1, source_target_pairs={{0,17},{1,16},{2,19},{3,18},{4,21},{5,20},{6,23},{7,22},{8,25},{9,... | collective-permute-start | bytes 442376 | tf_op jit(solution)/shard_map/ppermute | solution.py:241
  103.8 8.4 %collective-permute-start.7 = (bf16[192,384]{1,0:T(8,128)(2,1)}, bf16[192,384]{1,0:T(8,128)(2,1)S(1)}, u32[]{:S(2)}, u32[]{:S(2)}) collective-permute-start(bf16[192,384]{1,0:T(8,128)(2,1)} %get-tuple-element.10.own_ref), channel_id=1, source_target_pairs={{0,16},{1,17},{2,18},{3,19},{4,20},{5,21},{6,22},{7,23},{8,24},{9,... | collective-permute-start | bytes 442376 | tf_op jit(solution)/shard_map/ppermute | solution.py:241

commit v2 on v1

v2 whole, which is shorter than its diff:
```python
import functools
import math

import jax
import jax.numpy as jnp
from jax import lax
from jax.experimental import pallas as pl
from jax.experimental.pallas import tpu as pltpu
from jax.sharding import PartitionSpec as P

STEPS = 50
EPSILON = 1e-06
F32 = jnp.float32
BF16 = jnp.bfloat16
VMEM = pl.BlockSpec(memory_space=pltpu.VMEM)
SMEM = pl.BlockSpec(memory_space=pltpu.SMEM)


def dot(a, b):
    return jnp.dot(a, b, preferred_element_type=F32)


def time_embed(step_index, width):
    half_width = width // 2
    frequency = jnp.exp(-math.log(10000.0) * jnp.arange(half_width, dtype=F32) / half_width)
    angles = (step_index[0].astype(F32) * frequency).reshape(1, half_width)
    return jnp.cos(angles), jnp.sin(angles)


def column_of(row):
    count = row.shape[1]
    diagonal = lax.broadcasted_iota(jnp.int32, (count, count), 0) == lax.broadcasted_iota(
        jnp.int32, (count, count), 1
    )
    return jnp.sum(jnp.where(diagonal, row.astype(F32), 0.0), axis=1, keepdims=True)


def encode_kernel(
    step_ref, feats_ref, earlier_ref, weight_ref, bias_ref, latent_ref, noise_ref, hist_ref,
    level_ref, out_ref,
):
    frames, channels, pixels = feats_ref.shape
    lat = noise_ref.shape[1]
    patch = lat * 4
    cells = pixels // 4
    bias = column_of(bias_ref[...])
    step = jnp.full((lat, pixels), step_ref[0].astype(F32), F32)
    sigma = (STEPS - step) / STEPS
    row = lax.broadcasted_iota(jnp.int32, (lat, frames * patch), 0)
    lane = lax.broadcasted_iota(jnp.int32, (lat, frames * patch), 1)
    pixel = lax.broadcasted_iota(jnp.int32, (pixels, frames * patch), 0)
    feature = lax.broadcasted_iota(jnp.int32, (pixels, frames * patch), 1)
    keep = (pixel % 4) == (feature % 4)
    collect = (
        lax.broadcasted_iota(jnp.int32, (cells, pixels), 1) // 4
        == lax.broadcasted_iota(jnp.int32, (cells, pixels), 0)
    ).astype(BF16)
    patches = jnp.zeros((cells, frames * patch), F32)
    for t in range(frames):
        total = jnp.zeros((channels, pixels), F32)
        for tap in range(3):
            source = t - tap
            window = feats_ref[source] if source >= 0 else earlier_ref[frames + source]
            total = total + dot(weight_ref[tap], window)
        total = total + bias
        hidden = (total / (1.0 + jnp.exp(-total))).astype(BF16)
        mixed = dot(latent_ref[...], hidden)
        noisy = ((1.0 - sigma) * mixed + sigma * noise_ref[t].astype(F32)).astype(BF16)
        spread = (lane // 4 == row + t * lat).astype(BF16)
        wide = lax.dot_general(noisy, spread, (((0,), (0,)), ((), ())), preferred_element_type=F32)
        wide = jnp.where(keep, wide, 0.0).astype(BF16)
        patches = patches + dot(collect, wide)
    out_ref[0:cells, :] = patches.astype(BF16)
    slots = hist_ref.shape[0]
    level = jnp.broadcast_to(column_of(level_ref[...]), (slots, patch))
    tail = jnp.concatenate([hist_ref[...].astype(F32), level], axis=1)
    tail = jnp.concatenate([tail, jnp.zeros((out_ref.shape[0] - cells - slots, 2 * patch), F32)], axis=0)
    out_ref[cells:, :] = tail.astype(BF16)


def exact_parts(values):
    high = values.astype(BF16)
    rest = values - high.astype(F32)
    middle = rest.astype(BF16)
    return high, middle, (rest - middle.astype(F32)).astype(BF16)


def joint_kernel(*refs, cells, block, pieces, owner_masks, tile, query_rows):
    near, far = refs[:pieces], refs[pieces : 2 * pieces]
    (
        count_ref, w_in_ref, w_hist_ref, cos_ref, sin_ref, gain_ref, w_query_ref, w_key_ref, w_value_ref,
        q_gain_ref, k_gain_ref, hist_ref, own_ref, sib_ref,
        patch_ref, wide_ref, w_q_ref, w_kv_ref, tok_a_ref, tok_b_ref, q_ref, k_ref, v_ref, s_a_ref,
        s_b_ref, x_ref, out_ref, semaphores,
    ) = refs[2 * pieces :]
    heads, keys, size = k_ref.shape
    patch, width = w_in_ref.shape
    depth = heads * size
    lanes = near[0].shape[1]
    frames = lanes // patch
    rows = 4 * cells * frames
    group = lax.axis_index("grp")
    place = lax.axis_index("seq")
    start = pl.multiple_of((place % 2) * depth, depth)
    copies = [
        pltpu.make_async_copy(w_query_ref.at[:, pl.ds(start, depth)], w_q_ref, semaphores.at[0]),
        pltpu.make_async_copy(
            w_key_ref.at[:, pl.ds(start, depth)], w_kv_ref.at[:, 0:depth], semaphores.at[1]
        ),
        pltpu.make_async_copy(
            w_value_ref.at[:, pl.ds(start, depth)], w_kv_ref.at[:, depth : 2 * depth], semaphores.at[2]
        ),
    ]
    for copy in copies:
        copy.start()

    step = 512
    lane = lax.broadcasted_iota(jnp.int32, (1, lanes), 1)
    for n, source in ((0, cos_ref), (width // 2, sin_ref)):
        values = source[...]
        row = lax.broadcasted_iota(jnp.int32, (lanes - patch, values.shape[1]), 0)
        high, middle, low = exact_parts(values)
        extra = jnp.where(row == 0, high.astype(F32), 0.0)
        extra = jnp.where(row == 1, middle.astype(F32), extra)
        extra = jnp.where(row == 2, low.astype(F32), extra)
        wide_ref[patch:lanes, n : n + values.shape[1]] = extra.astype(BF16)
    wide_ref[0:patch, :] = w_in_ref[...]
    gram = jnp.zeros((lanes, lanes), F32)
    for n in range(0, width, step):
        part = wide_ref[:, n : n + step]
        gram = gram + lax.dot_general(part, part, (((1,), (1,)), ((), ())), preferred_element_type=F32)
    gram_parts = jnp.concatenate(exact_parts(gram), axis=0)

    ones = jnp.where(lane < patch + 3, 1.0, 0.0)
    held = near[0].shape[0] // block
    half = pieces * held
    fours = []
    for sources in (near, far):
        mine = sources[0][0:cells, :]
        theirs = sources[pieces // 2][0:cells, :]
        fours.append(jnp.where(group == 0, mine, theirs))
        fours.append(jnp.where(group == 0, theirs, mine))
    for sources in (near, far):
        for p in range(half):
            if p != 0 and p != half // 2:
                fours.append((sources[p // held], (p % held) * block))
    for spot, item in enumerate(fours):
        values = (item[0][item[1] : item[1] + cells, :] if isinstance(item, tuple) else item).astype(F32)
        for t in range(frames):
            moved = values if t == 0 else pltpu.roll(values, lanes - t * patch, 1)
            at = (spot // 4) * rows + t * 4 * cells + (spot % 4) * cells
            patch_ref[at : at + cells, :] = jnp.where(lane < patch, moved, ones).astype(BF16)

    def tokens_of(i, tok_ref):
        source = patch_ref[pl.ds(pl.multiple_of(i * tile, tile), tile), :]
        mixed = dot(jnp.concatenate([source] * 3, axis=1), gram_parts)
        mean = jnp.sum(mixed * source.astype(F32), axis=1, keepdims=True) / width
        inverse = lax.rsqrt(mean + EPSILON)
        for n in range(0, width, step):
            x = dot(source, wide_ref[:, n : n + step])
            tok_ref[:, n : n + step] = (x * inverse * gain_ref[:, n : n + step]).astype(BF16)

    def head_norm(values, gain):
        mean = jnp.mean(values * values, axis=1, keepdims=True)
        return (values * lax.rsqrt(mean + EPSILON) * gain).astype(BF16)

    def project(tokens, at):
        both = dot(tokens, w_kv_ref[...])
        count = tokens.shape[0]
        for h in range(heads):
            k_ref[h, pl.ds(at, count), :] = head_norm(both[:, h * size : (h + 1) * size], k_gain_ref[...])
            v_ref[h, pl.ds(at, count), :] = both[:, (heads + h) * size : (heads + h + 1) * size].astype(BF16)

    tokens_of(0, tok_a_ref)
    copies[0].wait()
    q = dot(tok_a_ref[0:rows, :], w_q_ref[...])
    for h in range(heads):
        q_ref[h] = head_norm(q[:, h * size : (h + 1) * size], q_gain_ref[...])
    copies[1].wait()
    copies[2].wait()
    tiles = patch_ref.shape[0] // tile

    def pair(j, carry):
        tokens_of(2 * j + 1, tok_b_ref)
        project(tok_a_ref[...], pl.multiple_of(2 * j * tile, tile))
        tokens_of(2 * j + 2, tok_a_ref)
        project(tok_b_ref[...], pl.multiple_of((2 * j + 1) * tile, tile))
        return carry

    if tiles > 2:
        lax.fori_loop(0, tiles // 2 - 1, pair, 0)
    tokens_of(tiles - 1, tok_b_ref)
    project(tok_a_ref[...], (tiles - 2) * tile)
    project(tok_b_ref[...], (tiles - 1) * tile)

    section = tiles * tile
    slots = hist_ref.shape[0]
    levels = w_hist_ref.shape[0]
    owners = len(owner_masks)
    spread = 128 // slots
    owner_blocks = [
        (sources[p // held], (p % held) * block + cells) for sources in (near, far) for p in range(half // 2)
    ]
    biases = []
    for r in range(0, owners, spread):
        taken = owner_blocks[r : r + spread]
        source = jnp.concatenate([ref[at : at + 16, :].astype(F32)[0:slots] for ref, at in taken], axis=0)
        count = source.shape[0]
        values, level = source[:, 0:patch], source[:, patch : 2 * patch]
        parts = [jnp.where(level == v, values, 0.0).astype(BF16) for v in range(levels)]
        squares = jnp.zeros((count, 128), F32)
        for n in range(0, width, step):
            x = dot(parts[0], w_hist_ref[0, :, n : n + step])
            for v in range(1, levels):
                x = x + dot(parts[v], w_hist_ref[v, :, n : n + step])
            x_ref[0:count, n : n + step] = x
            for m in range(0, step, 128):
                squares = squares + x[:, m : m + 128] * x[:, m : m + 128]
        inverse = lax.rsqrt(jnp.sum(squares, axis=1, keepdims=True) / width + EPSILON)
        for n in range(0, width, step):
            tok_a_ref[0:count, n : n + step] = (
                x_ref[0:count, n : n + step] * inverse * gain_ref[:, n : n + step]
            ).astype(BF16)
        project(tok_a_ref[0:count, :], section + r * slots)
        slot = lax.broadcasted_iota(jnp.int32, (1, count), 1)
        live = jnp.zeros((1, count), jnp.int32)
        for o in range(len(taken)):
            live = jnp.where(slot // slots == o, count_ref[place ^ owner_masks[r + o]], live)
        biases.append(jnp.where(slot % slots < live, 0.0, -1e30))

    scale = math.log2(math.e) / math.sqrt(size)
    chunk = 512
    fold = 128
    parts = [(a, chunk, None) for a in range(0, section, chunk)]
    parts += [(section + r * spread * slots, b.shape[1], b) for r, b in enumerate(biases)]
    units = [(h, a) for h in range(heads) for a in range(0, rows, query_rows)]
    buffers = (s_a_ref, s_b_ref)

    def score(unit, state, part):
        h, a = units[unit]
        at, length, bias = part
        for n in range(at, at + length, 256):
            span = min(256, at + length - n)
            s = lax.dot_general(
                q_ref[h, a : a + query_rows, :], k_ref[h, n : n + span, :], (((1,), (1,)), ((), ())),
                preferred_element_type=F32,
            )
            if bias is not None:
                s = s + bias[:, n - at : n - at + span]
            buffers[unit % 2][:, n : n + span] = s
            for m in range(0, span, fold):
                state = jnp.maximum(state, s[:, m : m + fold])
        return state

    fresh = jnp.full((query_rows, fold), -3e38, F32)
    state = fresh
    for part in parts:
        state = score(0, state, part)
    for unit, (h, a) in enumerate(units):
        top = jnp.max(state, axis=1, keepdims=True)
        state = fresh
        total = jnp.zeros((query_rows, fold), F32)
        weighted = jnp.zeros((query_rows, size), F32)
        for part in parts:
            at, length, _ = part
            soft = jnp.exp2((buffers[unit % 2][:, at : at + length] - top) * scale)
            for m in range(0, length, fold):
                total = total + soft[:, m : m + fold]
            weighted = weighted + dot(soft.astype(BF16), v_ref[h, at : at + length, :])
            if unit + 1 < len(units):
                state = score(unit + 1, state, part)
        out_ref[a : a + query_rows, h * size : (h + 1) * size] = (
            weighted / jnp.sum(total, axis=1, keepdims=True)
        ).astype(BF16)
    part = 2 * cells
    for t in range(frames):
        base = t * 4 * cells
        own_ref[t * part : (t + 1) * part, :] = out_ref[base : base + part, :]
        sib_ref[t * part : (t + 1) * part, :] = out_ref[base + part : base + 2 * part, :]


def combine_kernel(
    own_ref, sib_ref, across_ref, corner_ref, w_local_ref, w_across_ref, w_corner_ref, out_ref
):
    core = lax.axis_index("seq") % 2
    depth = own_ref.shape[1]
    mine = pl.ds(pl.multiple_of(core * depth, depth), depth)
    other = pl.ds(pl.multiple_of((1 - core) * depth, depth), depth)
    step = 512
    for n in range(0, out_ref.shape[1], step):
        columns = slice(n, n + step)
        total = dot(own_ref[...], w_local_ref[mine, columns])
        total = total + dot(sib_ref[...], w_local_ref[other, columns])
        total = total + dot(across_ref[...], w_across_ref[:, columns])
        total = total + dot(corner_ref[...], w_corner_ref[:, columns])
        out_ref[:, columns] = total.astype(BF16)


def flip(value, mask, seq_count):
    pairs = [(i, i ^ mask) for i in range(2 * seq_count)]
    return lax.ppermute(value, ("grp", "seq"), pairs)


def local(
    feats, conv_weight, conv_bias, latent_projection_weight, noise, step_index, hist, hist_level,
    hist_count, w_in, w_hist, norm_gain, w_query, w_key, w_value, q_gain, k_gain, w_out,
):
    frame_count, channels, pixels = feats.shape
    seq_count = lax.axis_size("seq")
    group = lax.axis_index("grp")
    place = lax.axis_index("seq")
    core = place % 2
    width = w_in.shape[1]
    patch = w_in.shape[0]
    cells = pixels // 4
    slots = hist.shape[0]
    block = cells + 16
    lanes = frame_count * patch
    size = q_gain.shape[0]
    heads = w_query.shape[1] // size // 2
    depth = heads * size

    earlier = lax.ppermute(feats, "seq", [(i, i + 1) for i in range(seq_count - 1)])
    gathered = pl.pallas_call(
        encode_kernel,
        out_shape=jax.ShapeDtypeStruct((block, lanes), BF16),
        in_specs=[SMEM] + [VMEM] * 8,
        out_specs=VMEM,
        name="encode",
    )(
        step_index, feats, earlier, conv_weight, conv_bias.reshape(1, channels),
        latent_projection_weight, noise, hist, hist_level.reshape(1, slots),
    )

    bits = []
    bit = seq_count // 2
    while bit > 1:
        bits.append(bit)
        bit //= 2
    owner_masks = [0]
    for bit in bits:
        owner_masks = owner_masks + [m ^ bit for m in owner_masks]
    owner_masks = tuple(owner_masks + [m ^ 1 for m in owner_masks])
    bits.append(seq_count)
    rounds = [bits[i : i + 2] for i in range(len(bits) % 2, len(bits), 2)]
    if len(bits) % 2:
        rounds = [bits[:1]] + rounds
    for number, pair in enumerate(rounds):
        masks = [0] + [pair[0]] + ([pair[1], pair[0] ^ pair[1]] if len(pair) > 1 else [])
        near = [gathered] + [flip(gathered, mask, seq_count) for mask in masks[1:]]
        if number + 1 < len(rounds):
            gathered = jnp.concatenate(near, axis=0)
    far = [flip(piece, 1, seq_count) for piece in near]

    columns = w_out.shape[1] // 2
    w_send = lax.dynamic_slice(w_out, (core * depth, (1 - group) * columns), (depth, columns))
    w_send, *near = lax.optimization_barrier((w_send, *near))
    w_across = flip(w_send, seq_count, seq_count)
    w_local = lax.dynamic_slice_in_dim(w_out, group * columns, columns, axis=1)

    tokens = 2 * seq_count * frame_count * cells
    keys = tokens + slots * seq_count
    rows = frame_count * 4 * cells
    tile = 2 * rows
    query_rows = rows
    while 2 * query_rows * keys * 4 > 12 * 2**20:
        query_rows //= 2
    cos, sin = time_embed(step_index, width)
    anywhere = pl.BlockSpec(memory_space=pl.ANY)
    own, sib = pl.pallas_call(
        functools.partial(
            joint_kernel, cells=cells, block=block, pieces=len(near), owner_masks=owner_masks, tile=tile,
            query_rows=query_rows,
        ),
        out_shape=[jax.ShapeDtypeStruct((rows // 2, depth), BF16)] * 2,
        in_specs=[VMEM] * (2 * len(near)) + [SMEM] + [VMEM] * 5 + [anywhere] * 3 + [VMEM] * 3,
        out_specs=[VMEM] * 2,
        scratch_shapes=[
            pltpu.VMEM((tokens, lanes), BF16),
            pltpu.VMEM((lanes, width), BF16),
            pltpu.VMEM((width, depth), BF16),
            pltpu.VMEM((width, 2 * depth), BF16),
            pltpu.VMEM((tile, width), BF16),
            pltpu.VMEM((tile, width), BF16),
            pltpu.VMEM((heads, rows, size), BF16),
            pltpu.VMEM((heads, keys, size), BF16),
            pltpu.VMEM((heads, keys, size), BF16),
            pltpu.VMEM((query_rows, keys), F32),
            pltpu.VMEM((query_rows, keys), F32),
            pltpu.VMEM((128, width), F32),
            pltpu.VMEM((rows, depth), BF16),
            pltpu.SemaphoreType.DMA((3,)),
        ],
        compiler_params=pltpu.CompilerParams(vmem_limit_bytes=60 * 2**20),
        cost_estimate=pl.CostEstimate(
            flops=2 * keys * width * 3 * depth + 4 * rows * keys * depth,
            bytes_accessed=6 * width * depth,
            transcendentals=rows * keys * heads,
        ),
        name="joint",
    )(
        *near, *far, hist_count, w_in, w_hist, cos, sin, norm_gain.reshape(1, width), w_query, w_key,
        w_value, q_gain.reshape(1, size), k_gain.reshape(1, size), hist,
    )
    w_across, own, sib = lax.optimization_barrier((w_across, own, sib))
    w_corner = flip(w_across, 1, seq_count)
    from_sib = flip(sib, 1, seq_count)
    across = flip(own, seq_count, seq_count)
    corner = flip(sib, seq_count + 1, seq_count)
    return pl.pallas_call(
        combine_kernel,
        out_shape=jax.ShapeDtypeStruct((rows // 2, columns), BF16),
        in_specs=[VMEM] * 7,
        out_specs=VMEM,
        compiler_params=pltpu.CompilerParams(vmem_limit_bytes=24 * 2**20),
        name="combine",
    )(own, from_sib, across, corner, w_local, w_across, w_corner)


def solution(mesh):
    placed = (
        P("seq", None, "grp"), P(), P(), P(), P("seq", None, "grp"), P(), P("seq", None), P("seq"),
        P(), P(), P(), P(), P(None, "grp"), P(None, "grp"), P(None, "grp"), P(), P(), P("grp", None),
    )
    return jax.shard_map(local, mesh=mesh, in_specs=placed, out_specs=P("seq", "grp"), check_vma=False)
```

time: 115 us -> 78.6 us (0.68)
  waiting for transfers between devices: 31 us -> 13 us
  Pallas kernels: 47.8 us -> 38.1 us
  local copies, waits for them, and re-layouts: 12.9 us -> 5.44 us
  other arithmetic: 7.58 us -> 1.54 us
  starting transfers between devices: 14.7 us -> 19.3 us
    ppermute x10 -> x15, waiting for transfers between devices: 31 us -> 12.7 us  [flip(): return lax.ppermute(value, ('grp', 'seq'), pairs)]
    pallas_call x1, Pallas kernels: 42.3 us -> 33.1 us  [local(): pl.pallas_call(functools.partial(joint_kernel, cells=cells, block=block,...]
    dynamic_slice x2 -> x0, local copies, waits for them, and re-layouts: 4.69 us -> none  [the longest x1 3 us: local(): lax.dynamic_slice_in_dim(w_value, core * depth, depth, axis=1)]
    ppermute x10 -> x15, starting transfers between devices: 12.3 us -> 16.9 us  [flip(): return lax.ppermute(value, ('grp', 'seq'), pairs)]
    concatenate x5 -> x1, other arithmetic: 5.28 us -> 0.72 us  [local(): gathered = jnp.concatenate(near, axis=0)]
    reshape x1 -> x0, local copies, waits for them, and re-layouts: 1.32 us -> none  [local(): hist_level.reshape(slots, 1)]
    unnamed x21 -> x23, local copies, waits for them, and re-layouts: 3.11 us -> 2.28 us
  transfers between devices with their start and end apart: 11 -> 16, of which waited for: 5 -> 8; matrix products, arithmetic and copies ran while one was open for 14% -> 5% of each run, Pallas kernels for 37% -> 42%
where the time goes in v2:
time: 78.6 us; the launch traced here: 78.3 us
  Pallas kernels  38.1 us (48%)
  starting transfers between devices  19.3 us (25%)
  waiting for transfers between devices  13 us (17%)
  local copies, waits for them, and re-layouts  5.44 us (7%)
  other arithmetic  1.54 us (2%)
  between operations  0.8 us (1%)
    pallas_call x1, Pallas kernels, local(): pl.pallas_call(functools.partial(joint_kernel, cells=cells, block=block,...  33.1 us
    ppermute x15, starting transfers between devices, flip(): return lax.ppermute(value, ('grp', 'seq'), pairs)  16.9 us
    ppermute x15, waiting for transfers between devices, flip(): return lax.ppermute(value, ('grp', 'seq'), pairs)  12.7 us
    pallas_call x1, Pallas kernels, local(): pl.pallas_call(encode_kernel, out_shape=jax.ShapeDtypeStruct((block, lane...  2.79 us
    ppermute x1, starting transfers between devices, local(): lax.ppermute(feats, 'seq', [(i, i + 1) for i in range(seq_count - 1)])  2.4 us
    unnamed x23, local copies, waits for them, and re-layouts  2.28 us
    pallas_call x1, Pallas kernels, local(): pl.pallas_call(combine_kernel, out_shape=jax.ShapeDtypeStruct((rows // 2,...  2.21 us
    dynamic_slice x1, local copies, waits for them, and re-layouts, local(): w_local = lax.dynamic_slice_in_dim(w_out, group * columns, columns, axis=1)  1.82 us
  transfers between devices with their start and end apart: 16, of which 8 were waited for; matrix products, arithmetic and copies ran while one was open for 5% of the time, Pallas kernels for 42%

profile of v2, /device:TPU:0, one launch (start us, length us, event | category | flops | bytes accessed | tf_op | source)
XLA Modules:
  0.0 78.3 jit_solution(6982750591051810154)
XLA Ops:
  0.0 1.0 %copy.20.feats_ref = bf16[2,128,192]{2,1,0:T(8,128)(2,1)S(1)} copy(bf16[2,128,192]{1,2,0:T(8,128)(2,1)} %param.18) | data formatting | bytes 196608 | tf_op args[0]
  1.0 0.0 copy-start.1
  1.0 2.4 %collective-permute-start = (bf16[2,128,192]{2,1,0:T(8,128)(2,1)S(1)}, bf16[2,128,192]{2,1,0:T(8,128)(2,1)S(1)}, u32[]{:S(2)}, u32[]{:S(2)}) collective-permute-start(bf16[2,128,192]{2,1,0:T(8,128)(2,1)S(1)} %copy.20.feats_ref), channel_id=1, source_target_pairs={{0,1},{1,2},{2,3},{3,4},{4,5},{5,6},{6,7},{7,8},{8,9},{9,10},{10,1... | collective-permute-start | bytes 294920 | tf_op jit(solution)/shard_map/ppermute | solution.py:323
  4.1 0.3 collective-permute-done.earlier_ref
  4.4 0.7 copy-done.2
  5.1 2.8 %encode.1 = bf16[64,128]{1,0:T(8,128)(2,1)} custom-call(s32[1]{0:T(128)S(6)} %copy.21.step_ref, bf16[2,128,192]{2,1,0:T(8,128)(2,1)} %copy-done.1, bf16[2,128,192]{2,1,0:T(8,128)(2,1)} %copy-done.2, bf16[3,128,128]{2,1,0:T(8,128)(2,1)} %weight_ref.1, f32[1,128]{1,0:T(1,128)} %bitcast.6, bf16[16,128]{1,0:T(8,128)(2,1)} %latent_ref.1, ...), custom_call_target="tpu_custom_call" | custom-call | tf_op jit(solution)/shard_map/encode/pallas_call | solution.py:324
  7.8 8.9 %collective-permute-start.3 = (bf16[64,128]{1,0:T(8,128)(2,1)}, bf16[64,128]{1,0:T(8,128)(2,1)S(1)}, u32[]{:S(2)}, u32[]{:S(2)}) collective-permute-start(bf16[64,128]{1,0:T(8,128)(2,1)} %encode.1), channel_id=1, source_target_pairs={{0,12},{1,13},{2,14},{3,15},{4,8},{5,9},{6,10},{7,11},{8,4},{9,5},... | collective-permute-start | bytes 49160 | tf_op jit(solution)/shard_map/ppermute | solution.py:301
  16.7 0.0 collective-permute-start.2
  16.7 0.6 collective-permute-start.1
  17.3 1.5 %collective-permute-done.3 = bf16[64,128]{1,0:T(8,128)(2,1)S(1)} collective-permute-done((bf16[64,128]{1,0:T(8,128)(2,1)}, bf16[64,128]{1,0:T(8,128)(2,1)S(1)}, u32[]{:S(2)}, u32[]{:S(2)}) %collective-permute-start.3) | collective-permute-done | bytes 16416 | tf_op jit(solution)/shard_map/ppermute | solution.py:301
  18.8 1.9 %collective-permute-done.2 = bf16[64,128]{1,0:T(8,128)(2,1)S(1)} collective-permute-done((bf16[64,128]{1,0:T(8,128)(2,1)}, bf16[64,128]{1,0:T(8,128)(2,1)S(1)}, u32[]{:S(2)}, u32[]{:S(2)}) %collective-permute-start.2) | collective-permute-done | bytes 16416 | tf_op jit(solution)/shard_map/ppermute | solution.py:301
  20.7 0.9 %collective-permute-done.1 = bf16[64,128]{1,0:T(8,128)(2,1)S(1)} collective-permute-done((bf16[64,128]{1,0:T(8,128)(2,1)}, bf16[64,128]{1,0:T(8,128)(2,1)S(1)}, u32[]{:S(2)}, u32[]{:S(2)}) %collective-permute-start.1) | collective-permute-done | bytes 16416 | tf_op jit(solution)/shard_map/ppermute | solution.py:301
  21.6 0.7 pad_maximum_fusion.refs_0_
  22.3 1.5 %collective-permute-start.6 = (bf16[256,128]{1,0:T(8,128)(2,1)S(1)}, bf16[256,128]{1,0:T(8,128)(2,1)S(1)}, u32[]{:S(2)}, u32[]{:S(2)}) collective-permute-start(bf16[256,128]{1,0:T(8,128)(2,1)S(1)} %pad_maximum_fusion.refs_0_), channel_id=1, source_target_pairs={{0,18},{1,19},{2,16},{3,17},{4,22},{5,23},{6,20},{7,21},{8,26},{9,... | collective-permute-start | bytes 196616 | tf_op jit(solution)/shard_map/ppermute | solution.py:301
  23.9 0.5 collective-permute-start.5
  24.4 1.4 %collective-permute-start.4 = (bf16[256,128]{1,0:T(8,128)(2,1)S(1)}, bf16[256,128]{1,0:T(8,128)(2,1)S(1)}, u32[]{:S(2)}, u32[]{:S(2)}) collective-permute-start(bf16[256,128]{1,0:T(8,128)(2,1)S(1)} %pad_maximum_fusion.refs_0_), channel_id=1, source_target_pairs={{0,2},{1,3},{2,0},{3,1},{4,6},{5,7},{6,4},{7,5},{8,10},{9,11},{10,... | collective-permute-start | bytes 196616 | tf_op jit(solution)/shard_map/ppermute | solution.py:301
  25.8 0.0 collective-permute-start.8
  25.8 1.7 %collective-permute-done.6.refs_3_ = bf16[256,128]{1,0:T(8,128)(2,1)S(1)} collective-permute-done((bf16[256,128]{1,0:T(8,128)(2,1)S(1)}, bf16[256,128]{1,0:T(8,128)(2,1)S(1)}, u32[]{:S(2)}, u32[]{:S(2)}) %collective-permute-start.6) | collective-permute-done | bytes 65568 | tf_op jit(solution)/shard_map/ppermute | solution.py:301
  27.5 0.0 collective-permute-start.11
  27.5 0.6 collective-permute-done.5.refs_2_
  28.1 0.0 collective-permute-start.10
  28.1 0.5 collective-permute-done.4.refs_1_
  28.7 0.0 collective-permute-start.9
  28.7 0.8 %fusion = (f32[1,1536]{1,0:T(1,128)}, f32[1,1536]{1,0:T(1,128)}) fusion(f32[]{:T(128)} %bitcast.2), kind=kLoop, calls=%fused_computation.2 | loop fusion | flops 3072 | bytes 12292 | tf_op jit(solution)/shard_map/sin | solution.py:27
  29.5 1.3 %dynamic_slice.6 = bf16[384,1536]{1,0:T(8,128)(2,1)S(1)} dynamic-slice(bf16[768,3072]{1,0:T(8,128)(2,1)} %param.35, s32[]{:T(128)S(6)} %select_n.17, s32[]{:T(128)S(6)} %select_n.18), dynamic_slice_sizes={384,1536} | dynamic-slice | bytes 2359300 | tf_op jit(solution)/shard_map/dynamic_slice | solution.py:356
  30.8 1.6 %collective-permute-start.7 = (bf16[384,1536]{1,0:T(8,128)(2,1)S(1)}, bf16[384,1536]{1,0:T(8,128)(2,1)S(1)}, u32[]{:S(2)}, u32[]{:S(2)}) collective-permute-start(bf16[384,1536]{1,0:T(8,128)(2,1)S(1)} %dynamic_slice.6), channel_id=1, source_target_pairs={{0,16},{1,17},{2,18},{3,19},{4,20},{5,21},{6,22},{7,23},{8,24},{9,... | collective-permute-start | bytes 3538952 | tf_op jit(solution)/shard_map/ppermute | solution.py:301
  32.4 0.0 collective-permute-done.8.refs_4_
  32.4 0.0 collective-permute-done.11.refs_7_
  32.4 0.0 collective-permute-done.10.refs_6_
  32.4 0.0 collective-permute-done.9.refs_5_
  32.4 0.0 copy-start.10
  32.4 0.0 copy-done.3
  32.5 0.5 copy-done.7
  33.0 0.0 copy-done.8
  33.0 0.0 copy-done.9
  33.1 0.0 copy-done.10
  33.1 33.1 %joint.1 = (bf16[192,384]{1,0:T(8,128)(2,1)}, bf16[192,384]{1,0:T(8,128)(2,1)}) custom-call(bf16[256,128]{1,0:T(8,128)(2,1)} %copy-done.3, bf16[256,128]{1,0:T(8,128)(2,1)} %copy-done.6, bf16[256,128]{1,0:T(8,128)(2,1)} %copy-done.5, bf16[256,128]{1,0:T(8,128)(2,1)} %copy-done.4, bf16[256,128]{1,0:T(8,128)(2,1)} %copy-done.7, bf16[256,128]{1,0:T(8,128)(2,1)} %copy-done.10, ...), custom_call_target="tpu_custom_call" | custom-call | flops 24536678400 | bytes 7077888 | tf_op jit(solution)/shard_map/joint/pallas_call | solution.py:370
  66.2 0.0 collective-permute-done.7.w_across_ref
  66.2 0.3 collective-permute-start.15
  66.5 0.4 collective-permute-start.14
  67.0 0.2 collective-permute-start.12
  67.2 1.5 %collective-permute-start.13 = (bf16[192,384]{1,0:T(8,128)(2,1)}, bf16[192,384]{1,0:T(8,128)(2,1)S(1)}, u32[]{:S(2)}, u32[]{:S(2)}) collective-permute-start(bf16[192,384]{1,0:T(8,128)(2,1)} %get-tuple-element.22.own_ref), channel_id=1, source_target_pairs={{0,16},{1,17},{2,18},{3,19},{4,20},{5,21},{6,22},{7,23},{8,24},{9,... | collective-permute-start | bytes 442376 | tf_op jit(solution)/shard_map/ppermute | solution.py:301
  68.7 1.8 %constant_dynamic-slice_fusion.w_local_ref = bf16[768,1536]{1,0:T(8,128)(2,1)S(1)} fusion(bf16[768,3072]{1,0:T(8,128)(2,1)} %param.35, s32[]{:T(128)S(6)} %select_n.19), kind=kLoop, calls=%fused_computation.4 | loop fusion | bytes 4718596 | tf_op jit(solution)/shard_map/dynamic_slice | solution.py:359
  70.5 5.6 %collective-permute-done.13.across_ref = bf16[192,384]{1,0:T(8,128)(2,1)S(1)} collective-permute-done((bf16[192,384]{1,0:T(8,128)(2,1)}, bf16[192,384]{1,0:T(8,128)(2,1)S(1)}, u32[]{:S(2)}, u32[]{:S(2)}) %collective-permute-start.13) | collective-permute-done | bytes 147488 | tf_op jit(solution)/shard_map/ppermute | solution.py:301
  76.0 0.0 collective-permute-done.14.corner_ref
  76.1 0.0 collective-permute-done.12.sib_ref
  76.1 0.0 collective-permute-done.15.w_corner_ref
  76.1 2.2 %combine.1 = bf16[192,1536]{1,0:T(8,128)(2,1)} custom-call(bf16[192,384]{1,0:T(8,128)(2,1)S(1)} %copy-done, bf16[192,384]{1,0:T(8,128)(2,1)S(1)} %collective-permute-done.12.sib_ref, bf16[192,384]{1,0:T(8,128)(2,1)S(1)} %collective-permute-done.13.across_ref, bf16[192,384]{1,0:T(8,128)(2,1)S(1)} %collective-permute-done.14.corner_ref, ...), custom_call_target="tpu_custom_call" | custom-call | tf_op jit(solution)/shard_map/combine/pallas_call | solution.py:410
  (14 shorter events, 0.0 us)
Async XLA Ops:
  1.0 3.4 %copy-start.1 = (bf16[2,128,192]{2,1,0:T(8,128)(2,1)}, bf16[2,128,192]{2,1,0:T(8,128)(2,1)S(1)}, u32[]{:S(2)}) copy-start(bf16[2,128,192]{2,1,0:T(8,128)(2,1)S(1)} %copy.20.feats_ref) | copy-start | bytes 294916
  1.0 3.4 %collective-permute-start = (bf16[2,128,192]{2,1,0:T(8,128)(2,1)S(1)}, bf16[2,128,192]{2,1,0:T(8,128)(2,1)S(1)}, u32[]{:S(2)}, u32[]{:S(2)}) collective-permute-start(bf16[2,128,192]{2,1,0:T(8,128)(2,1)S(1)} %copy.20.feats_ref), channel_id=1, source_target_pairs={{0,1},{1,2},{2,3},{3,4},{4,5},{5,6},{6,7},{7,8},{8,9},{9,10},{10,1... | collective-permute-start | bytes 294920 | tf_op jit(solution)/shard_map/ppermute | solution.py:323
  4.4 0.7 copy-start.2
  7.8 10.9 %collective-permute-start.3 = (bf16[64,128]{1,0:T(8,128)(2,1)}, bf16[64,128]{1,0:T(8,128)(2,1)S(1)}, u32[]{:S(2)}, u32[]{:S(2)}) collective-permute-start(bf16[64,128]{1,0:T(8,128)(2,1)} %encode.1), channel_id=1, source_target_pairs={{0,12},{1,13},{2,14},{3,15},{4,8},{5,9},{6,10},{7,11},{8,4},{9,5},... | collective-permute-start | bytes 49160 | tf_op jit(solution)/shard_map/ppermute | solution.py:301
  16.7 3.9 %collective-permute-start.2 = (bf16[64,128]{1,0:T(8,128)(2,1)}, bf16[64,128]{1,0:T(8,128)(2,1)S(1)}, u32[]{:S(2)}, u32[]{:S(2)}) collective-permute-start(bf16[64,128]{1,0:T(8,128)(2,1)} %encode.1), channel_id=1, source_target_pairs={{0,4},{1,5},{2,6},{3,7},{4,0},{5,1},{6,2},{7,3},{8,12},{9,13},{10,... | collective-permute-start | bytes 49160 | tf_op jit(solution)/shard_map/ppermute | solution.py:301
  16.7 4.8 %collective-permute-start.1 = (bf16[64,128]{1,0:T(8,128)(2,1)}, bf16[64,128]{1,0:T(8,128)(2,1)S(1)}, u32[]{:S(2)}, u32[]{:S(2)}) collective-permute-start(bf16[64,128]{1,0:T(8,128)(2,1)} %encode.1), channel_id=1, source_target_pairs={{0,8},{1,9},{2,10},{3,11},{4,12},{5,13},{6,14},{7,15},{8,0},{9,1},... | collective-permute-start | bytes 49160 | tf_op jit(solution)/shard_map/ppermute | solution.py:301
  22.3 10.1 %copy-start.3 = (bf16[256,128]{1,0:T(8,128)(2,1)}, bf16[256,128]{1,0:T(8,128)(2,1)S(1)}, u32[]{:S(2)}) copy-start(bf16[256,128]{1,0:T(8,128)(2,1)S(1)} %pad_maximum_fusion.refs_0_) | copy-start | bytes 196612
  22.3 5.2 %collective-permute-start.6 = (bf16[256,128]{1,0:T(8,128)(2,1)S(1)}, bf16[256,128]{1,0:T(8,128)(2,1)S(1)}, u32[]{:S(2)}, u32[]{:S(2)}) collective-permute-start(bf16[256,128]{1,0:T(8,128)(2,1)S(1)} %pad_maximum_fusion.refs_0_), channel_id=1, source_target_pairs={{0,18},{1,19},{2,16},{3,17},{4,22},{5,23},{6,20},{7,21},{8,26},{9,... | collective-permute-start | bytes 196616 | tf_op jit(solution)/shard_map/ppermute | solution.py:301
  23.9 4.3 %collective-permute-start.5 = (bf16[256,128]{1,0:T(8,128)(2,1)S(1)}, bf16[256,128]{1,0:T(8,128)(2,1)S(1)}, u32[]{:S(2)}, u32[]{:S(2)}) collective-permute-start(bf16[256,128]{1,0:T(8,128)(2,1)S(1)} %pad_maximum_fusion.refs_0_), channel_id=1, source_target_pairs={{0,16},{1,17},{2,18},{3,19},{4,20},{5,21},{6,22},{7,23},{8,24},{9,... | collective-permute-start | bytes 196616 | tf_op jit(solution)/shard_map/ppermute | solution.py:301
  24.4 4.3 %collective-permute-start.4 = (bf16[256,128]{1,0:T(8,128)(2,1)S(1)}, bf16[256,128]{1,0:T(8,128)(2,1)S(1)}, u32[]{:S(2)}, u32[]{:S(2)}) collective-permute-start(bf16[256,128]{1,0:T(8,128)(2,1)S(1)} %pad_maximum_fusion.refs_0_), channel_id=1, source_target_pairs={{0,2},{1,3},{2,0},{3,1},{4,6},{5,7},{6,4},{7,5},{8,10},{9,11},{10,... | collective-permute-start | bytes 196616 | tf_op jit(solution)/shard_map/ppermute | solution.py:301
  25.8 6.6 %collective-permute-start.8 = (bf16[256,128]{1,0:T(8,128)(2,1)S(1)}, bf16[256,128]{1,0:T(8,128)(2,1)S(1)}, u32[]{:S(2)}, u32[]{:S(2)}) collective-permute-start(bf16[256,128]{1,0:T(8,128)(2,1)S(1)} %pad_maximum_fusion.refs_0_), channel_id=1, source_target_pairs={{0,1},{1,0},{2,3},{3,2},{4,5},{5,4},{6,7},{7,6},{8,9},{9,8},{10,11... | collective-permute-start | bytes 196616 | tf_op jit(solution)/shard_map/ppermute | solution.py:301
  27.5 5.0 %copy-start.4 = (bf16[256,128]{1,0:T(8,128)(2,1)}, bf16[256,128]{1,0:T(8,128)(2,1)S(1)}, u32[]{:S(2)}) copy-start(bf16[256,128]{1,0:T(8,128)(2,1)S(1)} %collective-permute-done.6.refs_3_) | copy-start | bytes 196612
  27.5 4.9 %collective-permute-start.11 = (bf16[256,128]{1,0:T(8,128)(2,1)S(1)}, bf16[256,128]{1,0:T(8,128)(2,1)S(1)}, u32[]{:S(2)}, u32[]{:S(2)}) collective-permute-start(bf16[256,128]{1,0:T(8,128)(2,1)S(1)} %collective-permute-done.6.refs_3_), channel_id=1, source_target_pairs={{0,1},{1,0},{2,3},{3,2},{4,5},{5,4},{6,7},{7,6},{8,9},{9,8},{10,11... | collective-permute-start | bytes 196616 | tf_op jit(solution)/shard_map/ppermute | solution.py:301
  28.1 4.3 %copy-start.5 = (bf16[256,128]{1,0:T(8,128)(2,1)}, bf16[256,128]{1,0:T(8,128)(2,1)S(1)}, u32[]{:S(2)}) copy-start(bf16[256,128]{1,0:T(8,128)(2,1)S(1)} %collective-permute-done.5.refs_2_) | copy-start | bytes 196612
  28.1 4.3 %collective-permute-start.10 = (bf16[256,128]{1,0:T(8,128)(2,1)S(1)}, bf16[256,128]{1,0:T(8,128)(2,1)S(1)}, u32[]{:S(2)}, u32[]{:S(2)}) collective-permute-start(bf16[256,128]{1,0:T(8,128)(2,1)S(1)} %collective-permute-done.5.refs_2_), channel_id=1, source_target_pairs={{0,1},{1,0},{2,3},{3,2},{4,5},{5,4},{6,7},{7,6},{8,9},{9,8},{10,11... | collective-permute-start | bytes 196616 | tf_op jit(solution)/shard_map/ppermute | solution.py:301
  28.7 3.8 %copy-start.6 = (bf16[256,128]{1,0:T(8,128)(2,1)}, bf16[256,128]{1,0:T(8,128)(2,1)S(1)}, u32[]{:S(2)}) copy-start(bf16[256,128]{1,0:T(8,128)(2,1)S(1)} %collective-permute-done.4.refs_1_) | copy-start | bytes 196612
  28.7 3.8 %collective-permute-start.9 = (bf16[256,128]{1,0:T(8,128)(2,1)S(1)}, bf16[256,128]{1,0:T(8,128)(2,1)S(1)}, u32[]{:S(2)}, u32[]{:S(2)}) collective-permute-start(bf16[256,128]{1,0:T(8,128)(2,1)S(1)} %collective-permute-done.4.refs_1_), channel_id=1, source_target_pairs={{0,1},{1,0},{2,3},{3,2},{4,5},{5,4},{6,7},{7,6},{8,9},{9,8},{10,11... | collective-permute-start | bytes 196616 | tf_op jit(solution)/shard_map/ppermute | solution.py:301
  30.8 35.4 %collective-permute-start.7 = (bf16[384,1536]{1,0:T(8,128)(2,1)S(1)}, bf16[384,1536]{1,0:T(8,128)(2,1)S(1)}, u32[]{:S(2)}, u32[]{:S(2)}) collective-permute-start(bf16[384,1536]{1,0:T(8,128)(2,1)S(1)} %dynamic_slice.6), channel_id=1, source_target_pairs={{0,16},{1,17},{2,18},{3,19},{4,20},{5,21},{6,22},{7,23},{8,24},{9,... | collective-permute-start | bytes 3538952 | tf_op jit(solution)/shard_map/ppermute | solution.py:301
  32.4 0.6 copy-start.7
  32.4 0.7 copy-start.8
  32.4 0.6 copy-start.9
  32.4 0.6 copy-start.10
  66.2 9.8 %collective-permute-start.15 = (bf16[384,1536]{1,0:T(8,128)(2,1)S(1)}, bf16[384,1536]{1,0:T(8,128)(2,1)S(1)}, u32[]{:S(2)}, u32[]{:S(2)}) collective-permute-start(bf16[384,1536]{1,0:T(8,128)(2,1)S(1)} %collective-permute-done.7.w_across_ref), channel_id=1, source_target_pairs={{0,1},{1,0},{2,3},{3,2},{4,5},{5,4},{6,7},{7,6},{8,9},{9,8},{10,11... | collective-permute-start | bytes 3538952 | tf_op jit(solution)/shard_map/ppermute | solution.py:301
  66.5 9.5 %copy-start = (bf16[192,384]{1,0:T(8,128)(2,1)S(1)}, bf16[192,384]{1,0:T(8,128)(2,1)}, u32[]{:S(2)}) copy-start(bf16[192,384]{1,0:T(8,128)(2,1)} %get-tuple-element.22.own_ref) | copy-start | bytes 442372
  66.5 9.5 %collective-permute-start.14 = (bf16[192,384]{1,0:T(8,128)(2,1)}, bf16[192,384]{1,0:T(8,128)(2,1)S(1)}, u32[]{:S(2)}, u32[]{:S(2)}) collective-permute-start(bf16[192,384]{1,0:T(8,128)(2,1)} %get-tuple-element.23), channel_id=1, source_target_pairs={{0,17},{1,16},{2,19},{3,18},{4,21},{5,20},{6,23},{7,22},{8,25},{9,... | collective-permute-start | bytes 442376 | tf_op jit(solution)/shard_map/ppermute | solution.py:301
  67.0 9.1 %collective-permute-start.12 = (bf16[192,384]{1,0:T(8,128)(2,1)}, bf16[192,384]{1,0:T(8,128)(2,1)S(1)}, u32[]{:S(2)}, u32[]{:S(2)}) collective-permute-start(bf16[192,384]{1,0:T(8,128)(2,1)} %get-tuple-element.23), channel_id=1, source_target_pairs={{0,1},{1,0},{2,3},{3,2},{4,5},{5,4},{6,7},{7,6},{8,9},{9,8},{10,11... | collective-permute-start | bytes 442376 | tf_op jit(solution)/shard_map/ppermute | solution.py:301
  67.2 8.9 %collective-permute-start.13 = (bf16[192,384]{1,0:T(8,128)(2,1)}, bf16[192,384]{1,0:T(8,128)(2,1)S(1)}, u32[]{:S(2)}, u32[]{:S(2)}) collective-permute-start(bf16[192,384]{1,0:T(8,128)(2,1)} %get-tuple-element.22.own_ref), channel_id=1, source_target_pairs={{0,16},{1,17},{2,18},{3,19},{4,20},{5,21},{6,22},{7,23},{8,24},{9,... | collective-permute-start | bytes 442376 | tf_op jit(solution)/shard_map/ppermute | solution.py:301

commit v3 on v2

--- a/solution.py
+++ b/solution.py
@@ -20,6 +20,10 @@
     return jnp.dot(a, b, preferred_element_type=F32)
 
 
+def dot_rows(a, b):
+    return lax.dot_general(a, b, (((1,), (1,)), ((), ())), preferred_element_type=F32)
+
+
 def time_embed(step_index, width):
     half_width = width // 2
     frequency = jnp.exp(-math.log(10000.0) * jnp.arange(half_width, dtype=F32) / half_width)
@@ -35,15 +39,12 @@
     return jnp.sum(jnp.where(diagonal, row.astype(F32), 0.0), axis=1, keepdims=True)
 
 
-def encode_kernel(
-    step_ref, feats_ref, earlier_ref, weight_ref, bias_ref, latent_ref, noise_ref, hist_ref,
-    level_ref, out_ref,
-):
-    frames, channels, pixels = feats_ref.shape
+def encode_kernel(step_ref, earlier_ref, partial_ref, weight_ref, latent_ref, noise_ref, tail_ref, out_ref):
+    frames, pixels, channels = partial_ref.shape
     lat = noise_ref.shape[1]
     patch = lat * 4
     cells = pixels // 4
-    bias = column_of(bias_ref[...])
+    taps = weight_ref.shape[0] + 1
     step = jnp.full((lat, pixels), step_ref[0].astype(F32), F32)
     sigma = (STEPS - step) / STEPS
     row = lax.broadcasted_iota(jnp.int32, (lat, frames * patch), 0)
@@ -57,25 +58,18 @@
     ).astype(BF16)
     patches = jnp.zeros((cells, frames * patch), F32)
     for t in range(frames):
-        total = jnp.zeros((channels, pixels), F32)
-        for tap in range(3):
-            source = t - tap
-            window = feats_ref[source] if source >= 0 else earlier_ref[frames + source]
-            total = total + dot(weight_ref[tap], window)
-        total = total + bias
+        total = partial_ref[t]
+        for tap in range(t + 1, taps):
+            total = total + dot_rows(earlier_ref[frames + t - tap], weight_ref[tap - 1])
         hidden = (total / (1.0 + jnp.exp(-total))).astype(BF16)
-        mixed = dot(latent_ref[...], hidden)
+        mixed = dot_rows(latent_ref[...], hidden)
         noisy = ((1.0 - sigma) * mixed + sigma * noise_ref[t].astype(F32)).astype(BF16)
         spread = (lane // 4 == row + t * lat).astype(BF16)
         wide = lax.dot_general(noisy, spread, (((0,), (0,)), ((), ())), preferred_element_type=F32)
         wide = jnp.where(keep, wide, 0.0).astype(BF16)
         patches = patches + dot(collect, wide)
     out_ref[0:cells, :] = patches.astype(BF16)
-    slots = hist_ref.shape[0]
-    level = jnp.broadcast_to(column_of(level_ref[...]), (slots, patch))
-    tail = jnp.concatenate([hist_ref[...].astype(F32), level], axis=1)
-    tail = jnp.concatenate([tail, jnp.zeros((out_ref.shape[0] - cells - slots, 2 * patch), F32)], axis=0)
-    out_ref[cells:, :] = tail.astype(BF16)
+    out_ref[cells:, :] = tail_ref[...]
 
 
 def exact_parts(values):
@@ -85,16 +79,54 @@
     return high, middle, (rest - middle.astype(F32)).astype(BF16)
 
 
+def prepare_kernel(
+    w_in_ref, cos_ref, sin_ref, feats_ref, weight_ref, bias_ref, latent_ref, noise_ref, hist_ref, level_ref,
+    wide_ref, gram_ref, partial_ref, taps_ref, latent_out_ref, noise_out_ref, tail_ref,
+):
+    frames, pixels, channels = feats_ref.shape
+    for t in range(frames):
+        total = jnp.broadcast_to(bias_ref[...], (pixels, channels))
+        for tap in range(t + 1):
+            total = total + dot_rows(feats_ref[t - tap], weight_ref[tap])
+        partial_ref[t] = total
+    taps_ref[...] = weight_ref[1:]
+    latent_out_ref[...] = latent_ref[...]
+    noise_out_ref[...] = noise_ref[...]
+    patch, width = w_in_ref.shape
+    slots = hist_ref.shape[0]
+    level = jnp.broadcast_to(column_of(level_ref[...]), (slots, patch))
+    tail = jnp.concatenate([hist_ref[...].astype(F32), level], axis=1)
+    rest = jnp.zeros((tail_ref.shape[0] - slots, 2 * patch), F32)
+    tail_ref[...] = jnp.concatenate([tail, rest], axis=0).astype(BF16)
+    lanes = wide_ref.shape[0]
+    for n, source in ((0, cos_ref), (width // 2, sin_ref)):
+        values = source[...]
+        row = lax.broadcasted_iota(jnp.int32, (lanes - patch, values.shape[1]), 0)
+        high, middle, low = exact_parts(values)
+        extra = jnp.where(row == 0, high.astype(F32), 0.0)
+        extra = jnp.where(row == 1, middle.astype(F32), extra)
+        extra = jnp.where(row == 2, low.astype(F32), extra)
+        wide_ref[patch:lanes, n : n + values.shape[1]] = extra.astype(BF16)
+    wide_ref[0:patch, :] = w_in_ref[...]
+    gram = jnp.zeros((lanes, lanes), F32)
+    step = 512
+    for n in range(0, width, step):
+        part = wide_ref[:, n : n + step]
+        gram = gram + dot_rows(part, part)
+    for number, part in enumerate(exact_parts(gram)):
+        gram_ref[number * lanes : (number + 1) * lanes, :] = part
+
+
 def joint_kernel(*refs, cells, block, pieces, owner_masks, tile, query_rows):
     near, far = refs[:pieces], refs[pieces : 2 * pieces]
     (
-        count_ref, w_in_ref, w_hist_ref, cos_ref, sin_ref, gain_ref, w_query_ref, w_key_ref, w_value_ref,
+        count_ref, wide_ref, gram_ref, w_hist_ref, gain_ref, w_query_ref, w_key_ref, w_value_ref,
         q_gain_ref, k_gain_ref, hist_ref, own_ref, sib_ref,
-        patch_ref, wide_ref, w_q_ref, w_kv_ref, tok_a_ref, tok_b_ref, q_ref, k_ref, v_ref, s_a_ref,
+        patch_ref, w_q_ref, w_kv_ref, tok_a_ref, tok_b_ref, q_ref, k_ref, v_ref, s_a_ref,
         s_b_ref, x_ref, out_ref, semaphores,
     ) = refs[2 * pieces :]
     heads, keys, size = k_ref.shape
-    patch, width = w_in_ref.shape
+    levels, patch, width = w_hist_ref.shape
     depth = heads * size
     lanes = near[0].shape[1]
     frames = lanes // patch
@@ -116,21 +148,6 @@
 
     step = 512
     lane = lax.broadcasted_iota(jnp.int32, (1, lanes), 1)
-    for n, source in ((0, cos_ref), (width // 2, sin_ref)):
-        values = source[...]
-        row = lax.broadcasted_iota(jnp.int32, (lanes - patch, values.shape[1]), 0)
-        high, middle, low = exact_parts(values)
-        extra = jnp.where(row == 0, high.astype(F32), 0.0)
-        extra = jnp.where(row == 1, middle.astype(F32), extra)
-        extra = jnp.where(row == 2, low.astype(F32), extra)
-        wide_ref[patch:lanes, n : n + values.shape[1]] = extra.astype(BF16)
-    wide_ref[0:patch, :] = w_in_ref[...]
-    gram = jnp.zeros((lanes, lanes), F32)
-    for n in range(0, width, step):
-        part = wide_ref[:, n : n + step]
-        gram = gram + lax.dot_general(part, part, (((1,), (1,)), ((), ())), preferred_element_type=F32)
-    gram_parts = jnp.concatenate(exact_parts(gram), axis=0)
-
     ones = jnp.where(lane < patch + 3, 1.0, 0.0)
     held = near[0].shape[0] // block
     half = pieces * held
@@ -153,7 +170,7 @@
 
     def tokens_of(i, tok_ref):
         source = patch_ref[pl.ds(pl.multiple_of(i * tile, tile), tile), :]
-        mixed = dot(jnp.concatenate([source] * 3, axis=1), gram_parts)
+        mixed = dot(jnp.concatenate([source] * 3, axis=1), gram_ref[...])
         mean = jnp.sum(mixed * source.astype(F32), axis=1, keepdims=True) / width
         inverse = lax.rsqrt(mean + EPSILON)
         for n in range(0, width, step):
@@ -172,12 +189,11 @@
             v_ref[h, pl.ds(at, count), :] = both[:, (heads + h) * size : (heads + h + 1) * size].astype(BF16)
 
     tokens_of(0, tok_a_ref)
-    copies[0].wait()
+    for copy in copies:
+        copy.wait()
     q = dot(tok_a_ref[0:rows, :], w_q_ref[...])
     for h in range(heads):
         q_ref[h] = head_norm(q[:, h * size : (h + 1) * size], q_gain_ref[...])
-    copies[1].wait()
-    copies[2].wait()
     tiles = patch_ref.shape[0] // tile
 
     def pair(j, carry):
@@ -195,7 +211,6 @@
 
     section = tiles * tile
     slots = hist_ref.shape[0]
-    levels = w_hist_ref.shape[0]
     owners = len(owner_masks)
     spread = 128 // slots
     owner_blocks = [
@@ -296,6 +311,10 @@
         out_ref[:, columns] = total.astype(BF16)
 
 
+def in_hbm(*values):
+    return [pltpu.with_memory_space_constraint(value, pltpu.HBM) for value in values]
+
+
 def flip(value, mask, seq_count):
     pairs = [(i, i ^ mask) for i in range(2 * seq_count)]
     return lax.ppermute(value, ("grp", "seq"), pairs)
@@ -320,17 +339,41 @@
     heads = w_query.shape[1] // size // 2
     depth = heads * size
 
-    earlier = lax.ppermute(feats, "seq", [(i, i + 1) for i in range(seq_count - 1)])
+    swapped = feats.transpose(0, 2, 1)
+    earlier = lax.ppermute(swapped, "seq", [(i, i + 1) for i in range(seq_count - 1)])
+    cos, sin = time_embed(step_index, width)
+    wide, gram, partial, taps, latent, held_noise, tail = pl.pallas_call(
+        prepare_kernel,
+        out_shape=[
+            jax.ShapeDtypeStruct((lanes, width), BF16),
+            jax.ShapeDtypeStruct((3 * lanes, lanes), BF16),
+            jax.ShapeDtypeStruct(swapped.shape, F32),
+            jax.ShapeDtypeStruct((conv_weight.shape[0] - 1,) + conv_weight.shape[1:], BF16),
+            jax.ShapeDtypeStruct(latent_projection_weight.shape, BF16),
+            jax.ShapeDtypeStruct(noise.shape, BF16),
+            jax.ShapeDtypeStruct((block - cells, lanes), BF16),
+        ],
+        in_specs=[VMEM] * 10,
+        out_specs=[VMEM] * 7,
+        compiler_params=pltpu.CompilerParams(vmem_limit_bytes=10 * 2**20),
+        name="prepare",
+    )(
+        *in_hbm(
+            w_in, cos, sin, swapped, conv_weight, conv_bias.reshape(1, channels),
+            latent_projection_weight, noise, hist, hist_level.reshape(1, slots),
+        )
+    )
+    earlier, partial = lax.optimization_barrier((earlier, partial))
     gathered = pl.pallas_call(
         encode_kernel,
         out_shape=jax.ShapeDtypeStruct((block, lanes), BF16),
-        in_specs=[SMEM] + [VMEM] * 8,
+        in_specs=[SMEM] + [VMEM] * 6,
         out_specs=VMEM,
+        compiler_params=pltpu.CompilerParams(vmem_limit_bytes=6 * 2**20),
         name="encode",
-    )(
-        step_index, feats, earlier, conv_weight, conv_bias.reshape(1, channels),
-        latent_projection_weight, noise, hist, hist_level.reshape(1, slots),
-    )
+    )(step_index, earlier, partial, taps, latent, held_noise, tail)
+    columns = w_out.shape[1] // 2
+    w_send = lax.dynamic_slice(w_out, (core * depth, (1 - group) * columns), (depth, columns))
 
     bits = []
     bit = seq_count // 2
@@ -350,10 +393,9 @@
         near = [gathered] + [flip(gathered, mask, seq_count) for mask in masks[1:]]
         if number + 1 < len(rounds):
             gathered = jnp.concatenate(near, axis=0)
+            gathered, w_send = lax.optimization_barrier((gathered, w_send))
     far = [flip(piece, 1, seq_count) for piece in near]
 
-    columns = w_out.shape[1] // 2
-    w_send = lax.dynamic_slice(w_out, (core * depth, (1 - group) * columns), (depth, columns))
     w_send, *near = lax.optimization_barrier((w_send, *near))
     w_across = flip(w_send, seq_count, seq_count)
     w_local = lax.dynamic_slice_in_dim(w_out, group * columns, columns, axis=1)
@@ -365,19 +407,21 @@
     query_rows = rows
     while 2 * query_rows * keys * 4 > 12 * 2**20:
         query_rows //= 2
-    cos, sin = time_embed(step_index, width)
-    anywhere = pl.BlockSpec(memory_space=pl.ANY)
+    limit = (
+        2 * tokens * lanes + 6 * width * depth + 4 * tile * width + 4 * keys * depth
+        + 8 * query_rows * keys + 512 * width + 4 * rows * depth + 12 * 2**20
+    )
+    anywhere = pl.BlockSpec(memory_space=pltpu.HBM)
     own, sib = pl.pallas_call(
         functools.partial(
             joint_kernel, cells=cells, block=block, pieces=len(near), owner_masks=owner_masks, tile=tile,
             query_rows=query_rows,
         ),
         out_shape=[jax.ShapeDtypeStruct((rows // 2, depth), BF16)] * 2,
-        in_specs=[VMEM] * (2 * len(near)) + [SMEM] + [VMEM] * 5 + [anywhere] * 3 + [VMEM] * 3,
+        in_specs=[VMEM] * (2 * len(near)) + [SMEM] + [VMEM] * 4 + [anywhere] * 3 + [VMEM] * 3,
         out_specs=[VMEM] * 2,
         scratch_shapes=[
             pltpu.VMEM((tokens, lanes), BF16),
-            pltpu.VMEM((lanes, width), BF16),
             pltpu.VMEM((width, depth), BF16),
             pltpu.VMEM((width, 2 * depth), BF16),
             pltpu.VMEM((tile, width), BF16),
@@ -391,7 +435,7 @@
             pltpu.VMEM((rows, depth), BF16),
             pltpu.SemaphoreType.DMA((3,)),
         ],
-        compiler_params=pltpu.CompilerParams(vmem_limit_bytes=60 * 2**20),
+        compiler_params=pltpu.CompilerParams(vmem_limit_bytes=limit),
         cost_estimate=pl.CostEstimate(
             flops=2 * keys * width * 3 * depth + 4 * rows * keys * depth,
             bytes_accessed=6 * width * depth,
@@ -399,8 +443,8 @@
         ),
         name="joint",
     )(
-        *near, *far, hist_count, w_in, w_hist, cos, sin, norm_gain.reshape(1, width), w_query, w_key,
-        w_value, q_gain.reshape(1, size), k_gain.reshape(1, size), hist,
+        *near, *far, hist_count, wide, gram, w_hist, norm_gain.reshape(1, width),
+        *in_hbm(w_query, w_key, w_value), q_gain.reshape(1, size), k_gain.reshape(1, size), hist,
     )
     w_across, own, sib = lax.optimization_barrier((w_across, own, sib))
     w_corner = flip(w_across, 1, seq_count)
@@ -412,7 +456,7 @@
         out_shape=jax.ShapeDtypeStruct((rows // 2, columns), BF16),
         in_specs=[VMEM] * 7,
         out_specs=VMEM,
-        compiler_params=pltpu.CompilerParams(vmem_limit_bytes=24 * 2**20),
+        compiler_params=pltpu.CompilerParams(vmem_limit_bytes=10 * 2**20),
         name="combine",
     )(own, from_sib, across, corner, w_local, w_across, w_corner)
 

time: 78.6 us -> 70.2 us (0.89)
  waiting for transfers between devices: 13 us -> 10.8 us
  local copies, waits for them, and re-layouts: 5.44 us -> 3.28 us
  starting transfers between devices: 19.3 us -> 17.2 us
  Pallas kernels: 38.1 us -> 37 us
    unnamed x23 -> x12, local copies, waits for them, and re-layouts: 2.28 us -> 0.02 us
    ppermute x15, starting transfers between devices: 16.9 us -> 14.7 us  [flip(): return lax.ppermute(value, ('grp', 'seq'), pairs)]
    ppermute x15, waiting for transfers between devices: 12.7 us -> 10.8 us  [flip(): return lax.ppermute(value, ('grp', 'seq'), pairs)]
    pallas_call x1, Pallas kernels: 2.79 us -> 1.1 us  [local(): pl.pallas_call(encode_kernel, out_shape=jax.ShapeDtypeStruct((block, lane...]
    pallas_call x0 -> x1, Pallas kernels: none -> 1.62 us  [local(): pl.pallas_call(prepare_kernel, out_shape=[jax.ShapeDtypeStruct((lanes, wi...]
    pallas_call x1, Pallas kernels: 33.1 us -> 32.1 us  [local(): pl.pallas_call(functools.partial(joint_kernel, cells=cells, block=block,...]
  transfers between devices with their start and end apart: 16 -> 16, of which waited for: 8 -> 6; matrix products, arithmetic and copies ran while one was open for 5% -> 6% of each run, Pallas kernels for 42% -> 48%
where the time goes in v3:
time: 70.2 us; the launch traced here: 69.9 us
  Pallas kernels  37 us (53%)
  starting transfers between devices  17.2 us (25%)
  waiting for transfers between devices  10.8 us (15%)
  local copies, waits for them, and re-layouts  3.28 us (5%)
  other arithmetic  0.82 us (1%)
  between operations  0.78 us (1%)
    pallas_call x1, Pallas kernels, local(): pl.pallas_call(functools.partial(joint_kernel, cells=cells, block=block,...  32.1 us
    ppermute x15, starting transfers between devices, flip(): return lax.ppermute(value, ('grp', 'seq'), pairs)  14.7 us
    ppermute x15, waiting for transfers between devices, flip(): return lax.ppermute(value, ('grp', 'seq'), pairs)  10.8 us
    ppermute x1, starting transfers between devices, local(): lax.ppermute(swapped, 'seq', [(i, i + 1) for i in range(seq_count - 1)])  2.55 us
    pallas_call x1, Pallas kernels, local(): pl.pallas_call(combine_kernel, out_shape=jax.ShapeDtypeStruct((rows // 2,...  2.22 us
    dynamic_slice x1, local copies, waits for them, and re-layouts, local(): w_local = lax.dynamic_slice_in_dim(w_out, group * columns, columns, axis=1)  1.82 us
    pallas_call x1, Pallas kernels, local(): pl.pallas_call(prepare_kernel, out_shape=[jax.ShapeDtypeStruct((lanes, wi...  1.62 us
    dynamic_slice x1, local copies, waits for them, and re-layouts, local(): lax.dynamic_slice(w_out, (core * depth, (1 - group) * columns), (depth, c...  1.44 us
  transfers between devices with their start and end apart: 16, of which 6 were waited for; matrix products, arithmetic and copies ran while one was open for 6% of the time, Pallas kernels for 48%

profile of v3, /device:TPU:0, one launch (start us, length us, event | category | flops | bytes accessed | tf_op | source)
XLA Modules:
  0.0 69.9 jit_solution(6026924197004220485)
XLA Ops:
  0.0 0.0 copy-start
  0.0 0.0 copy-start.5
  0.0 0.0 copy-start.4
  0.0 2.6 %collective-permute-start = (bf16[2,192,128]{2,1,0:T(8,128)(2,1)}, bf16[2,192,128]{2,1,0:T(8,128)(2,1)S(1)}, u32[]{:S(2)}, u32[]{:S(2)}) collective-permute-start(bf16[2,192,128]{2,1,0:T(8,128)(2,1)} %bitcast.10), channel_id=1, source_target_pairs={{0,1},{1,2},{2,3},{3,4},{4,5},{5,6},{6,7},{7,8},{8,9},{9,10},{10,1... | collective-permute-start | bytes 294920 | tf_op jit(solution)/shard_map/ppermute | solution.py:343
  3.2 0.8 %fusion = (f32[1,1536]{1,0:T(1,128)}, f32[1,1536]{1,0:T(1,128)}) fusion(f32[]{:T(128)} %bitcast.1), kind=kLoop, calls=%fused_computation.2 | loop fusion | flops 3072 | bytes 12292 | tf_op jit(solution)/shard_map/sin | solution.py:31
  4.0 1.6 %prepare.1 = (bf16[128,3072]{1,0:T(8,128)(2,1)S(1)}, bf16[384,128]{1,0:T(8,128)(2,1)S(1)}, f32[2,192,128]{2,1,0:T(8,128)S(1)}, bf16[2,128,128]{2,1,0:T(8,128)(2,...) custom-call(bf16[64,3072]{1,0:T(8,128)(2,1)} %w_in_ref.1, ...), custom_call_target="tpu_custom_call" | custom-call | tf_op jit(solution)/shard_map/prepare/pallas_call | solution.py:345
  5.7 0.0 collective-permute-done.earlier_ref
  5.7 1.1 %encode.1 = bf16[64,128]{1,0:T(8,128)(2,1)S(1)} custom-call(s32[1]{0:T(128)S(6)} %copy.19.step_ref, bf16[2,192,128]{2,1,0:T(8,128)(2,1)S(1)} %collective-permute-done.earlier_ref, f32[2,192,128]{2,1,0:T(8,128)S(1)} %get-tuple-element.28.partial_ref, bf16[2,128,128]{2,1,0:T(8,128)(2,1)S(1)} %get-tuple-element.29.weight_ref, ...), custom_call_target="tpu_custom_call" | custom-call | tf_op jit(solution)/shard_map/encode/pallas_call | solution.py:367
  6.8 6.6 %collective-permute-start.3 = (bf16[64,128]{1,0:T(8,128)(2,1)S(1)}, bf16[64,128]{1,0:T(8,128)(2,1)S(1)}, u32[]{:S(2)}, u32[]{:S(2)}) collective-permute-start(bf16[64,128]{1,0:T(8,128)(2,1)S(1)} %encode.1), channel_id=1, source_target_pairs={{0,12},{1,13},{2,14},{3,15},{4,8},{5,9},{6,10},{7,11},{8,4},{9,5},... | collective-permute-start | bytes 49160 | tf_op jit(solution)/shard_map/ppermute | solution.py:320
  13.4 0.0 collective-permute-start.2
  13.4 0.6 collective-permute-start.1
  14.0 1.4 %dynamic_slice.6 = bf16[384,1536]{1,0:T(8,128)(2,1)S(1)} dynamic-slice(bf16[768,3072]{1,0:T(8,128)(2,1)} %param.35, s32[]{:T(128)S(6)} %select_n.17, s32[]{:T(128)S(6)} %select_n.18), dynamic_slice_sizes={384,1536} | dynamic-slice | bytes 2359300 | tf_op jit(solution)/shard_map/dynamic_slice | solution.py:376
  15.5 0.0 collective-permute-done.3
  15.5 1.6 %collective-permute-done.2 = bf16[64,128]{1,0:T(8,128)(2,1)S(1)} collective-permute-done((bf16[64,128]{1,0:T(8,128)(2,1)S(1)}, bf16[64,128]{1,0:T(8,128)(2,1)S(1)}, u32[]{:S(2)}, u32[]{:S(2)}) %collective-permute-start.2) | collective-permute-done | bytes 16416 | tf_op jit(solution)/shard_map/ppermute | solution.py:320
  17.1 0.9 %collective-permute-done.1 = bf16[64,128]{1,0:T(8,128)(2,1)S(1)} collective-permute-done((bf16[64,128]{1,0:T(8,128)(2,1)S(1)}, bf16[64,128]{1,0:T(8,128)(2,1)S(1)}, u32[]{:S(2)}, u32[]{:S(2)}) %collective-permute-start.1) | collective-permute-done | bytes 16416 | tf_op jit(solution)/shard_map/ppermute | solution.py:320
  18.1 1.5 %collective-permute-start.6 = (bf16[256,128]{1,0:T(8,128)(2,1)S(1)}, bf16[256,128]{1,0:T(8,128)(2,1)S(1)}, u32[]{:S(2)}, u32[]{:S(2)}) collective-permute-start(bf16[256,128]{1,0:T(8,128)(2,1)S(1)} %pad_maximum_fusion.refs_0_), channel_id=1, source_target_pairs={{0,18},{1,19},{2,16},{3,17},{4,22},{5,23},{6,20},{7,21},{8,26},{9,... | collective-permute-start | bytes 196616 | tf_op jit(solution)/shard_map/ppermute | solution.py:320
  19.6 0.5 collective-permute-start.5
  20.1 1.4 %collective-permute-start.4 = (bf16[256,128]{1,0:T(8,128)(2,1)S(1)}, bf16[256,128]{1,0:T(8,128)(2,1)S(1)}, u32[]{:S(2)}, u32[]{:S(2)}) collective-permute-start(bf16[256,128]{1,0:T(8,128)(2,1)S(1)} %pad_maximum_fusion.refs_0_), channel_id=1, source_target_pairs={{0,2},{1,3},{2,0},{3,1},{4,6},{5,7},{6,4},{7,5},{8,10},{9,11},{10,... | collective-permute-start | bytes 196616 | tf_op jit(solution)/shard_map/ppermute | solution.py:320
  21.5 0.0 collective-permute-start.8
  21.5 1.7 %collective-permute-done.6.refs_3_ = bf16[256,128]{1,0:T(8,128)(2,1)S(1)} collective-permute-done((bf16[256,128]{1,0:T(8,128)(2,1)S(1)}, bf16[256,128]{1,0:T(8,128)(2,1)S(1)}, u32[]{:S(2)}, u32[]{:S(2)}) %collective-permute-start.6) | collective-permute-done | bytes 65568 | tf_op jit(solution)/shard_map/ppermute | solution.py:320
  23.2 0.0 collective-permute-start.11
  23.2 0.6 collective-permute-done.5.refs_2_
  23.9 0.0 collective-permute-start.10
  23.9 0.5 collective-permute-done.4.refs_1_
  24.4 0.0 collective-permute-start.9
  24.4 1.5 %collective-permute-start.7 = (bf16[384,1536]{1,0:T(8,128)(2,1)S(1)}, bf16[384,1536]{1,0:T(8,128)(2,1)S(1)}, u32[]{:S(2)}, u32[]{:S(2)}) collective-permute-start(bf16[384,1536]{1,0:T(8,128)(2,1)S(1)} %dynamic_slice.6), channel_id=1, source_target_pairs={{0,16},{1,17},{2,18},{3,19},{4,20},{5,21},{6,22},{7,23},{8,24},{9,... | collective-permute-start | bytes 3538952 | tf_op jit(solution)/shard_map/ppermute | solution.py:320
  25.9 0.0 collective-permute-done.8.refs_4_
  25.9 0.0 collective-permute-done.11.refs_7_
  25.9 0.0 collective-permute-done.10.refs_6_
  25.9 0.0 collective-permute-done.9.refs_5_
  25.9 0.0 copy-done
  25.9 0.0 copy-done.5
  25.9 0.0 copy-done.4
  25.9 0.0 copy-done.2
  26.0 0.0 copy-done.3
  26.0 0.0 copy-done.1
  26.0 32.1 %joint.1 = (bf16[192,384]{1,0:T(8,128)(2,1)S(1)}, bf16[192,384]{1,0:T(8,128)(2,1)S(1)}) custom-call(bf16[256,128]{1,0:T(8,128)(2,1)S(1)} %pad_maximum_fusion.refs_0_, bf16[256,128]{1,0:T(8,128)(2,1)S(1)} %collective-permute-done.4.refs_1_, bf16[256,128]{1,0:T(8,128)(2,1)S(1)} %collective-permute-done.5.refs_2_, ...), custom_call_target="tpu_custom_call" | custom-call | flops 24536678400 | bytes 7077888 | tf_op jit(solution)/shard_map/joint/pallas_call | solution.py:415
  58.0 0.0 collective-permute-done.7.w_across_ref
  58.1 0.3 collective-permute-start.15
  58.3 1.1 %collective-permute-start.14 = (bf16[192,384]{1,0:T(8,128)(2,1)S(1)}, bf16[192,384]{1,0:T(8,128)(2,1)S(1)}, u32[]{:S(2)}, u32[]{:S(2)}) collective-permute-start(bf16[192,384]{1,0:T(8,128)(2,1)S(1)} %get-tuple-element.45), channel_id=1, source_target_pairs={{0,17},{1,16},{2,19},{3,18},{4,21},{5,20},{6,23},{7,22},{8,25},{9,... | collective-permute-start | bytes 442376 | tf_op jit(solution)/shard_map/ppermute | solution.py:320
  59.4 0.2 collective-permute-start.12
  59.6 0.9 %collective-permute-start.13 = (bf16[192,384]{1,0:T(8,128)(2,1)S(1)}, bf16[192,384]{1,0:T(8,128)(2,1)S(1)}, u32[]{:S(2)}, u32[]{:S(2)}) collective-permute-start(bf16[192,384]{1,0:T(8,128)(2,1)S(1)} %get-tuple-element.44.own_ref), channel_id=1, source_target_pairs={{0,16},{1,17},{2,18},{3,19},{4,20},{5,21},{6,22},{7,23},{8,24},{9,... | collective-permute-start | bytes 442376 | tf_op jit(solution)/shard_map/ppermute | solution.py:320
  60.5 1.8 %constant_dynamic-slice_fusion.w_local_ref = bf16[768,1536]{1,0:T(8,128)(2,1)S(1)} fusion(bf16[768,3072]{1,0:T(8,128)(2,1)} %param.35, s32[]{:T(128)S(6)} %select_n.19), kind=kLoop, calls=%fused_computation.4 | loop fusion | bytes 4718596 | tf_op jit(solution)/shard_map/dynamic_slice | solution.py:401
  62.3 5.3 %collective-permute-done.13.across_ref = bf16[192,384]{1,0:T(8,128)(2,1)S(1)} collective-permute-done((bf16[192,384]{1,0:T(8,128)(2,1)S(1)}, bf16[192,384]{1,0:T(8,128)(2,1)S(1)}, u32[]{:S(2)}, u32[]{:S(2)}) %collective-permute-start.13) | collective-permute-done | bytes 147488 | tf_op jit(solution)/shard_map/ppermute | solution.py:320
  67.7 0.0 collective-permute-done.14.corner_ref
  67.7 0.0 collective-permute-done.12.sib_ref
  67.7 0.0 collective-permute-done.15.w_corner_ref
  67.7 2.2 %combine.1 = bf16[192,1536]{1,0:T(8,128)(2,1)} custom-call(bf16[192,384]{1,0:T(8,128)(2,1)S(1)} %get-tuple-element.44.own_ref, bf16[192,384]{1,0:T(8,128)(2,1)S(1)} %collective-permute-done.12.sib_ref, bf16[192,384]{1,0:T(8,128)(2,1)S(1)} %collective-permute-done.13.across_ref, bf16[192,384]{1,0:T(8,128)(2,1)S(1)} %collective-permute-done.14.corner_ref, ...), custom_call_target="tpu_custom_call" | custom-call | tf_op jit(solution)/shard_map/combine/pallas_call | solution.py:454
  (4 shorter events, 0.0 us)
Async XLA Ops:
  0.0 25.9 %copy-start = (bf16[8,64]{1,0:T(8,128)(2,1)S(1)}, bf16[8,64]{1,0:T(8,128)(2,1)}, u32[]{:S(2)}) copy-start(bf16[8,64]{1,0:T(8,128)(2,1)} %refs_18_.1) | copy-start | bytes 3076
  0.0 25.9 %copy-start.5 = (f32[128]{0:T(128)S(1)}, f32[128]{0:T(128)}, u32[]{:S(2)}) copy-start(f32[128]{0:T(128)} %param.34) | copy-start | bytes 1540
  0.0 25.9 %copy-start.4 = (f32[128]{0:T(128)S(1)}, f32[128]{0:T(128)}, u32[]{:S(2)}) copy-start(f32[128]{0:T(128)} %param.33) | copy-start | bytes 1540
  0.0 25.9 %copy-start.2 = (f32[3072]{0:T(1024)S(1)}, f32[3072]{0:T(1024)}, u32[]{:S(2)}) copy-start(f32[3072]{0:T(1024)} %param.29) | copy-start | bytes 36868
  0.0 26.0 %copy-start.3 = (s32[16]{0:T(128)S(1)}, s32[16]{0:T(128)}, u32[]{:S(2)}) copy-start(s32[16]{0:T(128)} %refs_8_.1) | copy-start | bytes 196
  0.0 5.6 %collective-permute-start = (bf16[2,192,128]{2,1,0:T(8,128)(2,1)}, bf16[2,192,128]{2,1,0:T(8,128)(2,1)S(1)}, u32[]{:S(2)}, u32[]{:S(2)}) collective-permute-start(bf16[2,192,128]{2,1,0:T(8,128)(2,1)} %bitcast.10), channel_id=1, source_target_pairs={{0,1},{1,2},{2,3},{3,4},{4,5},{5,6},{6,7},{7,8},{8,9},{9,10},{10,1... | collective-permute-start | bytes 294920 | tf_op jit(solution)/shard_map/ppermute | solution.py:343
  6.8 8.7 %collective-permute-start.3 = (bf16[64,128]{1,0:T(8,128)(2,1)S(1)}, bf16[64,128]{1,0:T(8,128)(2,1)S(1)}, u32[]{:S(2)}, u32[]{:S(2)}) collective-permute-start(bf16[64,128]{1,0:T(8,128)(2,1)S(1)} %encode.1), channel_id=1, source_target_pairs={{0,12},{1,13},{2,14},{3,15},{4,8},{5,9},{6,10},{7,11},{8,4},{9,5},... | collective-permute-start | bytes 49160 | tf_op jit(solution)/shard_map/ppermute | solution.py:320
  13.4 3.7 %collective-permute-start.2 = (bf16[64,128]{1,0:T(8,128)(2,1)S(1)}, bf16[64,128]{1,0:T(8,128)(2,1)S(1)}, u32[]{:S(2)}, u32[]{:S(2)}) collective-permute-start(bf16[64,128]{1,0:T(8,128)(2,1)S(1)} %encode.1), channel_id=1, source_target_pairs={{0,4},{1,5},{2,6},{3,7},{4,0},{5,1},{6,2},{7,3},{8,12},{9,13},{10,... | collective-permute-start | bytes 49160 | tf_op jit(solution)/shard_map/ppermute | solution.py:320
  13.4 4.6 %collective-permute-start.1 = (bf16[64,128]{1,0:T(8,128)(2,1)S(1)}, bf16[64,128]{1,0:T(8,128)(2,1)S(1)}, u32[]{:S(2)}, u32[]{:S(2)}) collective-permute-start(bf16[64,128]{1,0:T(8,128)(2,1)S(1)} %encode.1), channel_id=1, source_target_pairs={{0,8},{1,9},{2,10},{3,11},{4,12},{5,13},{6,14},{7,15},{8,0},{9,1},... | collective-permute-start | bytes 49160 | tf_op jit(solution)/shard_map/ppermute | solution.py:320
  14.0 11.9 %copy-start.1 = (bf16[3,64,3072]{2,1,0:T(8,128)(2,1)S(1)}, bf16[3,64,3072]{2,1,0:T(8,128)(2,1)}, u32[]{:S(2)}) copy-start(bf16[3,64,3072]{2,1,0:T(8,128)(2,1)} %refs_11_.1) | copy-start | bytes 3538948
  18.1 5.2 %collective-permute-start.6 = (bf16[256,128]{1,0:T(8,128)(2,1)S(1)}, bf16[256,128]{1,0:T(8,128)(2,1)S(1)}, u32[]{:S(2)}, u32[]{:S(2)}) collective-permute-start(bf16[256,128]{1,0:T(8,128)(2,1)S(1)} %pad_maximum_fusion.refs_0_), channel_id=1, source_target_pairs={{0,18},{1,19},{2,16},{3,17},{4,22},{5,23},{6,20},{7,21},{8,26},{9,... | collective-permute-start | bytes 196616 | tf_op jit(solution)/shard_map/ppermute | solution.py:320
  19.6 4.3 %collective-permute-start.5 = (bf16[256,128]{1,0:T(8,128)(2,1)S(1)}, bf16[256,128]{1,0:T(8,128)(2,1)S(1)}, u32[]{:S(2)}, u32[]{:S(2)}) collective-permute-start(bf16[256,128]{1,0:T(8,128)(2,1)S(1)} %pad_maximum_fusion.refs_0_), channel_id=1, source_target_pairs={{0,16},{1,17},{2,18},{3,19},{4,20},{5,21},{6,22},{7,23},{8,24},{9,... | collective-permute-start | bytes 196616 | tf_op jit(solution)/shard_map/ppermute | solution.py:320
  20.1 4.3 %collective-permute-start.4 = (bf16[256,128]{1,0:T(8,128)(2,1)S(1)}, bf16[256,128]{1,0:T(8,128)(2,1)S(1)}, u32[]{:S(2)}, u32[]{:S(2)}) collective-permute-start(bf16[256,128]{1,0:T(8,128)(2,1)S(1)} %pad_maximum_fusion.refs_0_), channel_id=1, source_target_pairs={{0,2},{1,3},{2,0},{3,1},{4,6},{5,7},{6,4},{7,5},{8,10},{9,11},{10,... | collective-permute-start | bytes 196616 | tf_op jit(solution)/shard_map/ppermute | solution.py:320
  21.5 4.4 %collective-permute-start.8 = (bf16[256,128]{1,0:T(8,128)(2,1)S(1)}, bf16[256,128]{1,0:T(8,128)(2,1)S(1)}, u32[]{:S(2)}, u32[]{:S(2)}) collective-permute-start(bf16[256,128]{1,0:T(8,128)(2,1)S(1)} %pad_maximum_fusion.refs_0_), channel_id=1, source_target_pairs={{0,1},{1,0},{2,3},{3,2},{4,5},{5,4},{6,7},{7,6},{8,9},{9,8},{10,11... | collective-permute-start | bytes 196616 | tf_op jit(solution)/shard_map/ppermute | solution.py:320
  23.2 2.7 %collective-permute-start.11 = (bf16[256,128]{1,0:T(8,128)(2,1)S(1)}, bf16[256,128]{1,0:T(8,128)(2,1)S(1)}, u32[]{:S(2)}, u32[]{:S(2)}) collective-permute-start(bf16[256,128]{1,0:T(8,128)(2,1)S(1)} %collective-permute-done.6.refs_3_), channel_id=1, source_target_pairs={{0,1},{1,0},{2,3},{3,2},{4,5},{5,4},{6,7},{7,6},{8,9},{9,8},{10,11... | collective-permute-start | bytes 196616 | tf_op jit(solution)/shard_map/ppermute | solution.py:320
  23.9 2.0 %collective-permute-start.10 = (bf16[256,128]{1,0:T(8,128)(2,1)S(1)}, bf16[256,128]{1,0:T(8,128)(2,1)S(1)}, u32[]{:S(2)}, u32[]{:S(2)}) collective-permute-start(bf16[256,128]{1,0:T(8,128)(2,1)S(1)} %collective-permute-done.5.refs_2_), channel_id=1, source_target_pairs={{0,1},{1,0},{2,3},{3,2},{4,5},{5,4},{6,7},{7,6},{8,9},{9,8},{10,11... | collective-permute-start | bytes 196616 | tf_op jit(solution)/shard_map/ppermute | solution.py:320
  24.4 1.5 %collective-permute-start.9 = (bf16[256,128]{1,0:T(8,128)(2,1)S(1)}, bf16[256,128]{1,0:T(8,128)(2,1)S(1)}, u32[]{:S(2)}, u32[]{:S(2)}) collective-permute-start(bf16[256,128]{1,0:T(8,128)(2,1)S(1)} %collective-permute-done.4.refs_1_), channel_id=1, source_target_pairs={{0,1},{1,0},{2,3},{3,2},{4,5},{5,4},{6,7},{7,6},{8,9},{9,8},{10,11... | collective-permute-start | bytes 196616 | tf_op jit(solution)/shard_map/ppermute | solution.py:320
  24.4 33.6 %collective-permute-start.7 = (bf16[384,1536]{1,0:T(8,128)(2,1)S(1)}, bf16[384,1536]{1,0:T(8,128)(2,1)S(1)}, u32[]{:S(2)}, u32[]{:S(2)}) collective-permute-start(bf16[384,1536]{1,0:T(8,128)(2,1)S(1)} %dynamic_slice.6), channel_id=1, source_target_pairs={{0,16},{1,17},{2,18},{3,19},{4,20},{5,21},{6,22},{7,23},{8,24},{9,... | collective-permute-start | bytes 3538952 | tf_op jit(solution)/shard_map/ppermute | solution.py:320
  58.1 9.6 %collective-permute-start.15 = (bf16[384,1536]{1,0:T(8,128)(2,1)S(1)}, bf16[384,1536]{1,0:T(8,128)(2,1)S(1)}, u32[]{:S(2)}, u32[]{:S(2)}) collective-permute-start(bf16[384,1536]{1,0:T(8,128)(2,1)S(1)} %collective-permute-done.7.w_across_ref), channel_id=1, source_target_pairs={{0,1},{1,0},{2,3},{3,2},{4,5},{5,4},{6,7},{7,6},{8,9},{9,8},{10,11... | collective-permute-start | bytes 3538952 | tf_op jit(solution)/shard_map/ppermute | solution.py:320
  58.3 9.3 %collective-permute-start.14 = (bf16[192,384]{1,0:T(8,128)(2,1)S(1)}, bf16[192,384]{1,0:T(8,128)(2,1)S(1)}, u32[]{:S(2)}, u32[]{:S(2)}) collective-permute-start(bf16[192,384]{1,0:T(8,128)(2,1)S(1)} %get-tuple-element.45), channel_id=1, source_target_pairs={{0,17},{1,16},{2,19},{3,18},{4,21},{5,20},{6,23},{7,22},{8,25},{9,... | collective-permute-start | bytes 442376 | tf_op jit(solution)/shard_map/ppermute | solution.py:320
  59.4 8.2 %collective-permute-start.12 = (bf16[192,384]{1,0:T(8,128)(2,1)S(1)}, bf16[192,384]{1,0:T(8,128)(2,1)S(1)}, u32[]{:S(2)}, u32[]{:S(2)}) collective-permute-start(bf16[192,384]{1,0:T(8,128)(2,1)S(1)} %get-tuple-element.45), channel_id=1, source_target_pairs={{0,1},{1,0},{2,3},{3,2},{4,5},{5,4},{6,7},{7,6},{8,9},{9,8},{10,11... | collective-permute-start | bytes 442376 | tf_op jit(solution)/shard_map/ppermute | solution.py:320
  59.6 8.1 %collective-permute-start.13 = (bf16[192,384]{1,0:T(8,128)(2,1)S(1)}, bf16[192,384]{1,0:T(8,128)(2,1)S(1)}, u32[]{:S(2)}, u32[]{:S(2)}) collective-permute-start(bf16[192,384]{1,0:T(8,128)(2,1)S(1)} %get-tuple-element.44.own_ref), channel_id=1, source_target_pairs={{0,16},{1,17},{2,18},{3,19},{4,20},{5,21},{6,22},{7,23},{8,24},{9,... | collective-permute-start | bytes 442376 | tf_op jit(solution)/shard_map/ppermute | solution.py:320

commit v4 on v3

--- a/solution.py
+++ b/solution.py
@@ -8,6 +8,7 @@
 from jax.experimental.pallas import tpu as pltpu
 from jax.sharding import PartitionSpec as P
 
+
 STEPS = 50
 EPSILON = 1e-06
 F32 = jnp.float32
@@ -40,7 +41,7 @@
 
 
 def encode_kernel(step_ref, earlier_ref, partial_ref, weight_ref, latent_ref, noise_ref, tail_ref, out_ref):
-    frames, pixels, channels = partial_ref.shape
+    frames, pixels, _ = partial_ref.shape
     lat = noise_ref.shape[1]
     patch = lat * 4
     cells = pixels // 4
@@ -125,7 +126,7 @@
         patch_ref, w_q_ref, w_kv_ref, tok_a_ref, tok_b_ref, q_ref, k_ref, v_ref, s_a_ref,
         s_b_ref, x_ref, out_ref, semaphores,
     ) = refs[2 * pieces :]
-    heads, keys, size = k_ref.shape
+    heads, _, size = k_ref.shape
     levels, patch, width = w_hist_ref.shape
     depth = heads * size
     lanes = near[0].shape[1]
@@ -168,14 +169,14 @@
             at = (spot // 4) * rows + t * 4 * cells + (spot % 4) * cells
             patch_ref[at : at + cells, :] = jnp.where(lane < patch, moved, ones).astype(BF16)
 
-    def tokens_of(i, tok_ref):
-        source = patch_ref[pl.ds(pl.multiple_of(i * tile, tile), tile), :]
+    def tokens_of(at, count, tok_ref):
+        source = patch_ref[pl.ds(at, count), :]
         mixed = dot(jnp.concatenate([source] * 3, axis=1), gram_ref[...])
         mean = jnp.sum(mixed * source.astype(F32), axis=1, keepdims=True) / width
         inverse = lax.rsqrt(mean + EPSILON)
         for n in range(0, width, step):
             x = dot(source, wide_ref[:, n : n + step])
-            tok_ref[:, n : n + step] = (x * inverse * gain_ref[:, n : n + step]).astype(BF16)
+            tok_ref[0:count, n : n + step] = (x * inverse * gain_ref[:, n : n + step]).astype(BF16)
 
     def head_norm(values, gain):
         mean = jnp.mean(values * values, axis=1, keepdims=True)
@@ -188,28 +189,33 @@
             k_ref[h, pl.ds(at, count), :] = head_norm(both[:, h * size : (h + 1) * size], k_gain_ref[...])
             v_ref[h, pl.ds(at, count), :] = both[:, (heads + h) * size : (heads + h + 1) * size].astype(BF16)
 
-    tokens_of(0, tok_a_ref)
+    tokens_of(0, rows, tok_a_ref)
     for copy in copies:
         copy.wait()
+    tokens_of(rows, tile, tok_b_ref)
     q = dot(tok_a_ref[0:rows, :], w_q_ref[...])
     for h in range(heads):
         q_ref[h] = head_norm(q[:, h * size : (h + 1) * size], q_gain_ref[...])
-    tiles = patch_ref.shape[0] // tile
+    project(tok_a_ref[0:rows, :], 0)
+    section = patch_ref.shape[0]
 
     def pair(j, carry):
-        tokens_of(2 * j + 1, tok_b_ref)
-        project(tok_a_ref[...], pl.multiple_of(2 * j * tile, tile))
-        tokens_of(2 * j + 2, tok_a_ref)
-        project(tok_b_ref[...], pl.multiple_of((2 * j + 1) * tile, tile))
+        at = pl.multiple_of(rows + 2 * j * tile, rows)
+        tokens_of(at + tile, tile, tok_a_ref)
+        project(tok_b_ref[...], at)
+        tokens_of(at + 2 * tile, tile, tok_b_ref)
+        project(tok_a_ref[...], at + tile)
         return carry
 
-    if tiles > 2:
-        lax.fori_loop(0, tiles // 2 - 1, pair, 0)
-    tokens_of(tiles - 1, tok_b_ref)
-    project(tok_a_ref[...], (tiles - 2) * tile)
-    project(tok_b_ref[...], (tiles - 1) * tile)
-
-    section = tiles * tile
+    pairs = (section - 2 * rows) // tile // 2
+    if pairs == 1:
+        pair(0, 0)
+    elif pairs > 1:
+        lax.fori_loop(0, pairs, pair, 0)
+    tokens_of(section - rows, rows, tok_a_ref)
+    project(tok_b_ref[...], section - rows - tile)
+    project(tok_a_ref[0:rows, :], section - rows)
+
     slots = hist_ref.shape[0]
     owners = len(owner_masks)
     spread = 128 // slots
@@ -233,10 +239,10 @@
                 squares = squares + x[:, m : m + 128] * x[:, m : m + 128]
         inverse = lax.rsqrt(jnp.sum(squares, axis=1, keepdims=True) / width + EPSILON)
         for n in range(0, width, step):
-            tok_a_ref[0:count, n : n + step] = (
+            tok_b_ref[0:count, n : n + step] = (
                 x_ref[0:count, n : n + step] * inverse * gain_ref[:, n : n + step]
             ).astype(BF16)
-        project(tok_a_ref[0:count, :], section + r * slots)
+        project(tok_b_ref[0:count, :], section + r * slots)
         slot = lax.broadcasted_iota(jnp.int32, (1, count), 1)
         live = jnp.zeros((1, count), jnp.int32)
         for o in range(len(taken)):
@@ -294,21 +300,32 @@
         sib_ref[t * part : (t + 1) * part, :] = out_ref[base + part : base + 2 * part, :]
 
 
-def combine_kernel(
-    own_ref, sib_ref, across_ref, corner_ref, w_local_ref, w_across_ref, w_corner_ref, out_ref
-):
+def combine_local_kernel(own_ref, sib_ref, w_local_ref, total_ref):
     core = lax.axis_index("seq") % 2
     depth = own_ref.shape[1]
     mine = pl.ds(pl.multiple_of(core * depth, depth), depth)
     other = pl.ds(pl.multiple_of((1 - core) * depth, depth), depth)
     step = 512
-    for n in range(0, out_ref.shape[1], step):
+    for n in range(0, total_ref.shape[1], step):
         columns = slice(n, n + step)
         total = dot(own_ref[...], w_local_ref[mine, columns])
-        total = total + dot(sib_ref[...], w_local_ref[other, columns])
-        total = total + dot(across_ref[...], w_across_ref[:, columns])
+        total_ref[:, columns] = total + dot(sib_ref[...], w_local_ref[other, columns])
+
+
+def combine_kernel(total_ref, across_ref, corner_ref, w_across_ref, w_corner_ref, out_ref, held_ref, semaphores):
+    step = 512
+    copies = []
+    for number, n in enumerate(range(0, held_ref.shape[1], step)):
+        columns = slice(n, n + step)
+        total = total_ref[:, columns] + dot(across_ref[...], w_across_ref[:, columns])
         total = total + dot(corner_ref[...], w_corner_ref[:, columns])
-        out_ref[:, columns] = total.astype(BF16)
+        held_ref[:, columns] = total.astype(BF16)
+        copies.append(
+            pltpu.make_async_copy(held_ref.at[:, columns], out_ref.at[:, columns], semaphores.at[number])
+        )
+        copies[-1].start()
+    for copy in copies:
+        copy.wait()
 
 
 def in_hbm(*values):
@@ -394,9 +411,9 @@
         if number + 1 < len(rounds):
             gathered = jnp.concatenate(near, axis=0)
             gathered, w_send = lax.optimization_barrier((gathered, w_send))
-    far = [flip(piece, 1, seq_count) for piece in near]
-
-    w_send, *near = lax.optimization_barrier((w_send, *near))
+    far = [flip(near[0], 1, seq_count)]
+    far += [flip(piece, 1, seq_count) for piece in near[1:]]
+
     w_across = flip(w_send, seq_count, seq_count)
     w_local = lax.dynamic_slice_in_dim(w_out, group * columns, columns, axis=1)
 
@@ -451,14 +468,25 @@
     from_sib = flip(sib, 1, seq_count)
     across = flip(own, seq_count, seq_count)
     corner = flip(sib, seq_count + 1, seq_count)
+    total = pl.pallas_call(
+        combine_local_kernel,
+        out_shape=jax.ShapeDtypeStruct((rows // 2, columns), F32),
+        in_specs=[VMEM] * 3,
+        out_specs=VMEM,
+        compiler_params=pltpu.CompilerParams(vmem_limit_bytes=10 * 2**20),
+        name="combine_local",
+    )(own, from_sib, w_local)
     return pl.pallas_call(
         combine_kernel,
         out_shape=jax.ShapeDtypeStruct((rows // 2, columns), BF16),
-        in_specs=[VMEM] * 7,
-        out_specs=VMEM,
+        in_specs=[VMEM] * 5,
+        out_specs=anywhere,
+        scratch_shapes=[
+            pltpu.VMEM((rows // 2, columns), BF16), pltpu.SemaphoreType.DMA((columns // 512,))
+        ],
         compiler_params=pltpu.CompilerParams(vmem_limit_bytes=10 * 2**20),
         name="combine",
-    )(own, from_sib, across, corner, w_local, w_across, w_corner)
+    )(total, across, corner, w_across, w_corner)
 
 
 def solution(mesh):

time: 70.2 us -> 72.9 us (1.038)
  waiting for transfers between devices: 10.8 us -> 12.9 us
  Pallas kernels: 37 us -> 38.2 us
    ppermute x15, waiting for transfers between devices: 10.8 us -> 12.9 us  [flip(): return lax.ppermute(value, ('grp', 'seq'), pairs)]
    pallas_call x1, Pallas kernels: 32.1 us -> 33.2 us  [local(): pl.pallas_call(functools.partial(joint_kernel, cells=cells, block=block,...]
    pallas_call x0 -> x1, Pallas kernels: none -> 0.78 us  [local(): pl.pallas_call(combine_local_kernel, out_shape=jax.ShapeDtypeStruct((rows...]
    pallas_call x1, Pallas kernels: 2.22 us -> 1.49 us  [local(): pl.pallas_call(combine_kernel, out_shape=jax.ShapeDtypeStruct((rows // 2,...]
  transfers between devices with their start and end apart: 16 -> 16, of which waited for: 6 -> 8; matrix products, arithmetic and copies ran while one was open for 6% -> 6% of each run, Pallas kernels for 48% -> 49%
where the time goes in v4:
time: 72.9 us; the launch traced here: 72.7 us
  Pallas kernels  38.2 us (52%)
  starting transfers between devices  16.5 us (23%)
  waiting for transfers between devices  12.9 us (18%)
  local copies, waits for them, and re-layouts  3.28 us (4%)
  between operations  0.94 us (1%)
  other arithmetic  0.82 us (1%)
    pallas_call x1, Pallas kernels, local(): pl.pallas_call(functools.partial(joint_kernel, cells=cells, block=block,...  33.2 us
    ppermute x15, starting transfers between devices, flip(): return lax.ppermute(value, ('grp', 'seq'), pairs)  14 us
    ppermute x15, waiting for transfers between devices, flip(): return lax.ppermute(value, ('grp', 'seq'), pairs)  12.9 us
    ppermute x1, starting transfers between devices, local(): lax.ppermute(swapped, 'seq', [(i, i + 1) for i in range(seq_count - 1)])  2.55 us
    dynamic_slice x1, local copies, waits for them, and re-layouts, local(): w_local = lax.dynamic_slice_in_dim(w_out, group * columns, columns, axis=1)  1.82 us
    pallas_call x1, Pallas kernels, local(): pl.pallas_call(prepare_kernel, out_shape=[jax.ShapeDtypeStruct((lanes, wi...  1.62 us
    pallas_call x1, Pallas kernels, local(): pl.pallas_call(combine_kernel, out_shape=jax.ShapeDtypeStruct((rows // 2,...  1.49 us
  transfers between devices with their start and end apart: 16, of which 8 were waited for; matrix products, arithmetic and copies ran while one was open for 6% of the time, Pallas kernels for 49%

profile of v4, /device:TPU:0, one launch (start us, length us, event | category | flops | bytes accessed | tf_op | source)
XLA Modules:
  0.0 72.7 jit_solution(14675551801015432119)
XLA Ops:
  0.0 0.0 copy-start
  0.0 0.0 copy-start.2
  0.0 2.6 %collective-permute-start = (bf16[2,192,128]{2,1,0:T(8,128)(2,1)}, bf16[2,192,128]{2,1,0:T(8,128)(2,1)S(1)}, u32[]{:S(2)}, u32[]{:S(2)}) collective-permute-start(bf16[2,192,128]{2,1,0:T(8,128)(2,1)} %bitcast.10), channel_id=1, source_target_pairs={{0,1},{1,2},{2,3},{3,4},{4,5},{5,6},{6,7},{7,8},{8,9},{9,10},{10,1... | collective-permute-start | bytes 294920 | tf_op jit(solution)/shard_map/ppermute | solution.py:360
  3.2 0.8 %fusion = (f32[1,1536]{1,0:T(1,128)}, f32[1,1536]{1,0:T(1,128)}) fusion(f32[]{:T(128)} %bitcast.1), kind=kLoop, calls=%fused_computation.2 | loop fusion | flops 3072 | bytes 12292 | tf_op jit(solution)/shard_map/sin | solution.py:32
  4.0 1.6 %prepare.1 = (bf16[128,3072]{1,0:T(8,128)(2,1)S(1)}, bf16[384,128]{1,0:T(8,128)(2,1)S(1)}, f32[2,192,128]{2,1,0:T(8,128)S(1)}, bf16[2,128,128]{2,1,0:T(8,128)(2,...) custom-call(bf16[64,3072]{1,0:T(8,128)(2,1)} %w_in_ref.1, ...), custom_call_target="tpu_custom_call" | custom-call | tf_op jit(solution)/shard_map/prepare/pallas_call | solution.py:362
  5.7 0.0 collective-permute-done.earlier_ref
  5.7 1.1 %encode.1 = bf16[64,128]{1,0:T(8,128)(2,1)S(1)} custom-call(s32[1]{0:T(128)S(6)} %copy.19.step_ref, bf16[2,192,128]{2,1,0:T(8,128)(2,1)S(1)} %collective-permute-done.earlier_ref, f32[2,192,128]{2,1,0:T(8,128)S(1)} %get-tuple-element.23.partial_ref, bf16[2,128,128]{2,1,0:T(8,128)(2,1)S(1)} %get-tuple-element.24.weight_ref, ...), custom_call_target="tpu_custom_call" | custom-call | tf_op jit(solution)/shard_map/encode/pallas_call | solution.py:384
  6.8 5.6 %collective-permute-start.1 = (bf16[64,128]{1,0:T(8,128)(2,1)S(1)}, bf16[64,128]{1,0:T(8,128)(2,1)S(1)}, u32[]{:S(2)}, u32[]{:S(2)}) collective-permute-start(bf16[64,128]{1,0:T(8,128)(2,1)S(1)} %encode.1), channel_id=1, source_target_pairs={{0,8},{1,9},{2,10},{3,11},{4,12},{5,13},{6,14},{7,15},{8,0},{9,1},... | collective-permute-start | bytes 49160 | tf_op jit(solution)/shard_map/ppermute | solution.py:337
  12.4 1.6 %collective-permute-start.2 = (bf16[64,128]{1,0:T(8,128)(2,1)S(1)}, bf16[64,128]{1,0:T(8,128)(2,1)S(1)}, u32[]{:S(2)}, u32[]{:S(2)}) collective-permute-start(bf16[64,128]{1,0:T(8,128)(2,1)S(1)} %encode.1), channel_id=1, source_target_pairs={{0,4},{1,5},{2,6},{3,7},{4,0},{5,1},{6,2},{7,3},{8,12},{9,13},{10,... | collective-permute-start | bytes 49160 | tf_op jit(solution)/shard_map/ppermute | solution.py:337
  14.0 0.0 collective-permute-start.3
  14.0 1.4 %dynamic_slice.6 = bf16[384,1536]{1,0:T(8,128)(2,1)S(1)} dynamic-slice(bf16[768,3072]{1,0:T(8,128)(2,1)} %param.35, s32[]{:T(128)S(6)} %select_n.17, s32[]{:T(128)S(6)} %select_n.18), dynamic_slice_sizes={384,1536} | dynamic-slice | bytes 2359300 | tf_op jit(solution)/shard_map/dynamic_slice | solution.py:393
  15.4 0.0 collective-permute-done.1
  15.4 0.7 collective-permute-done.2
  16.1 3.4 %collective-permute-done.3 = bf16[64,128]{1,0:T(8,128)(2,1)S(1)} collective-permute-done((bf16[64,128]{1,0:T(8,128)(2,1)S(1)}, bf16[64,128]{1,0:T(8,128)(2,1)S(1)}, u32[]{:S(2)}, u32[]{:S(2)}) %collective-permute-start.3) | collective-permute-done | bytes 16416 | tf_op jit(solution)/shard_map/ppermute | solution.py:337
  19.5 1.5 %collective-permute-start.6 = (bf16[256,128]{1,0:T(8,128)(2,1)S(1)}, bf16[256,128]{1,0:T(8,128)(2,1)S(1)}, u32[]{:S(2)}, u32[]{:S(2)}) collective-permute-start(bf16[256,128]{1,0:T(8,128)(2,1)S(1)} %pad_maximum_fusion.refs_0_), channel_id=1, source_target_pairs={{0,16},{1,17},{2,18},{3,19},{4,20},{5,21},{6,22},{7,23},{8,24},{9,... | collective-permute-start | bytes 196616 | tf_op jit(solution)/shard_map/ppermute | solution.py:337
  21.0 0.6 collective-permute-start.7
  21.6 1.4 %collective-permute-start.5 = (bf16[256,128]{1,0:T(8,128)(2,1)S(1)}, bf16[256,128]{1,0:T(8,128)(2,1)S(1)}, u32[]{:S(2)}, u32[]{:S(2)}) collective-permute-start(bf16[256,128]{1,0:T(8,128)(2,1)S(1)} %pad_maximum_fusion.refs_0_), channel_id=1, source_target_pairs={{0,2},{1,3},{2,0},{3,1},{4,6},{5,7},{6,4},{7,5},{8,10},{9,11},{10,... | collective-permute-start | bytes 196616 | tf_op jit(solution)/shard_map/ppermute | solution.py:337
  23.0 0.0 collective-permute-start.8
  23.0 0.8 %collective-permute-done.6.refs_2_ = bf16[256,128]{1,0:T(8,128)(2,1)S(1)} collective-permute-done((bf16[256,128]{1,0:T(8,128)(2,1)S(1)}, bf16[256,128]{1,0:T(8,128)(2,1)S(1)}, u32[]{:S(2)}, u32[]{:S(2)}) %collective-permute-start.6) | collective-permute-done | bytes 65568 | tf_op jit(solution)/shard_map/ppermute | solution.py:337
  23.8 0.0 collective-permute-start.10
  23.8 2.5 %collective-permute-done.7.refs_3_ = bf16[256,128]{1,0:T(8,128)(2,1)S(1)} collective-permute-done((bf16[256,128]{1,0:T(8,128)(2,1)S(1)}, bf16[256,128]{1,0:T(8,128)(2,1)S(1)}, u32[]{:S(2)}, u32[]{:S(2)}) %collective-permute-start.7) | collective-permute-done | bytes 65568 | tf_op jit(solution)/shard_map/ppermute | solution.py:337
  26.3 0.0 collective-permute-start.11
  26.3 0.3 collective-permute-done.5.refs_1_
  26.6 0.2 collective-permute-start.9
  26.8 0.6 collective-permute-start.4
  27.4 0.0 collective-permute-done.8.refs_4_
  27.4 0.0 collective-permute-done.10.refs_6_
  27.4 0.1 collective-permute-done.11.refs_7_
  27.5 0.3 collective-permute-done.9.refs_5_
  27.8 0.0 copy-done
  27.8 0.0 copy-done.2
  27.8 0.0 copy-done.4
  27.8 0.0 copy-done.5
  27.8 0.0 copy-done.3
  27.8 0.0 copy-done.1
  27.9 33.2 %joint.1 = (bf16[192,384]{1,0:T(8,128)(2,1)S(1)}, bf16[192,384]{1,0:T(8,128)(2,1)S(1)}) custom-call(bf16[256,128]{1,0:T(8,128)(2,1)S(1)} %pad_maximum_fusion.refs_0_, bf16[256,128]{1,0:T(8,128)(2,1)S(1)} %collective-permute-done.5.refs_1_, bf16[256,128]{1,0:T(8,128)(2,1)S(1)} %collective-permute-done.6.refs_2_, ...), custom_call_target="tpu_custom_call" | custom-call | flops 24536678400 | bytes 7077888 | tf_op jit(solution)/shard_map/joint/pallas_call | solution.py:432
  61.1 0.0 collective-permute-done.4.w_across_ref
  61.1 0.3 collective-permute-start.15
  61.4 0.3 collective-permute-start.12
  61.7 0.7 %collective-permute-start.14 = (bf16[192,384]{1,0:T(8,128)(2,1)S(1)}, bf16[192,384]{1,0:T(8,128)(2,1)S(1)}, u32[]{:S(2)}, u32[]{:S(2)}) collective-permute-start(bf16[192,384]{1,0:T(8,128)(2,1)S(1)} %get-tuple-element.35), channel_id=1, source_target_pairs={{0,17},{1,16},{2,19},{3,18},{4,21},{5,20},{6,23},{7,22},{8,25},{9,... | collective-permute-start | bytes 442376 | tf_op jit(solution)/shard_map/ppermute | solution.py:337
  62.4 1.1 %collective-permute-start.13 = (bf16[192,384]{1,0:T(8,128)(2,1)S(1)}, bf16[192,384]{1,0:T(8,128)(2,1)S(1)}, u32[]{:S(2)}, u32[]{:S(2)}) collective-permute-start(bf16[192,384]{1,0:T(8,128)(2,1)S(1)} %get-tuple-element.34.own_ref), channel_id=1, source_target_pairs={{0,16},{1,17},{2,18},{3,19},{4,20},{5,21},{6,22},{7,23},{8,24},{9,... | collective-permute-start | bytes 442376 | tf_op jit(solution)/shard_map/ppermute | solution.py:337
  63.5 1.8 %constant_dynamic-slice_fusion.w_local_ref = bf16[768,1536]{1,0:T(8,128)(2,1)S(1)} fusion(bf16[768,3072]{1,0:T(8,128)(2,1)} %param.35, s32[]{:T(128)S(6)} %select_n.19), kind=kLoop, calls=%fused_computation.4 | loop fusion | bytes 4718596 | tf_op jit(solution)/shard_map/dynamic_slice | solution.py:418
  65.4 0.0 collective-permute-done.12.sib_ref
  65.4 0.8 %combine_local.1.total_ref = f32[192,1536]{1,0:T(8,128)S(1)} custom-call(bf16[192,384]{1,0:T(8,128)(2,1)S(1)} %get-tuple-element.34.own_ref, bf16[192,384]{1,0:T(8,128)(2,1)S(1)} %collective-permute-done.12.sib_ref, bf16[768,1536]{1,0:T(8,128)(2,1)S(1)} %constant_dynamic-slice_fusion.w_local_ref), custom_call_target="tpu_custom_call" | custom-call | tf_op jit(solution)/shard_map/combine_local/pallas_call | solution.py:471
  66.2 4.8 %collective-permute-done.13.across_ref = bf16[192,384]{1,0:T(8,128)(2,1)S(1)} collective-permute-done((bf16[192,384]{1,0:T(8,128)(2,1)S(1)}, bf16[192,384]{1,0:T(8,128)(2,1)S(1)}, u32[]{:S(2)}, u32[]{:S(2)}) %collective-permute-start.13) | collective-permute-done | bytes 147488 | tf_op jit(solution)/shard_map/ppermute | solution.py:337
  71.0 0.0 collective-permute-done.14.corner_ref
  71.0 0.0 collective-permute-done.15.w_corner_ref
  71.0 1.5 %combine.1 = bf16[192,1536]{1,0:T(8,128)(2,1)} custom-call(f32[192,1536]{1,0:T(8,128)S(1)} %combine_local.1.total_ref, bf16[192,384]{1,0:T(8,128)(2,1)S(1)} %collective-permute-done.13.across_ref, bf16[192,384]{1,0:T(8,128)(2,1)S(1)} %collective-permute-done.14.corner_ref, bf16[384,1536]{1,0:T(8,128)(2,1)S(1)} %collective-permute-done.4.w_across_ref, ...), custom_call_target="tpu_custom_call" | custom-call | tf_op jit(solution)/shard_map/combine/pallas_call | solution.py:479
  (5 shorter events, 0.0 us)
Async XLA Ops:
  0.0 27.8 %copy-start = (bf16[8,64]{1,0:T(8,128)(2,1)S(1)}, bf16[8,64]{1,0:T(8,128)(2,1)}, u32[]{:S(2)}) copy-start(bf16[8,64]{1,0:T(8,128)(2,1)} %refs_18_.1) | copy-start | bytes 3076
  0.0 27.8 %copy-start.2 = (f32[3072]{0:T(1024)S(1)}, f32[3072]{0:T(1024)}, u32[]{:S(2)}) copy-start(f32[3072]{0:T(1024)} %param.29) | copy-start | bytes 36868
  0.0 27.8 %copy-start.4 = (f32[128]{0:T(128)S(1)}, f32[128]{0:T(128)}, u32[]{:S(2)}) copy-start(f32[128]{0:T(128)} %param.33) | copy-start | bytes 1540
  0.0 27.8 %copy-start.5 = (f32[128]{0:T(128)S(1)}, f32[128]{0:T(128)}, u32[]{:S(2)}) copy-start(f32[128]{0:T(128)} %param.34) | copy-start | bytes 1540
  0.0 27.8 %copy-start.3 = (s32[16]{0:T(128)S(1)}, s32[16]{0:T(128)}, u32[]{:S(2)}) copy-start(s32[16]{0:T(128)} %refs_8_.1) | copy-start | bytes 196
  0.0 5.6 %collective-permute-start = (bf16[2,192,128]{2,1,0:T(8,128)(2,1)}, bf16[2,192,128]{2,1,0:T(8,128)(2,1)S(1)}, u32[]{:S(2)}, u32[]{:S(2)}) collective-permute-start(bf16[2,192,128]{2,1,0:T(8,128)(2,1)} %bitcast.10), channel_id=1, source_target_pairs={{0,1},{1,2},{2,3},{3,4},{4,5},{5,6},{6,7},{7,8},{8,9},{9,10},{10,1... | collective-permute-start | bytes 294920 | tf_op jit(solution)/shard_map/ppermute | solution.py:360
  6.8 8.7 %collective-permute-start.1 = (bf16[64,128]{1,0:T(8,128)(2,1)S(1)}, bf16[64,128]{1,0:T(8,128)(2,1)S(1)}, u32[]{:S(2)}, u32[]{:S(2)}) collective-permute-start(bf16[64,128]{1,0:T(8,128)(2,1)S(1)} %encode.1), channel_id=1, source_target_pairs={{0,8},{1,9},{2,10},{3,11},{4,12},{5,13},{6,14},{7,15},{8,0},{9,1},... | collective-permute-start | bytes 49160 | tf_op jit(solution)/shard_map/ppermute | solution.py:337
  12.4 3.7 %collective-permute-start.2 = (bf16[64,128]{1,0:T(8,128)(2,1)S(1)}, bf16[64,128]{1,0:T(8,128)(2,1)S(1)}, u32[]{:S(2)}, u32[]{:S(2)}) collective-permute-start(bf16[64,128]{1,0:T(8,128)(2,1)S(1)} %encode.1), channel_id=1, source_target_pairs={{0,4},{1,5},{2,6},{3,7},{4,0},{5,1},{6,2},{7,3},{8,12},{9,13},{10,... | collective-permute-start | bytes 49160 | tf_op jit(solution)/shard_map/ppermute | solution.py:337
  14.0 5.5 %collective-permute-start.3 = (bf16[64,128]{1,0:T(8,128)(2,1)S(1)}, bf16[64,128]{1,0:T(8,128)(2,1)S(1)}, u32[]{:S(2)}, u32[]{:S(2)}) collective-permute-start(bf16[64,128]{1,0:T(8,128)(2,1)S(1)} %encode.1), channel_id=1, source_target_pairs={{0,12},{1,13},{2,14},{3,15},{4,8},{5,9},{6,10},{7,11},{8,4},{9,5},... | collective-permute-start | bytes 49160 | tf_op jit(solution)/shard_map/ppermute | solution.py:337
  14.0 13.9 %copy-start.1 = (bf16[3,64,3072]{2,1,0:T(8,128)(2,1)S(1)}, bf16[3,64,3072]{2,1,0:T(8,128)(2,1)}, u32[]{:S(2)}) copy-start(bf16[3,64,3072]{2,1,0:T(8,128)(2,1)} %refs_11_.1) | copy-start | bytes 3538948
  19.5 4.3 %collective-permute-start.6 = (bf16[256,128]{1,0:T(8,128)(2,1)S(1)}, bf16[256,128]{1,0:T(8,128)(2,1)S(1)}, u32[]{:S(2)}, u32[]{:S(2)}) collective-permute-start(bf16[256,128]{1,0:T(8,128)(2,1)S(1)} %pad_maximum_fusion.refs_0_), channel_id=1, source_target_pairs={{0,16},{1,17},{2,18},{3,19},{4,20},{5,21},{6,22},{7,23},{8,24},{9,... | collective-permute-start | bytes 196616 | tf_op jit(solution)/shard_map/ppermute | solution.py:337
  21.0 5.3 %collective-permute-start.7 = (bf16[256,128]{1,0:T(8,128)(2,1)S(1)}, bf16[256,128]{1,0:T(8,128)(2,1)S(1)}, u32[]{:S(2)}, u32[]{:S(2)}) collective-permute-start(bf16[256,128]{1,0:T(8,128)(2,1)S(1)} %pad_maximum_fusion.refs_0_), channel_id=1, source_target_pairs={{0,18},{1,19},{2,16},{3,17},{4,22},{5,23},{6,20},{7,21},{8,26},{9,... | collective-permute-start | bytes 196616 | tf_op jit(solution)/shard_map/ppermute | solution.py:337
  21.6 5.0 %collective-permute-start.5 = (bf16[256,128]{1,0:T(8,128)(2,1)S(1)}, bf16[256,128]{1,0:T(8,128)(2,1)S(1)}, u32[]{:S(2)}, u32[]{:S(2)}) collective-permute-start(bf16[256,128]{1,0:T(8,128)(2,1)S(1)} %pad_maximum_fusion.refs_0_), channel_id=1, source_target_pairs={{0,2},{1,3},{2,0},{3,1},{4,6},{5,7},{6,4},{7,5},{8,10},{9,11},{10,... | collective-permute-start | bytes 196616 | tf_op jit(solution)/shard_map/ppermute | solution.py:337
  23.0 4.4 %collective-permute-start.8 = (bf16[256,128]{1,0:T(8,128)(2,1)S(1)}, bf16[256,128]{1,0:T(8,128)(2,1)S(1)}, u32[]{:S(2)}, u32[]{:S(2)}) collective-permute-start(bf16[256,128]{1,0:T(8,128)(2,1)S(1)} %pad_maximum_fusion.refs_0_), channel_id=1, source_target_pairs={{0,1},{1,0},{2,3},{3,2},{4,5},{5,4},{6,7},{7,6},{8,9},{9,8},{10,11... | collective-permute-start | bytes 196616 | tf_op jit(solution)/shard_map/ppermute | solution.py:337
  23.8 3.6 %collective-permute-start.10 = (bf16[256,128]{1,0:T(8,128)(2,1)S(1)}, bf16[256,128]{1,0:T(8,128)(2,1)S(1)}, u32[]{:S(2)}, u32[]{:S(2)}) collective-permute-start(bf16[256,128]{1,0:T(8,128)(2,1)S(1)} %collective-permute-done.6.refs_2_), channel_id=1, source_target_pairs={{0,1},{1,0},{2,3},{3,2},{4,5},{5,4},{6,7},{7,6},{8,9},{9,8},{10,11... | collective-permute-start | bytes 196616 | tf_op jit(solution)/shard_map/ppermute | solution.py:337
  26.3 1.3 %collective-permute-start.11 = (bf16[256,128]{1,0:T(8,128)(2,1)S(1)}, bf16[256,128]{1,0:T(8,128)(2,1)S(1)}, u32[]{:S(2)}, u32[]{:S(2)}) collective-permute-start(bf16[256,128]{1,0:T(8,128)(2,1)S(1)} %collective-permute-done.7.refs_3_), channel_id=1, source_target_pairs={{0,1},{1,0},{2,3},{3,2},{4,5},{5,4},{6,7},{7,6},{8,9},{9,8},{10,11... | collective-permute-start | bytes 196616 | tf_op jit(solution)/shard_map/ppermute | solution.py:337
  26.6 1.3 %collective-permute-start.9 = (bf16[256,128]{1,0:T(8,128)(2,1)S(1)}, bf16[256,128]{1,0:T(8,128)(2,1)S(1)}, u32[]{:S(2)}, u32[]{:S(2)}) collective-permute-start(bf16[256,128]{1,0:T(8,128)(2,1)S(1)} %collective-permute-done.5.refs_1_), channel_id=1, source_target_pairs={{0,1},{1,0},{2,3},{3,2},{4,5},{5,4},{6,7},{7,6},{8,9},{9,8},{10,11... | collective-permute-start | bytes 196616 | tf_op jit(solution)/shard_map/ppermute | solution.py:337
  26.8 34.3 %collective-permute-start.4 = (bf16[384,1536]{1,0:T(8,128)(2,1)S(1)}, bf16[384,1536]{1,0:T(8,128)(2,1)S(1)}, u32[]{:S(2)}, u32[]{:S(2)}) collective-permute-start(bf16[384,1536]{1,0:T(8,128)(2,1)S(1)} %dynamic_slice.6), channel_id=1, source_target_pairs={{0,16},{1,17},{2,18},{3,19},{4,20},{5,21},{6,22},{7,23},{8,24},{9,... | collective-permute-start | bytes 3538952 | tf_op jit(solution)/shard_map/ppermute | solution.py:337
  61.1 9.9 %collective-permute-start.15 = (bf16[384,1536]{1,0:T(8,128)(2,1)S(1)}, bf16[384,1536]{1,0:T(8,128)(2,1)S(1)}, u32[]{:S(2)}, u32[]{:S(2)}) collective-permute-start(bf16[384,1536]{1,0:T(8,128)(2,1)S(1)} %collective-permute-done.4.w_across_ref), channel_id=1, source_target_pairs={{0,1},{1,0},{2,3},{3,2},{4,5},{5,4},{6,7},{7,6},{8,9},{9,8},{10,11... | collective-permute-start | bytes 3538952 | tf_op jit(solution)/shard_map/ppermute | solution.py:337
  61.4 4.0 %collective-permute-start.12 = (bf16[192,384]{1,0:T(8,128)(2,1)S(1)}, bf16[192,384]{1,0:T(8,128)(2,1)S(1)}, u32[]{:S(2)}, u32[]{:S(2)}) collective-permute-start(bf16[192,384]{1,0:T(8,128)(2,1)S(1)} %get-tuple-element.35), channel_id=1, source_target_pairs={{0,1},{1,0},{2,3},{3,2},{4,5},{5,4},{6,7},{7,6},{8,9},{9,8},{10,11... | collective-permute-start | bytes 442376 | tf_op jit(solution)/shard_map/ppermute | solution.py:337
  61.7 9.3 %collective-permute-start.14 = (bf16[192,384]{1,0:T(8,128)(2,1)S(1)}, bf16[192,384]{1,0:T(8,128)(2,1)S(1)}, u32[]{:S(2)}, u32[]{:S(2)}) collective-permute-start(bf16[192,384]{1,0:T(8,128)(2,1)S(1)} %get-tuple-element.35), channel_id=1, source_target_pairs={{0,17},{1,16},{2,19},{3,18},{4,21},{5,20},{6,23},{7,22},{8,25},{9,... | collective-permute-start | bytes 442376 | tf_op jit(solution)/shard_map/ppermute | solution.py:337
  62.4 8.6 %collective-permute-start.13 = (bf16[192,384]{1,0:T(8,128)(2,1)S(1)}, bf16[192,384]{1,0:T(8,128)(2,1)S(1)}, u32[]{:S(2)}, u32[]{:S(2)}) collective-permute-start(bf16[192,384]{1,0:T(8,128)(2,1)S(1)} %get-tuple-element.34.own_ref), channel_id=1, source_target_pairs={{0,16},{1,17},{2,18},{3,19},{4,20},{5,21},{6,22},{7,23},{8,24},{9,... | collective-permute-start | bytes 442376 | tf_op jit(solution)/shard_map/ppermute | solution.py:337

commit v5 on v4

--- a/solution.py
+++ b/solution.py
@@ -169,14 +169,14 @@
             at = (spot // 4) * rows + t * 4 * cells + (spot % 4) * cells
             patch_ref[at : at + cells, :] = jnp.where(lane < patch, moved, ones).astype(BF16)
 
-    def tokens_of(at, count, tok_ref):
-        source = patch_ref[pl.ds(at, count), :]
+    def tokens_of(i, tok_ref):
+        source = patch_ref[pl.ds(pl.multiple_of(i * tile, tile), tile), :]
         mixed = dot(jnp.concatenate([source] * 3, axis=1), gram_ref[...])
         mean = jnp.sum(mixed * source.astype(F32), axis=1, keepdims=True) / width
         inverse = lax.rsqrt(mean + EPSILON)
         for n in range(0, width, step):
             x = dot(source, wide_ref[:, n : n + step])
-            tok_ref[0:count, n : n + step] = (x * inverse * gain_ref[:, n : n + step]).astype(BF16)
+            tok_ref[:, n : n + step] = (x * inverse * gain_ref[:, n : n + step]).astype(BF16)
 
     def head_norm(values, gain):
         mean = jnp.mean(values * values, axis=1, keepdims=True)
@@ -189,33 +189,28 @@
             k_ref[h, pl.ds(at, count), :] = head_norm(both[:, h * size : (h + 1) * size], k_gain_ref[...])
             v_ref[h, pl.ds(at, count), :] = both[:, (heads + h) * size : (heads + h + 1) * size].astype(BF16)
 
-    tokens_of(0, rows, tok_a_ref)
+    tokens_of(0, tok_a_ref)
     for copy in copies:
         copy.wait()
-    tokens_of(rows, tile, tok_b_ref)
     q = dot(tok_a_ref[0:rows, :], w_q_ref[...])
     for h in range(heads):
         q_ref[h] = head_norm(q[:, h * size : (h + 1) * size], q_gain_ref[...])
-    project(tok_a_ref[0:rows, :], 0)
-    section = patch_ref.shape[0]
+    tiles = patch_ref.shape[0] // tile
 
     def pair(j, carry):
-        at = pl.multiple_of(rows + 2 * j * tile, rows)
-        tokens_of(at + tile, tile, tok_a_ref)
-        project(tok_b_ref[...], at)
-        tokens_of(at + 2 * tile, tile, tok_b_ref)
-        project(tok_a_ref[...], at + tile)
+        tokens_of(2 * j + 1, tok_b_ref)
+        project(tok_a_ref[...], pl.multiple_of(2 * j * tile, tile))
+        tokens_of(2 * j + 2, tok_a_ref)
+        project(tok_b_ref[...], pl.multiple_of((2 * j + 1) * tile, tile))
         return carry
 
-    pairs = (section - 2 * rows) // tile // 2
-    if pairs == 1:
-        pair(0, 0)
-    elif pairs > 1:
-        lax.fori_loop(0, pairs, pair, 0)
-    tokens_of(section - rows, rows, tok_a_ref)
-    project(tok_b_ref[...], section - rows - tile)
-    project(tok_a_ref[0:rows, :], section - rows)
-
+    if tiles > 2:
+        lax.fori_loop(0, tiles // 2 - 1, pair, 0)
+    tokens_of(tiles - 1, tok_b_ref)
+    project(tok_a_ref[...], (tiles - 2) * tile)
+    project(tok_b_ref[...], (tiles - 1) * tile)
+
+    section = tiles * tile
     slots = hist_ref.shape[0]
     owners = len(owner_masks)
     spread = 128 // slots
@@ -239,10 +234,10 @@
                 squares = squares + x[:, m : m + 128] * x[:, m : m + 128]
         inverse = lax.rsqrt(jnp.sum(squares, axis=1, keepdims=True) / width + EPSILON)
         for n in range(0, width, step):
-            tok_b_ref[0:count, n : n + step] = (
+            tok_a_ref[0:count, n : n + step] = (
                 x_ref[0:count, n : n + step] * inverse * gain_ref[:, n : n + step]
             ).astype(BF16)
-        project(tok_b_ref[0:count, :], section + r * slots)
+        project(tok_a_ref[0:count, :], section + r * slots)
         slot = lax.broadcasted_iota(jnp.int32, (1, count), 1)
         live = jnp.zeros((1, count), jnp.int32)
         for o in range(len(taken)):
@@ -407,7 +402,9 @@
         rounds = [bits[:1]] + rounds
     for number, pair in enumerate(rounds):
         masks = [0] + [pair[0]] + ([pair[1], pair[0] ^ pair[1]] if len(pair) > 1 else [])
-        near = [gathered] + [flip(gathered, mask, seq_count) for mask in masks[1:]]
+        near = [gathered]
+        for mask in masks[1:]:
+            near.append(flip(gathered, mask, seq_count))
         if number + 1 < len(rounds):
             gathered = jnp.concatenate(near, axis=0)
             gathered, w_send = lax.optimization_barrier((gathered, w_send))

time: 72.9 us -> 71.8 us (0.985)
  Pallas kernels: 38.2 us -> 37.1 us
    pallas_call x1, Pallas kernels: 33.2 us -> 32.1 us  [local(): pl.pallas_call(functools.partial(joint_kernel, cells=cells, block=block,...]
  transfers between devices with their start and end apart: 16 -> 16, of which waited for: 8 -> 8; matrix products, arithmetic and copies ran while one was open for 6% -> 6% of each run, Pallas kernels for 49% -> 48%
where the time goes in v5:
time: 71.8 us; the launch traced here: 71.5 us
  Pallas kernels  37.1 us (52%)
  starting transfers between devices  16.5 us (23%)
  waiting for transfers between devices  12.9 us (18%)
  local copies, waits for them, and re-layouts  3.28 us (5%)
  between operations  0.94 us (1%)
  other arithmetic  0.82 us (1%)
    pallas_call x1, Pallas kernels, local(): pl.pallas_call(functools.partial(joint_kernel, cells=cells, block=block,...  32.1 us
    ppermute x15, starting transfers between devices, flip(): return lax.ppermute(value, ('grp', 'seq'), pairs)  14 us
    ppermute x15, waiting for transfers between devices, flip(): return lax.ppermute(value, ('grp', 'seq'), pairs)  12.9 us
    ppermute x1, starting transfers between devices, local(): lax.ppermute(swapped, 'seq', [(i, i + 1) for i in range(seq_count - 1)])  2.55 us
    dynamic_slice x1, local copies, waits for them, and re-layouts, local(): w_local = lax.dynamic_slice_in_dim(w_out, group * columns, columns, axis=1)  1.82 us
    pallas_call x1, Pallas kernels, local(): pl.pallas_call(prepare_kernel, out_shape=[jax.ShapeDtypeStruct((lanes, wi...  1.62 us
    pallas_call x1, Pallas kernels, local(): pl.pallas_call(combine_kernel, out_shape=jax.ShapeDtypeStruct((rows // 2,...  1.49 us
    dynamic_slice x1, local copies, waits for them, and re-layouts, local(): lax.dynamic_slice(w_out, (core * depth, (1 - group) * columns), (depth, c...  1.44 us
  transfers between devices with their start and end apart: 16, of which 8 were waited for; matrix products, arithmetic and copies ran while one was open for 6% of the time, Pallas kernels for 48%

profile of v5, /device:TPU:0, one launch (start us, length us, event | category | flops | bytes accessed | tf_op | source)
XLA Modules:
  0.0 71.5 jit_solution(11509885873018443603)
XLA Ops:
  0.0 0.0 copy-start
  0.0 0.0 copy-start.2
  0.0 2.6 %collective-permute-start = (bf16[2,192,128]{2,1,0:T(8,128)(2,1)}, bf16[2,192,128]{2,1,0:T(8,128)(2,1)S(1)}, u32[]{:S(2)}, u32[]{:S(2)}) collective-permute-start(bf16[2,192,128]{2,1,0:T(8,128)(2,1)} %bitcast.10), channel_id=1, source_target_pairs={{0,1},{1,2},{2,3},{3,4},{4,5},{5,6},{6,7},{7,8},{8,9},{9,10},{10,1... | collective-permute-start | bytes 294920 | tf_op jit(solution)/shard_map/ppermute | solution.py:355
  3.2 0.8 %fusion = (f32[1,1536]{1,0:T(1,128)}, f32[1,1536]{1,0:T(1,128)}) fusion(f32[]{:T(128)} %bitcast.1), kind=kLoop, calls=%fused_computation.2 | loop fusion | flops 3072 | bytes 12292 | tf_op jit(solution)/shard_map/sin | solution.py:32
  4.0 1.6 %prepare.1 = (bf16[128,3072]{1,0:T(8,128)(2,1)S(1)}, bf16[384,128]{1,0:T(8,128)(2,1)S(1)}, f32[2,192,128]{2,1,0:T(8,128)S(1)}, bf16[2,128,128]{2,1,0:T(8,128)(2,...) custom-call(bf16[64,3072]{1,0:T(8,128)(2,1)} %w_in_ref.1, ...), custom_call_target="tpu_custom_call" | custom-call | tf_op jit(solution)/shard_map/prepare/pallas_call | solution.py:357
  5.7 0.0 collective-permute-done.earlier_ref
  5.7 1.1 %encode.1 = bf16[64,128]{1,0:T(8,128)(2,1)S(1)} custom-call(s32[1]{0:T(128)S(6)} %copy.19.step_ref, bf16[2,192,128]{2,1,0:T(8,128)(2,1)S(1)} %collective-permute-done.earlier_ref, f32[2,192,128]{2,1,0:T(8,128)S(1)} %get-tuple-element.23.partial_ref, bf16[2,128,128]{2,1,0:T(8,128)(2,1)S(1)} %get-tuple-element.24.weight_ref, ...), custom_call_target="tpu_custom_call" | custom-call | tf_op jit(solution)/shard_map/encode/pallas_call | solution.py:379
  6.8 5.6 %collective-permute-start.1 = (bf16[64,128]{1,0:T(8,128)(2,1)S(1)}, bf16[64,128]{1,0:T(8,128)(2,1)S(1)}, u32[]{:S(2)}, u32[]{:S(2)}) collective-permute-start(bf16[64,128]{1,0:T(8,128)(2,1)S(1)} %encode.1), channel_id=1, source_target_pairs={{0,8},{1,9},{2,10},{3,11},{4,12},{5,13},{6,14},{7,15},{8,0},{9,1},... | collective-permute-start | bytes 49160 | tf_op jit(solution)/shard_map/ppermute | solution.py:332
  12.4 1.6 %collective-permute-start.2 = (bf16[64,128]{1,0:T(8,128)(2,1)S(1)}, bf16[64,128]{1,0:T(8,128)(2,1)S(1)}, u32[]{:S(2)}, u32[]{:S(2)}) collective-permute-start(bf16[64,128]{1,0:T(8,128)(2,1)S(1)} %encode.1), channel_id=1, source_target_pairs={{0,4},{1,5},{2,6},{3,7},{4,0},{5,1},{6,2},{7,3},{8,12},{9,13},{10,... | collective-permute-start | bytes 49160 | tf_op jit(solution)/shard_map/ppermute | solution.py:332
  14.0 0.0 collective-permute-start.3
  14.0 1.4 %dynamic_slice.6 = bf16[384,1536]{1,0:T(8,128)(2,1)S(1)} dynamic-slice(bf16[768,3072]{1,0:T(8,128)(2,1)} %param.35, s32[]{:T(128)S(6)} %select_n.17, s32[]{:T(128)S(6)} %select_n.18), dynamic_slice_sizes={384,1536} | dynamic-slice | bytes 2359300 | tf_op jit(solution)/shard_map/dynamic_slice | solution.py:388
  15.4 0.0 collective-permute-done.1
  15.4 0.7 collective-permute-done.2
  16.1 3.4 %collective-permute-done.3 = bf16[64,128]{1,0:T(8,128)(2,1)S(1)} collective-permute-done((bf16[64,128]{1,0:T(8,128)(2,1)S(1)}, bf16[64,128]{1,0:T(8,128)(2,1)S(1)}, u32[]{:S(2)}, u32[]{:S(2)}) %collective-permute-start.3) | collective-permute-done | bytes 16416 | tf_op jit(solution)/shard_map/ppermute | solution.py:332
  19.5 1.5 %collective-permute-start.6 = (bf16[256,128]{1,0:T(8,128)(2,1)S(1)}, bf16[256,128]{1,0:T(8,128)(2,1)S(1)}, u32[]{:S(2)}, u32[]{:S(2)}) collective-permute-start(bf16[256,128]{1,0:T(8,128)(2,1)S(1)} %pad_maximum_fusion.refs_0_), channel_id=1, source_target_pairs={{0,16},{1,17},{2,18},{3,19},{4,20},{5,21},{6,22},{7,23},{8,24},{9,... | collective-permute-start | bytes 196616 | tf_op jit(solution)/shard_map/ppermute | solution.py:332
  21.0 0.6 collective-permute-start.7
  21.6 1.4 %collective-permute-start.5 = (bf16[256,128]{1,0:T(8,128)(2,1)S(1)}, bf16[256,128]{1,0:T(8,128)(2,1)S(1)}, u32[]{:S(2)}, u32[]{:S(2)}) collective-permute-start(bf16[256,128]{1,0:T(8,128)(2,1)S(1)} %pad_maximum_fusion.refs_0_), channel_id=1, source_target_pairs={{0,2},{1,3},{2,0},{3,1},{4,6},{5,7},{6,4},{7,5},{8,10},{9,11},{10,... | collective-permute-start | bytes 196616 | tf_op jit(solution)/shard_map/ppermute | solution.py:332
  23.0 0.0 collective-permute-start.8
  23.0 0.8 %collective-permute-done.6.refs_2_ = bf16[256,128]{1,0:T(8,128)(2,1)S(1)} collective-permute-done((bf16[256,128]{1,0:T(8,128)(2,1)S(1)}, bf16[256,128]{1,0:T(8,128)(2,1)S(1)}, u32[]{:S(2)}, u32[]{:S(2)}) %collective-permute-start.6) | collective-permute-done | bytes 65568 | tf_op jit(solution)/shard_map/ppermute | solution.py:332
  23.8 0.0 collective-permute-start.10
  23.8 2.5 %collective-permute-done.7.refs_3_ = bf16[256,128]{1,0:T(8,128)(2,1)S(1)} collective-permute-done((bf16[256,128]{1,0:T(8,128)(2,1)S(1)}, bf16[256,128]{1,0:T(8,128)(2,1)S(1)}, u32[]{:S(2)}, u32[]{:S(2)}) %collective-permute-start.7) | collective-permute-done | bytes 65568 | tf_op jit(solution)/shard_map/ppermute | solution.py:332
  26.3 0.0 collective-permute-start.11
  26.3 0.3 collective-permute-done.5.refs_1_
  26.6 0.2 collective-permute-start.9
  26.8 0.6 collective-permute-start.4
  27.4 0.0 collective-permute-done.8.refs_4_
  27.4 0.0 collective-permute-done.10.refs_6_
  27.4 0.1 collective-permute-done.11.refs_7_
  27.5 0.3 collective-permute-done.9.refs_5_
  27.8 0.0 copy-done
  27.8 0.0 copy-done.2
  27.8 0.0 copy-done.4
  27.8 0.0 copy-done.5
  27.8 0.0 copy-done.3
  27.8 0.0 copy-done.1
  27.9 32.1 %joint.1 = (bf16[192,384]{1,0:T(8,128)(2,1)S(1)}, bf16[192,384]{1,0:T(8,128)(2,1)S(1)}) custom-call(bf16[256,128]{1,0:T(8,128)(2,1)S(1)} %pad_maximum_fusion.refs_0_, bf16[256,128]{1,0:T(8,128)(2,1)S(1)} %collective-permute-done.5.refs_1_, bf16[256,128]{1,0:T(8,128)(2,1)S(1)} %collective-permute-done.6.refs_2_, ...), custom_call_target="tpu_custom_call" | custom-call | flops 24536678400 | bytes 7077888 | tf_op jit(solution)/shard_map/joint/pallas_call | solution.py:429
  59.9 0.0 collective-permute-done.4.w_across_ref
  59.9 0.3 collective-permute-start.15
  60.2 0.3 collective-permute-start.12
  60.5 0.7 %collective-permute-start.14 = (bf16[192,384]{1,0:T(8,128)(2,1)S(1)}, bf16[192,384]{1,0:T(8,128)(2,1)S(1)}, u32[]{:S(2)}, u32[]{:S(2)}) collective-permute-start(bf16[192,384]{1,0:T(8,128)(2,1)S(1)} %get-tuple-element.35), channel_id=1, source_target_pairs={{0,17},{1,16},{2,19},{3,18},{4,21},{5,20},{6,23},{7,22},{8,25},{9,... | collective-permute-start | bytes 442376 | tf_op jit(solution)/shard_map/ppermute | solution.py:332
  61.2 1.1 %collective-permute-start.13 = (bf16[192,384]{1,0:T(8,128)(2,1)S(1)}, bf16[192,384]{1,0:T(8,128)(2,1)S(1)}, u32[]{:S(2)}, u32[]{:S(2)}) collective-permute-start(bf16[192,384]{1,0:T(8,128)(2,1)S(1)} %get-tuple-element.34.own_ref), channel_id=1, source_target_pairs={{0,16},{1,17},{2,18},{3,19},{4,20},{5,21},{6,22},{7,23},{8,24},{9,... | collective-permute-start | bytes 442376 | tf_op jit(solution)/shard_map/ppermute | solution.py:332
  62.4 1.8 %constant_dynamic-slice_fusion.w_local_ref = bf16[768,1536]{1,0:T(8,128)(2,1)S(1)} fusion(bf16[768,3072]{1,0:T(8,128)(2,1)} %param.35, s32[]{:T(128)S(6)} %select_n.19), kind=kLoop, calls=%fused_computation.4 | loop fusion | bytes 4718596 | tf_op jit(solution)/shard_map/dynamic_slice | solution.py:415
  64.2 0.0 collective-permute-done.12.sib_ref
  64.2 0.8 %combine_local.1.total_ref = f32[192,1536]{1,0:T(8,128)S(1)} custom-call(bf16[192,384]{1,0:T(8,128)(2,1)S(1)} %get-tuple-element.34.own_ref, bf16[192,384]{1,0:T(8,128)(2,1)S(1)} %collective-permute-done.12.sib_ref, bf16[768,1536]{1,0:T(8,128)(2,1)S(1)} %constant_dynamic-slice_fusion.w_local_ref), custom_call_target="tpu_custom_call" | custom-call | tf_op jit(solution)/shard_map/combine_local/pallas_call | solution.py:468
  65.0 4.8 %collective-permute-done.13.across_ref = bf16[192,384]{1,0:T(8,128)(2,1)S(1)} collective-permute-done((bf16[192,384]{1,0:T(8,128)(2,1)S(1)}, bf16[192,384]{1,0:T(8,128)(2,1)S(1)}, u32[]{:S(2)}, u32[]{:S(2)}) %collective-permute-start.13) | collective-permute-done | bytes 147488 | tf_op jit(solution)/shard_map/ppermute | solution.py:332
  69.8 0.0 collective-permute-done.14.corner_ref
  69.8 0.0 collective-permute-done.15.w_corner_ref
  69.8 1.5 %combine.1 = bf16[192,1536]{1,0:T(8,128)(2,1)} custom-call(f32[192,1536]{1,0:T(8,128)S(1)} %combine_local.1.total_ref, bf16[192,384]{1,0:T(8,128)(2,1)S(1)} %collective-permute-done.13.across_ref, bf16[192,384]{1,0:T(8,128)(2,1)S(1)} %collective-permute-done.14.corner_ref, bf16[384,1536]{1,0:T(8,128)(2,1)S(1)} %collective-permute-done.4.w_across_ref, ...), custom_call_target="tpu_custom_call" | custom-call | tf_op jit(solution)/shard_map/combine/pallas_call | solution.py:476
  (5 shorter events, 0.0 us)
Async XLA Ops:
  0.0 27.8 %copy-start = (bf16[8,64]{1,0:T(8,128)(2,1)S(1)}, bf16[8,64]{1,0:T(8,128)(2,1)}, u32[]{:S(2)}) copy-start(bf16[8,64]{1,0:T(8,128)(2,1)} %refs_18_.1) | copy-start | bytes 3076
  0.0 27.8 %copy-start.2 = (f32[3072]{0:T(1024)S(1)}, f32[3072]{0:T(1024)}, u32[]{:S(2)}) copy-start(f32[3072]{0:T(1024)} %param.29) | copy-start | bytes 36868
  0.0 27.8 %copy-start.4 = (f32[128]{0:T(128)S(1)}, f32[128]{0:T(128)}, u32[]{:S(2)}) copy-start(f32[128]{0:T(128)} %param.33) | copy-start | bytes 1540
  0.0 27.8 %copy-start.5 = (f32[128]{0:T(128)S(1)}, f32[128]{0:T(128)}, u32[]{:S(2)}) copy-start(f32[128]{0:T(128)} %param.34) | copy-start | bytes 1540
  0.0 27.8 %copy-start.3 = (s32[16]{0:T(128)S(1)}, s32[16]{0:T(128)}, u32[]{:S(2)}) copy-start(s32[16]{0:T(128)} %refs_8_.1) | copy-start | bytes 196
  0.0 5.6 %collective-permute-start = (bf16[2,192,128]{2,1,0:T(8,128)(2,1)}, bf16[2,192,128]{2,1,0:T(8,128)(2,1)S(1)}, u32[]{:S(2)}, u32[]{:S(2)}) collective-permute-start(bf16[2,192,128]{2,1,0:T(8,128)(2,1)} %bitcast.10), channel_id=1, source_target_pairs={{0,1},{1,2},{2,3},{3,4},{4,5},{5,6},{6,7},{7,8},{8,9},{9,10},{10,1... | collective-permute-start | bytes 294920 | tf_op jit(solution)/shard_map/ppermute | solution.py:355
  6.8 8.7 %collective-permute-start.1 = (bf16[64,128]{1,0:T(8,128)(2,1)S(1)}, bf16[64,128]{1,0:T(8,128)(2,1)S(1)}, u32[]{:S(2)}, u32[]{:S(2)}) collective-permute-start(bf16[64,128]{1,0:T(8,128)(2,1)S(1)} %encode.1), channel_id=1, source_target_pairs={{0,8},{1,9},{2,10},{3,11},{4,12},{5,13},{6,14},{7,15},{8,0},{9,1},... | collective-permute-start | bytes 49160 | tf_op jit(solution)/shard_map/ppermute | solution.py:332
  12.4 3.7 %collective-permute-start.2 = (bf16[64,128]{1,0:T(8,128)(2,1)S(1)}, bf16[64,128]{1,0:T(8,128)(2,1)S(1)}, u32[]{:S(2)}, u32[]{:S(2)}) collective-permute-start(bf16[64,128]{1,0:T(8,128)(2,1)S(1)} %encode.1), channel_id=1, source_target_pairs={{0,4},{1,5},{2,6},{3,7},{4,0},{5,1},{6,2},{7,3},{8,12},{9,13},{10,... | collective-permute-start | bytes 49160 | tf_op jit(solution)/shard_map/ppermute | solution.py:332
  14.0 5.5 %collective-permute-start.3 = (bf16[64,128]{1,0:T(8,128)(2,1)S(1)}, bf16[64,128]{1,0:T(8,128)(2,1)S(1)}, u32[]{:S(2)}, u32[]{:S(2)}) collective-permute-start(bf16[64,128]{1,0:T(8,128)(2,1)S(1)} %encode.1), channel_id=1, source_target_pairs={{0,12},{1,13},{2,14},{3,15},{4,8},{5,9},{6,10},{7,11},{8,4},{9,5},... | collective-permute-start | bytes 49160 | tf_op jit(solution)/shard_map/ppermute | solution.py:332
  14.0 13.9 %copy-start.1 = (bf16[3,64,3072]{2,1,0:T(8,128)(2,1)S(1)}, bf16[3,64,3072]{2,1,0:T(8,128)(2,1)}, u32[]{:S(2)}) copy-start(bf16[3,64,3072]{2,1,0:T(8,128)(2,1)} %refs_11_.1) | copy-start | bytes 3538948
  19.5 4.3 %collective-permute-start.6 = (bf16[256,128]{1,0:T(8,128)(2,1)S(1)}, bf16[256,128]{1,0:T(8,128)(2,1)S(1)}, u32[]{:S(2)}, u32[]{:S(2)}) collective-permute-start(bf16[256,128]{1,0:T(8,128)(2,1)S(1)} %pad_maximum_fusion.refs_0_), channel_id=1, source_target_pairs={{0,16},{1,17},{2,18},{3,19},{4,20},{5,21},{6,22},{7,23},{8,24},{9,... | collective-permute-start | bytes 196616 | tf_op jit(solution)/shard_map/ppermute | solution.py:332
  21.0 5.3 %collective-permute-start.7 = (bf16[256,128]{1,0:T(8,128)(2,1)S(1)}, bf16[256,128]{1,0:T(8,128)(2,1)S(1)}, u32[]{:S(2)}, u32[]{:S(2)}) collective-permute-start(bf16[256,128]{1,0:T(8,128)(2,1)S(1)} %pad_maximum_fusion.refs_0_), channel_id=1, source_target_pairs={{0,18},{1,19},{2,16},{3,17},{4,22},{5,23},{6,20},{7,21},{8,26},{9,... | collective-permute-start | bytes 196616 | tf_op jit(solution)/shard_map/ppermute | solution.py:332
  21.6 5.0 %collective-permute-start.5 = (bf16[256,128]{1,0:T(8,128)(2,1)S(1)}, bf16[256,128]{1,0:T(8,128)(2,1)S(1)}, u32[]{:S(2)}, u32[]{:S(2)}) collective-permute-start(bf16[256,128]{1,0:T(8,128)(2,1)S(1)} %pad_maximum_fusion.refs_0_), channel_id=1, source_target_pairs={{0,2},{1,3},{2,0},{3,1},{4,6},{5,7},{6,4},{7,5},{8,10},{9,11},{10,... | collective-permute-start | bytes 196616 | tf_op jit(solution)/shard_map/ppermute | solution.py:332
  23.0 4.4 %collective-permute-start.8 = (bf16[256,128]{1,0:T(8,128)(2,1)S(1)}, bf16[256,128]{1,0:T(8,128)(2,1)S(1)}, u32[]{:S(2)}, u32[]{:S(2)}) collective-permute-start(bf16[256,128]{1,0:T(8,128)(2,1)S(1)} %pad_maximum_fusion.refs_0_), channel_id=1, source_target_pairs={{0,1},{1,0},{2,3},{3,2},{4,5},{5,4},{6,7},{7,6},{8,9},{9,8},{10,11... | collective-permute-start | bytes 196616 | tf_op jit(solution)/shard_map/ppermute | solution.py:332
  23.8 3.6 %collective-permute-start.10 = (bf16[256,128]{1,0:T(8,128)(2,1)S(1)}, bf16[256,128]{1,0:T(8,128)(2,1)S(1)}, u32[]{:S(2)}, u32[]{:S(2)}) collective-permute-start(bf16[256,128]{1,0:T(8,128)(2,1)S(1)} %collective-permute-done.6.refs_2_), channel_id=1, source_target_pairs={{0,1},{1,0},{2,3},{3,2},{4,5},{5,4},{6,7},{7,6},{8,9},{9,8},{10,11... | collective-permute-start | bytes 196616 | tf_op jit(solution)/shard_map/ppermute | solution.py:332
  26.3 1.3 %collective-permute-start.11 = (bf16[256,128]{1,0:T(8,128)(2,1)S(1)}, bf16[256,128]{1,0:T(8,128)(2,1)S(1)}, u32[]{:S(2)}, u32[]{:S(2)}) collective-permute-start(bf16[256,128]{1,0:T(8,128)(2,1)S(1)} %collective-permute-done.7.refs_3_), channel_id=1, source_target_pairs={{0,1},{1,0},{2,3},{3,2},{4,5},{5,4},{6,7},{7,6},{8,9},{9,8},{10,11... | collective-permute-start | bytes 196616 | tf_op jit(solution)/shard_map/ppermute | solution.py:332
  26.6 1.3 %collective-permute-start.9 = (bf16[256,128]{1,0:T(8,128)(2,1)S(1)}, bf16[256,128]{1,0:T(8,128)(2,1)S(1)}, u32[]{:S(2)}, u32[]{:S(2)}) collective-permute-start(bf16[256,128]{1,0:T(8,128)(2,1)S(1)} %collective-permute-done.5.refs_1_), channel_id=1, source_target_pairs={{0,1},{1,0},{2,3},{3,2},{4,5},{5,4},{6,7},{7,6},{8,9},{9,8},{10,11... | collective-permute-start | bytes 196616 | tf_op jit(solution)/shard_map/ppermute | solution.py:332
  26.8 33.1 %collective-permute-start.4 = (bf16[384,1536]{1,0:T(8,128)(2,1)S(1)}, bf16[384,1536]{1,0:T(8,128)(2,1)S(1)}, u32[]{:S(2)}, u32[]{:S(2)}) collective-permute-start(bf16[384,1536]{1,0:T(8,128)(2,1)S(1)} %dynamic_slice.6), channel_id=1, source_target_pairs={{0,16},{1,17},{2,18},{3,19},{4,20},{5,21},{6,22},{7,23},{8,24},{9,... | collective-permute-start | bytes 3538952 | tf_op jit(solution)/shard_map/ppermute | solution.py:332
  59.9 9.9 %collective-permute-start.15 = (bf16[384,1536]{1,0:T(8,128)(2,1)S(1)}, bf16[384,1536]{1,0:T(8,128)(2,1)S(1)}, u32[]{:S(2)}, u32[]{:S(2)}) collective-permute-start(bf16[384,1536]{1,0:T(8,128)(2,1)S(1)} %collective-permute-done.4.w_across_ref), channel_id=1, source_target_pairs={{0,1},{1,0},{2,3},{3,2},{4,5},{5,4},{6,7},{7,6},{8,9},{9,8},{10,11... | collective-permute-start | bytes 3538952 | tf_op jit(solution)/shard_map/ppermute | solution.py:332
  60.2 4.0 %collective-permute-start.12 = (bf16[192,384]{1,0:T(8,128)(2,1)S(1)}, bf16[192,384]{1,0:T(8,128)(2,1)S(1)}, u32[]{:S(2)}, u32[]{:S(2)}) collective-permute-start(bf16[192,384]{1,0:T(8,128)(2,1)S(1)} %get-tuple-element.35), channel_id=1, source_target_pairs={{0,1},{1,0},{2,3},{3,2},{4,5},{5,4},{6,7},{7,6},{8,9},{9,8},{10,11... | collective-permute-start | bytes 442376 | tf_op jit(solution)/shard_map/ppermute | solution.py:332
  60.5 9.3 %collective-permute-start.14 = (bf16[192,384]{1,0:T(8,128)(2,1)S(1)}, bf16[192,384]{1,0:T(8,128)(2,1)S(1)}, u32[]{:S(2)}, u32[]{:S(2)}) collective-permute-start(bf16[192,384]{1,0:T(8,128)(2,1)S(1)} %get-tuple-element.35), channel_id=1, source_target_pairs={{0,17},{1,16},{2,19},{3,18},{4,21},{5,20},{6,23},{7,22},{8,25},{9,... | collective-permute-start | bytes 442376 | tf_op jit(solution)/shard_map/ppermute | solution.py:332
  61.2 8.6 %collective-permute-start.13 = (bf16[192,384]{1,0:T(8,128)(2,1)S(1)}, bf16[192,384]{1,0:T(8,128)(2,1)S(1)}, u32[]{:S(2)}, u32[]{:S(2)}) collective-permute-start(bf16[192,384]{1,0:T(8,128)(2,1)S(1)} %get-tuple-element.34.own_ref), channel_id=1, source_target_pairs={{0,16},{1,17},{2,18},{3,19},{4,20},{5,21},{6,22},{7,23},{8,24},{9,... | collective-permute-start | bytes 442376 | tf_op jit(solution)/shard_map/ppermute | solution.py:332

commit v6 on v5

--- a/solution.py
+++ b/solution.py
@@ -118,12 +118,30 @@
         gram_ref[number * lanes : (number + 1) * lanes, :] = part
 
 
+def fold_kernel(wide_ref, gain_ref, w_value_ref, folded_ref, w_v_ref, semaphore):
+    depth = folded_ref.shape[1]
+    lanes, width = wide_ref.shape
+    start = pl.multiple_of((lax.axis_index("seq") % 2) * depth, depth)
+    copy = pltpu.make_async_copy(w_value_ref.at[:, pl.ds(start, depth)], w_v_ref, semaphore)
+    copy.start()
+    copy.wait()
+    total = jnp.zeros((lanes, depth), F32)
+    step = 512
+    for n in range(0, width, step):
+        values = wide_ref[:, n : n + step].astype(F32) * gain_ref[:, n : n + step]
+        stacked = jnp.concatenate(exact_parts(values), axis=0)
+        product = dot(stacked, w_v_ref[n : n + step, :])
+        total = total + (product[0:lanes] + (product[lanes : 2 * lanes] + product[2 * lanes :]))
+    for number, part in enumerate(exact_parts(total)):
+        folded_ref[number * lanes : (number + 1) * lanes, :] = part
+
+
 def joint_kernel(*refs, cells, block, pieces, owner_masks, tile, query_rows):
     near, far = refs[:pieces], refs[pieces : 2 * pieces]
     (
-        count_ref, wide_ref, gram_ref, w_hist_ref, gain_ref, w_query_ref, w_key_ref, w_value_ref,
+        count_ref, wide_ref, gram_ref, folded_ref, w_v_ref, w_hist_ref, gain_ref, w_query_ref, w_key_ref,
         q_gain_ref, k_gain_ref, hist_ref, own_ref, sib_ref,
-        patch_ref, w_q_ref, w_kv_ref, tok_a_ref, tok_b_ref, q_ref, k_ref, v_ref, s_a_ref,
+        patch_ref, w_q_ref, w_k_ref, tok_a_ref, tok_b_ref, q_ref, k_ref, v_ref, s_a_ref,
         s_b_ref, x_ref, out_ref, semaphores,
     ) = refs[2 * pieces :]
     heads, _, size = k_ref.shape
@@ -137,12 +155,7 @@
     start = pl.multiple_of((place % 2) * depth, depth)
     copies = [
         pltpu.make_async_copy(w_query_ref.at[:, pl.ds(start, depth)], w_q_ref, semaphores.at[0]),
-        pltpu.make_async_copy(
-            w_key_ref.at[:, pl.ds(start, depth)], w_kv_ref.at[:, 0:depth], semaphores.at[1]
-        ),
-        pltpu.make_async_copy(
-            w_value_ref.at[:, pl.ds(start, depth)], w_kv_ref.at[:, depth : 2 * depth], semaphores.at[2]
-        ),
+        pltpu.make_async_copy(w_key_ref.at[:, pl.ds(start, depth)], w_k_ref, semaphores.at[1]),
     ]
     for copy in copies:
         copy.start()
@@ -169,11 +182,17 @@
             at = (spot // 4) * rows + t * 4 * cells + (spot % 4) * cells
             patch_ref[at : at + cells, :] = jnp.where(lane < patch, moved, ones).astype(BF16)
 
+    def store_values(values, at):
+        for h in range(heads):
+            v_ref[h, pl.ds(at, values.shape[0]), :] = values[:, h * size : (h + 1) * size].astype(BF16)
+
     def tokens_of(i, tok_ref):
         source = patch_ref[pl.ds(pl.multiple_of(i * tile, tile), tile), :]
-        mixed = dot(jnp.concatenate([source] * 3, axis=1), gram_ref[...])
+        tripled = jnp.concatenate([source] * 3, axis=1)
+        mixed = dot(tripled, gram_ref[...])
         mean = jnp.sum(mixed * source.astype(F32), axis=1, keepdims=True) / width
         inverse = lax.rsqrt(mean + EPSILON)
+        store_values(dot(tripled, folded_ref[...]) * inverse, pl.multiple_of(i * tile, tile))
         for n in range(0, width, step):
             x = dot(source, wide_ref[:, n : n + step])
             tok_ref[:, n : n + step] = (x * inverse * gain_ref[:, n : n + step]).astype(BF16)
@@ -183,11 +202,11 @@
         return (values * lax.rsqrt(mean + EPSILON) * gain).astype(BF16)
 
     def project(tokens, at):
-        both = dot(tokens, w_kv_ref[...])
-        count = tokens.shape[0]
+        found = dot(tokens, w_k_ref[...])
         for h in range(heads):
-            k_ref[h, pl.ds(at, count), :] = head_norm(both[:, h * size : (h + 1) * size], k_gain_ref[...])
-            v_ref[h, pl.ds(at, count), :] = both[:, (heads + h) * size : (heads + h + 1) * size].astype(BF16)
+            k_ref[h, pl.ds(at, tokens.shape[0]), :] = head_norm(
+                found[:, h * size : (h + 1) * size], k_gain_ref[...]
+            )
 
     tokens_of(0, tok_a_ref)
     for copy in copies:
@@ -238,6 +257,7 @@
                 x_ref[0:count, n : n + step] * inverse * gain_ref[:, n : n + step]
             ).astype(BF16)
         project(tok_a_ref[0:count, :], section + r * slots)
+        store_values(dot(tok_a_ref[0:count, :], w_v_ref[...]), section + r * slots)
         slot = lax.broadcasted_iota(jnp.int32, (1, count), 1)
         live = jnp.zeros((1, count), jnp.int32)
         for o in range(len(taken)):
@@ -387,6 +407,17 @@
     columns = w_out.shape[1] // 2
     w_send = lax.dynamic_slice(w_out, (core * depth, (1 - group) * columns), (depth, columns))
 
+    folded, w_v = pl.pallas_call(
+        fold_kernel,
+        out_shape=[
+            jax.ShapeDtypeStruct((3 * lanes, depth), BF16), jax.ShapeDtypeStruct((width, depth), BF16)
+        ],
+        in_specs=[VMEM] * 2 + [pl.BlockSpec(memory_space=pltpu.HBM)],
+        out_specs=[VMEM] * 2,
+        scratch_shapes=[pltpu.SemaphoreType.DMA],
+        compiler_params=pltpu.CompilerParams(vmem_limit_bytes=10 * 2**20),
+        name="fold",
+    )(wide, norm_gain.reshape(1, width), *in_hbm(w_value))
     bits = []
     bit = seq_count // 2
     while bit > 1:
@@ -407,7 +438,7 @@
             near.append(flip(gathered, mask, seq_count))
         if number + 1 < len(rounds):
             gathered = jnp.concatenate(near, axis=0)
-            gathered, w_send = lax.optimization_barrier((gathered, w_send))
+            gathered, w_send, folded = lax.optimization_barrier((gathered, w_send, folded))
     far = [flip(near[0], 1, seq_count)]
     far += [flip(piece, 1, seq_count) for piece in near[1:]]
 
@@ -422,7 +453,7 @@
     while 2 * query_rows * keys * 4 > 12 * 2**20:
         query_rows //= 2
     limit = (
-        2 * tokens * lanes + 6 * width * depth + 4 * tile * width + 4 * keys * depth
+        2 * tokens * lanes + 4 * width * depth + 4 * tile * width + 4 * keys * depth
         + 8 * query_rows * keys + 512 * width + 4 * rows * depth + 12 * 2**20
     )
     anywhere = pl.BlockSpec(memory_space=pltpu.HBM)
@@ -432,12 +463,12 @@
             query_rows=query_rows,
         ),
         out_shape=[jax.ShapeDtypeStruct((rows // 2, depth), BF16)] * 2,
-        in_specs=[VMEM] * (2 * len(near)) + [SMEM] + [VMEM] * 4 + [anywhere] * 3 + [VMEM] * 3,
+        in_specs=[VMEM] * (2 * len(near)) + [SMEM] + [VMEM] * 6 + [anywhere] * 2 + [VMEM] * 3,
         out_specs=[VMEM] * 2,
         scratch_shapes=[
             pltpu.VMEM((tokens, lanes), BF16),
             pltpu.VMEM((width, depth), BF16),
-            pltpu.VMEM((width, 2 * depth), BF16),
+            pltpu.VMEM((width, depth), BF16),
             pltpu.VMEM((tile, width), BF16),
             pltpu.VMEM((tile, width), BF16),
             pltpu.VMEM((heads, rows, size), BF16),
@@ -447,7 +478,7 @@
             pltpu.VMEM((query_rows, keys), F32),
             pltpu.VMEM((128, width), F32),
             pltpu.VMEM((rows, depth), BF16),
-            pltpu.SemaphoreType.DMA((3,)),
+            pltpu.SemaphoreType.DMA((2,)),
         ],
         compiler_params=pltpu.CompilerParams(vmem_limit_bytes=limit),
         cost_estimate=pl.CostEstimate(
@@ -457,8 +488,8 @@
         ),
         name="joint",
     )(
-        *near, *far, hist_count, wide, gram, w_hist, norm_gain.reshape(1, width),
-        *in_hbm(w_query, w_key, w_value), q_gain.reshape(1, size), k_gain.reshape(1, size), hist,
+        *near, *far, hist_count, wide, gram, folded, w_v, w_hist, norm_gain.reshape(1, width),
+        *in_hbm(w_query, w_key), q_gain.reshape(1, size), k_gain.reshape(1, size), hist,
     )
     w_across, own, sib = lax.optimization_barrier((w_across, own, sib))
     w_corner = flip(w_across, 1, seq_count)

time: 71.8 us -> 67.2 us (0.936)
  waiting for transfers between devices: 12.9 us -> 9.7 us
  Pallas kernels: 37.1 us -> 35.8 us
    pallas_call x1, Pallas kernels: 32.1 us -> 27.6 us  [local(): pl.pallas_call(functools.partial(joint_kernel, cells=cells, block=block,...]
    pallas_call x0 -> x1, Pallas kernels: none -> 3.18 us  [local(): pl.pallas_call(fold_kernel, out_shape=[jax.ShapeDtypeStruct((3 * lanes, d...]
    ppermute x15, waiting for transfers between devices: 12.9 us -> 9.7 us  [flip(): return lax.ppermute(value, ('grp', 'seq'), pairs)]
  transfers between devices with their start and end apart: 16 -> 16, of which waited for: 8 -> 7; matrix products, arithmetic and copies ran while one was open for 6% -> 6% of each run, Pallas kernels for 48% -> 50%
where the time goes in v6:
time: 67.2 us; the launch traced here: 67 us
  Pallas kernels  35.8 us (53%)
  starting transfers between devices  16.5 us (25%)
  waiting for transfers between devices  9.7 us (14%)
  local copies, waits for them, and re-layouts  3.2 us (5%)
  between operations  0.97 us (1%)
  other arithmetic  0.83 us (1%)
    pallas_call x1, Pallas kernels, local(): pl.pallas_call(functools.partial(joint_kernel, cells=cells, block=block,...  27.6 us
    ppermute x15, starting transfers between devices, flip(): return lax.ppermute(value, ('grp', 'seq'), pairs)  14 us
    ppermute x15, waiting for transfers between devices, flip(): return lax.ppermute(value, ('grp', 'seq'), pairs)  9.7 us
    pallas_call x1, Pallas kernels, local(): pl.pallas_call(fold_kernel, out_shape=[jax.ShapeDtypeStruct((3 * lanes, d...  3.18 us
    ppermute x1, starting transfers between devices, local(): lax.ppermute(swapped, 'seq', [(i, i + 1) for i in range(seq_count - 1)])  2.52 us
    dynamic_slice x1, local copies, waits for them, and re-layouts, local(): w_local = lax.dynamic_slice_in_dim(w_out, group * columns, columns, axis=1)  1.82 us
    pallas_call x1, Pallas kernels, local(): pl.pallas_call(prepare_kernel, out_shape=[jax.ShapeDtypeStruct((lanes, wi...  1.62 us
    pallas_call x1, Pallas kernels, local(): pl.pallas_call(combine_kernel, out_shape=jax.ShapeDtypeStruct((rows // 2,...  1.49 us
  transfers between devices with their start and end apart: 16, of which 7 were waited for; matrix products, arithmetic and copies ran while one was open for 6% of the time, Pallas kernels for 50%

profile of v6, /device:TPU:0, one launch (start us, length us, event | category | flops | bytes accessed | tf_op | source)
XLA Modules:
  0.0 67.0 jit_solution(17303095756504061718)
XLA Ops:
  0.0 2.5 %collective-permute-start = (bf16[2,192,128]{2,1,0:T(8,128)(2,1)}, bf16[2,192,128]{2,1,0:T(8,128)(2,1)S(1)}, u32[]{:S(2)}, u32[]{:S(2)}) collective-permute-start(bf16[2,192,128]{2,1,0:T(8,128)(2,1)} %bitcast.11), channel_id=1, source_target_pairs={{0,1},{1,2},{2,3},{3,4},{4,5},{5,6},{6,7},{7,8},{8,9},{9,10},{10,1... | collective-permute-start | bytes 294920 | tf_op jit(solution)/shard_map/ppermute | solution.py:375
  3.2 0.8 %fusion = (f32[1,1536]{1,0:T(1,128)}, f32[1,1536]{1,0:T(1,128)}) fusion(f32[]{:T(128)} %bitcast.1), kind=kLoop, calls=%fused_computation.2 | loop fusion | flops 3072 | bytes 12292 | tf_op jit(solution)/shard_map/sin | solution.py:32
  4.0 1.6 %prepare.1 = (bf16[128,3072]{1,0:T(8,128)(2,1)S(1)}, bf16[384,128]{1,0:T(8,128)(2,1)S(1)}, f32[2,192,128]{2,1,0:T(8,128)S(1)}, bf16[2,128,128]{2,1,0:T(8,128)(2,...) custom-call(bf16[64,3072]{1,0:T(8,128)(2,1)} %w_in_ref.1, ...), custom_call_target="tpu_custom_call" | custom-call | tf_op jit(solution)/shard_map/prepare/pallas_call | solution.py:377
  5.6 0.0 collective-permute-done.earlier_ref
  5.6 1.1 %encode.1 = bf16[64,128]{1,0:T(8,128)(2,1)S(1)} custom-call(s32[1]{0:T(128)S(6)} %copy.19.step_ref, bf16[2,192,128]{2,1,0:T(8,128)(2,1)S(1)} %collective-permute-done.earlier_ref, f32[2,192,128]{2,1,0:T(8,128)S(1)} %get-tuple-element.26.partial_ref, bf16[2,128,128]{2,1,0:T(8,128)(2,1)S(1)} %get-tuple-element.27.weight_ref, ...), custom_call_target="tpu_custom_call" | custom-call | tf_op jit(solution)/shard_map/encode/pallas_call | solution.py:399
  6.7 5.6 %collective-permute-start.1 = (bf16[64,128]{1,0:T(8,128)(2,1)S(1)}, bf16[64,128]{1,0:T(8,128)(2,1)S(1)}, u32[]{:S(2)}, u32[]{:S(2)}) collective-permute-start(bf16[64,128]{1,0:T(8,128)(2,1)S(1)} %encode.1), channel_id=1, source_target_pairs={{0,8},{1,9},{2,10},{3,11},{4,12},{5,13},{6,14},{7,15},{8,0},{9,1},... | collective-permute-start | bytes 49160 | tf_op jit(solution)/shard_map/ppermute | solution.py:352
  12.4 1.6 %collective-permute-start.2 = (bf16[64,128]{1,0:T(8,128)(2,1)S(1)}, bf16[64,128]{1,0:T(8,128)(2,1)S(1)}, u32[]{:S(2)}, u32[]{:S(2)}) collective-permute-start(bf16[64,128]{1,0:T(8,128)(2,1)S(1)} %encode.1), channel_id=1, source_target_pairs={{0,4},{1,5},{2,6},{3,7},{4,0},{5,1},{6,2},{7,3},{8,12},{9,13},{10,... | collective-permute-start | bytes 49160 | tf_op jit(solution)/shard_map/ppermute | solution.py:352
  13.9 0.0 collective-permute-start.3
  13.9 1.3 %dynamic_slice.6 = bf16[384,1536]{1,0:T(8,128)(2,1)S(1)} dynamic-slice(bf16[768,3072]{1,0:T(8,128)(2,1)} %param.35, s32[]{:T(128)S(6)} %select_n.17, s32[]{:T(128)S(6)} %select_n.18), dynamic_slice_sizes={384,1536} | dynamic-slice | bytes 2359300 | tf_op jit(solution)/shard_map/dynamic_slice | solution.py:408
  15.3 0.0 copy-done
  15.3 0.0 copy-start.1
  15.3 0.0 copy-start.2
  15.3 0.0 copy-start.3
  15.3 0.0 copy-start.4
  15.3 0.0 copy-start.5
  15.4 3.2 %fold.1 = (bf16[384,384]{1,0:T(8,128)(2,1)S(1)}, bf16[3072,384]{1,0:T(8,128)(2,1)S(1)}) custom-call(bf16[128,3072]{1,0:T(8,128)(2,1)S(1)} %get-tuple-element.31.wide_ref.refs_9_, f32[1,3072]{1,0:T(1,128)S(1)} %bitcast.7, bf16[3072,768]{1,0:T(8,128)(2,1)} %w_value_ref.1), custom_call_target="tpu_custom_call" | custom-call | tf_op jit(solution)/shard_map/fold/pallas_call | solution.py:410
  18.5 0.0 collective-permute-done.1
  18.6 0.0 collective-permute-done.2
  18.6 0.9 %collective-permute-done.3 = bf16[64,128]{1,0:T(8,128)(2,1)S(1)} collective-permute-done((bf16[64,128]{1,0:T(8,128)(2,1)S(1)}, bf16[64,128]{1,0:T(8,128)(2,1)S(1)}, u32[]{:S(2)}, u32[]{:S(2)}) %collective-permute-start.3) | collective-permute-done | bytes 16416 | tf_op jit(solution)/shard_map/ppermute | solution.py:352
  19.5 1.5 %collective-permute-start.6 = (bf16[256,128]{1,0:T(8,128)(2,1)S(1)}, bf16[256,128]{1,0:T(8,128)(2,1)S(1)}, u32[]{:S(2)}, u32[]{:S(2)}) collective-permute-start(bf16[256,128]{1,0:T(8,128)(2,1)S(1)} %pad_maximum_fusion.refs_0_), channel_id=1, source_target_pairs={{0,16},{1,17},{2,18},{3,19},{4,20},{5,21},{6,22},{7,23},{8,24},{9,... | collective-permute-start | bytes 196616 | tf_op jit(solution)/shard_map/ppermute | solution.py:352
  21.0 0.6 collective-permute-start.7
  21.6 1.4 %collective-permute-start.5 = (bf16[256,128]{1,0:T(8,128)(2,1)S(1)}, bf16[256,128]{1,0:T(8,128)(2,1)S(1)}, u32[]{:S(2)}, u32[]{:S(2)}) collective-permute-start(bf16[256,128]{1,0:T(8,128)(2,1)S(1)} %pad_maximum_fusion.refs_0_), channel_id=1, source_target_pairs={{0,2},{1,3},{2,0},{3,1},{4,6},{5,7},{6,4},{7,5},{8,10},{9,11},{10,... | collective-permute-start | bytes 196616 | tf_op jit(solution)/shard_map/ppermute | solution.py:352
  23.0 0.0 collective-permute-start.8
  23.0 0.9 %collective-permute-done.6.refs_2_ = bf16[256,128]{1,0:T(8,128)(2,1)S(1)} collective-permute-done((bf16[256,128]{1,0:T(8,128)(2,1)S(1)}, bf16[256,128]{1,0:T(8,128)(2,1)S(1)}, u32[]{:S(2)}, u32[]{:S(2)}) %collective-permute-start.6) | collective-permute-done | bytes 65568 | tf_op jit(solution)/shard_map/ppermute | solution.py:352
  23.8 0.0 collective-permute-start.10
  23.8 2.4 %collective-permute-done.7.refs_3_ = bf16[256,128]{1,0:T(8,128)(2,1)S(1)} collective-permute-done((bf16[256,128]{1,0:T(8,128)(2,1)S(1)}, bf16[256,128]{1,0:T(8,128)(2,1)S(1)}, u32[]{:S(2)}, u32[]{:S(2)}) %collective-permute-start.7) | collective-permute-done | bytes 65568 | tf_op jit(solution)/shard_map/ppermute | solution.py:352
  26.2 0.0 collective-permute-start.11
  26.2 0.3 collective-permute-done.5.refs_1_
  26.5 0.2 collective-permute-start.9
  26.7 0.6 collective-permute-start.4
  27.4 0.0 collective-permute-done.8.refs_4_
  27.4 0.0 collective-permute-done.10.refs_6_
  27.4 0.1 collective-permute-done.11.refs_7_
  27.5 0.3 collective-permute-done.9.refs_5_
  27.8 0.0 copy-done.2
  27.8 27.6 %joint.1 = (bf16[192,384]{1,0:T(8,128)(2,1)S(1)}, bf16[192,384]{1,0:T(8,128)(2,1)S(1)}) custom-call(bf16[256,128]{1,0:T(8,128)(2,1)S(1)} %pad_maximum_fusion.refs_0_, bf16[256,128]{1,0:T(8,128)(2,1)S(1)} %collective-permute-done.5.refs_1_, bf16[256,128]{1,0:T(8,128)(2,1)S(1)} %collective-permute-done.6.refs_2_, ...), custom_call_target="tpu_custom_call" | custom-call | flops 24536678400 | bytes 7077888 | tf_op jit(solution)/shard_map/joint/pallas_call | solution.py:460
  55.4 0.0 collective-permute-done.4.w_across_ref
  55.4 0.3 collective-permute-start.15
  55.7 0.3 collective-permute-start.12
  56.0 0.7 %collective-permute-start.14 = (bf16[192,384]{1,0:T(8,128)(2,1)S(1)}, bf16[192,384]{1,0:T(8,128)(2,1)S(1)}, u32[]{:S(2)}, u32[]{:S(2)}) collective-permute-start(bf16[192,384]{1,0:T(8,128)(2,1)S(1)} %get-tuple-element.41), channel_id=1, source_target_pairs={{0,17},{1,16},{2,19},{3,18},{4,21},{5,20},{6,23},{7,22},{8,25},{9,... | collective-permute-start | bytes 442376 | tf_op jit(solution)/shard_map/ppermute | solution.py:352
  56.7 1.1 %collective-permute-start.13 = (bf16[192,384]{1,0:T(8,128)(2,1)S(1)}, bf16[192,384]{1,0:T(8,128)(2,1)S(1)}, u32[]{:S(2)}, u32[]{:S(2)}) collective-permute-start(bf16[192,384]{1,0:T(8,128)(2,1)S(1)} %get-tuple-element.40.own_ref), channel_id=1, source_target_pairs={{0,16},{1,17},{2,18},{3,19},{4,20},{5,21},{6,22},{7,23},{8,24},{9,... | collective-permute-start | bytes 442376 | tf_op jit(solution)/shard_map/ppermute | solution.py:352
  57.9 1.8 %constant_dynamic-slice_fusion.w_local_ref = bf16[768,1536]{1,0:T(8,128)(2,1)S(1)} fusion(bf16[768,3072]{1,0:T(8,128)(2,1)} %param.35, s32[]{:T(128)S(6)} %select_n.19), kind=kLoop, calls=%fused_computation.4 | loop fusion | bytes 4718596 | tf_op jit(solution)/shard_map/dynamic_slice | solution.py:446
  59.7 0.0 collective-permute-done.12.sib_ref
  59.7 0.8 %combine_local.1.total_ref = f32[192,1536]{1,0:T(8,128)S(1)} custom-call(bf16[192,384]{1,0:T(8,128)(2,1)S(1)} %get-tuple-element.40.own_ref, bf16[192,384]{1,0:T(8,128)(2,1)S(1)} %collective-permute-done.12.sib_ref, bf16[768,1536]{1,0:T(8,128)(2,1)S(1)} %constant_dynamic-slice_fusion.w_local_ref), custom_call_target="tpu_custom_call" | custom-call | tf_op jit(solution)/shard_map/combine_local/pallas_call | solution.py:499
  60.5 4.8 %collective-permute-done.13.across_ref = bf16[192,384]{1,0:T(8,128)(2,1)S(1)} collective-permute-done((bf16[192,384]{1,0:T(8,128)(2,1)S(1)}, bf16[192,384]{1,0:T(8,128)(2,1)S(1)}, u32[]{:S(2)}, u32[]{:S(2)}) %collective-permute-start.13) | collective-permute-done | bytes 147488 | tf_op jit(solution)/shard_map/ppermute | solution.py:352
  65.3 0.0 collective-permute-done.14.corner_ref
  65.3 0.0 collective-permute-done.15.w_corner_ref
  65.3 1.5 %combine.1 = bf16[192,1536]{1,0:T(8,128)(2,1)} custom-call(f32[192,1536]{1,0:T(8,128)S(1)} %combine_local.1.total_ref, bf16[192,384]{1,0:T(8,128)(2,1)S(1)} %collective-permute-done.13.across_ref, bf16[192,384]{1,0:T(8,128)(2,1)S(1)} %collective-permute-done.14.corner_ref, bf16[384,1536]{1,0:T(8,128)(2,1)S(1)} %collective-permute-done.4.w_across_ref, ...), custom_call_target="tpu_custom_call" | custom-call | tf_op jit(solution)/shard_map/combine/pallas_call | solution.py:507
  (6 shorter events, 0.0 us)
Async XLA Ops:
  0.0 15.3 %copy-start = (f32[3072]{0:T(1024)S(1)}, f32[3072]{0:T(1024)}, u32[]{:S(2)}) copy-start(f32[3072]{0:T(1024)} %param.29) | copy-start | bytes 36868
  0.0 5.6 %collective-permute-start = (bf16[2,192,128]{2,1,0:T(8,128)(2,1)}, bf16[2,192,128]{2,1,0:T(8,128)(2,1)S(1)}, u32[]{:S(2)}, u32[]{:S(2)}) collective-permute-start(bf16[2,192,128]{2,1,0:T(8,128)(2,1)} %bitcast.11), channel_id=1, source_target_pairs={{0,1},{1,2},{2,3},{3,4},{4,5},{5,6},{6,7},{7,8},{8,9},{9,10},{10,1... | collective-permute-start | bytes 294920 | tf_op jit(solution)/shard_map/ppermute | solution.py:375
  6.7 11.8 %collective-permute-start.1 = (bf16[64,128]{1,0:T(8,128)(2,1)S(1)}, bf16[64,128]{1,0:T(8,128)(2,1)S(1)}, u32[]{:S(2)}, u32[]{:S(2)}) collective-permute-start(bf16[64,128]{1,0:T(8,128)(2,1)S(1)} %encode.1), channel_id=1, source_target_pairs={{0,8},{1,9},{2,10},{3,11},{4,12},{5,13},{6,14},{7,15},{8,0},{9,1},... | collective-permute-start | bytes 49160 | tf_op jit(solution)/shard_map/ppermute | solution.py:352
  12.4 6.2 %collective-permute-start.2 = (bf16[64,128]{1,0:T(8,128)(2,1)S(1)}, bf16[64,128]{1,0:T(8,128)(2,1)S(1)}, u32[]{:S(2)}, u32[]{:S(2)}) collective-permute-start(bf16[64,128]{1,0:T(8,128)(2,1)S(1)} %encode.1), channel_id=1, source_target_pairs={{0,4},{1,5},{2,6},{3,7},{4,0},{5,1},{6,2},{7,3},{8,12},{9,13},{10,... | collective-permute-start | bytes 49160 | tf_op jit(solution)/shard_map/ppermute | solution.py:352
  13.9 5.5 %collective-permute-start.3 = (bf16[64,128]{1,0:T(8,128)(2,1)S(1)}, bf16[64,128]{1,0:T(8,128)(2,1)S(1)}, u32[]{:S(2)}, u32[]{:S(2)}) collective-permute-start(bf16[64,128]{1,0:T(8,128)(2,1)S(1)} %encode.1), channel_id=1, source_target_pairs={{0,12},{1,13},{2,14},{3,15},{4,8},{5,9},{6,10},{7,11},{8,4},{9,5},... | collective-permute-start | bytes 49160 | tf_op jit(solution)/shard_map/ppermute | solution.py:352
  15.3 12.5 %copy-start.1 = (bf16[8,64]{1,0:T(8,128)(2,1)S(1)}, bf16[8,64]{1,0:T(8,128)(2,1)}, u32[]{:S(2)}) copy-start(bf16[8,64]{1,0:T(8,128)(2,1)} %refs_19_.1) | copy-start | bytes 3076
  15.3 12.5 %copy-start.2 = (bf16[3,64,3072]{2,1,0:T(8,128)(2,1)S(1)}, bf16[3,64,3072]{2,1,0:T(8,128)(2,1)}, u32[]{:S(2)}) copy-start(bf16[3,64,3072]{2,1,0:T(8,128)(2,1)} %refs_13_.1) | copy-start | bytes 3538948
  15.3 12.5 %copy-start.3 = (s32[16]{0:T(128)S(1)}, s32[16]{0:T(128)}, u32[]{:S(2)}) copy-start(s32[16]{0:T(128)} %refs_8_.1) | copy-start | bytes 196
  15.3 12.5 %copy-start.4 = (f32[128]{0:T(128)S(1)}, f32[128]{0:T(128)}, u32[]{:S(2)}) copy-start(f32[128]{0:T(128)} %param.33) | copy-start | bytes 1540
  15.3 12.5 %copy-start.5 = (f32[128]{0:T(128)S(1)}, f32[128]{0:T(128)}, u32[]{:S(2)}) copy-start(f32[128]{0:T(128)} %param.34) | copy-start | bytes 1540
  19.5 4.3 %collective-permute-start.6 = (bf16[256,128]{1,0:T(8,128)(2,1)S(1)}, bf16[256,128]{1,0:T(8,128)(2,1)S(1)}, u32[]{:S(2)}, u32[]{:S(2)}) collective-permute-start(bf16[256,128]{1,0:T(8,128)(2,1)S(1)} %pad_maximum_fusion.refs_0_), channel_id=1, source_target_pairs={{0,16},{1,17},{2,18},{3,19},{4,20},{5,21},{6,22},{7,23},{8,24},{9,... | collective-permute-start | bytes 196616 | tf_op jit(solution)/shard_map/ppermute | solution.py:352
  21.0 5.3 %collective-permute-start.7 = (bf16[256,128]{1,0:T(8,128)(2,1)S(1)}, bf16[256,128]{1,0:T(8,128)(2,1)S(1)}, u32[]{:S(2)}, u32[]{:S(2)}) collective-permute-start(bf16[256,128]{1,0:T(8,128)(2,1)S(1)} %pad_maximum_fusion.refs_0_), channel_id=1, source_target_pairs={{0,18},{1,19},{2,16},{3,17},{4,22},{5,23},{6,20},{7,21},{8,26},{9,... | collective-permute-start | bytes 196616 | tf_op jit(solution)/shard_map/ppermute | solution.py:352
  21.6 5.0 %collective-permute-start.5 = (bf16[256,128]{1,0:T(8,128)(2,1)S(1)}, bf16[256,128]{1,0:T(8,128)(2,1)S(1)}, u32[]{:S(2)}, u32[]{:S(2)}) collective-permute-start(bf16[256,128]{1,0:T(8,128)(2,1)S(1)} %pad_maximum_fusion.refs_0_), channel_id=1, source_target_pairs={{0,2},{1,3},{2,0},{3,1},{4,6},{5,7},{6,4},{7,5},{8,10},{9,11},{10,... | collective-permute-start | bytes 196616 | tf_op jit(solution)/shard_map/ppermute | solution.py:352
  23.0 4.4 %collective-permute-start.8 = (bf16[256,128]{1,0:T(8,128)(2,1)S(1)}, bf16[256,128]{1,0:T(8,128)(2,1)S(1)}, u32[]{:S(2)}, u32[]{:S(2)}) collective-permute-start(bf16[256,128]{1,0:T(8,128)(2,1)S(1)} %pad_maximum_fusion.refs_0_), channel_id=1, source_target_pairs={{0,1},{1,0},{2,3},{3,2},{4,5},{5,4},{6,7},{7,6},{8,9},{9,8},{10,11... | collective-permute-start | bytes 196616 | tf_op jit(solution)/shard_map/ppermute | solution.py:352
  23.8 3.6 %collective-permute-start.10 = (bf16[256,128]{1,0:T(8,128)(2,1)S(1)}, bf16[256,128]{1,0:T(8,128)(2,1)S(1)}, u32[]{:S(2)}, u32[]{:S(2)}) collective-permute-start(bf16[256,128]{1,0:T(8,128)(2,1)S(1)} %collective-permute-done.6.refs_2_), channel_id=1, source_target_pairs={{0,1},{1,0},{2,3},{3,2},{4,5},{5,4},{6,7},{7,6},{8,9},{9,8},{10,11... | collective-permute-start | bytes 196616 | tf_op jit(solution)/shard_map/ppermute | solution.py:352
  26.2 1.3 %collective-permute-start.11 = (bf16[256,128]{1,0:T(8,128)(2,1)S(1)}, bf16[256,128]{1,0:T(8,128)(2,1)S(1)}, u32[]{:S(2)}, u32[]{:S(2)}) collective-permute-start(bf16[256,128]{1,0:T(8,128)(2,1)S(1)} %collective-permute-done.7.refs_3_), channel_id=1, source_target_pairs={{0,1},{1,0},{2,3},{3,2},{4,5},{5,4},{6,7},{7,6},{8,9},{9,8},{10,11... | collective-permute-start | bytes 196616 | tf_op jit(solution)/shard_map/ppermute | solution.py:352
  26.5 1.3 %collective-permute-start.9 = (bf16[256,128]{1,0:T(8,128)(2,1)S(1)}, bf16[256,128]{1,0:T(8,128)(2,1)S(1)}, u32[]{:S(2)}, u32[]{:S(2)}) collective-permute-start(bf16[256,128]{1,0:T(8,128)(2,1)S(1)} %collective-permute-done.5.refs_1_), channel_id=1, source_target_pairs={{0,1},{1,0},{2,3},{3,2},{4,5},{5,4},{6,7},{7,6},{8,9},{9,8},{10,11... | collective-permute-start | bytes 196616 | tf_op jit(solution)/shard_map/ppermute | solution.py:352
  26.7 28.7 %collective-permute-start.4 = (bf16[384,1536]{1,0:T(8,128)(2,1)S(1)}, bf16[384,1536]{1,0:T(8,128)(2,1)S(1)}, u32[]{:S(2)}, u32[]{:S(2)}) collective-permute-start(bf16[384,1536]{1,0:T(8,128)(2,1)S(1)} %dynamic_slice.6), channel_id=1, source_target_pairs={{0,16},{1,17},{2,18},{3,19},{4,20},{5,21},{6,22},{7,23},{8,24},{9,... | collective-permute-start | bytes 3538952 | tf_op jit(solution)/shard_map/ppermute | solution.py:352
  55.4 9.9 %collective-permute-start.15 = (bf16[384,1536]{1,0:T(8,128)(2,1)S(1)}, bf16[384,1536]{1,0:T(8,128)(2,1)S(1)}, u32[]{:S(2)}, u32[]{:S(2)}) collective-permute-start(bf16[384,1536]{1,0:T(8,128)(2,1)S(1)} %collective-permute-done.4.w_across_ref), channel_id=1, source_target_pairs={{0,1},{1,0},{2,3},{3,2},{4,5},{5,4},{6,7},{7,6},{8,9},{9,8},{10,11... | collective-permute-start | bytes 3538952 | tf_op jit(solution)/shard_map/ppermute | solution.py:352
  55.7 4.0 %collective-permute-start.12 = (bf16[192,384]{1,0:T(8,128)(2,1)S(1)}, bf16[192,384]{1,0:T(8,128)(2,1)S(1)}, u32[]{:S(2)}, u32[]{:S(2)}) collective-permute-start(bf16[192,384]{1,0:T(8,128)(2,1)S(1)} %get-tuple-element.41), channel_id=1, source_target_pairs={{0,1},{1,0},{2,3},{3,2},{4,5},{5,4},{6,7},{7,6},{8,9},{9,8},{10,11... | collective-permute-start | bytes 442376 | tf_op jit(solution)/shard_map/ppermute | solution.py:352
  56.0 9.3 %collective-permute-start.14 = (bf16[192,384]{1,0:T(8,128)(2,1)S(1)}, bf16[192,384]{1,0:T(8,128)(2,1)S(1)}, u32[]{:S(2)}, u32[]{:S(2)}) collective-permute-start(bf16[192,384]{1,0:T(8,128)(2,1)S(1)} %get-tuple-element.41), channel_id=1, source_target_pairs={{0,17},{1,16},{2,19},{3,18},{4,21},{5,20},{6,23},{7,22},{8,25},{9,... | collective-permute-start | bytes 442376 | tf_op jit(solution)/shard_map/ppermute | solution.py:352
  56.7 8.6 %collective-permute-start.13 = (bf16[192,384]{1,0:T(8,128)(2,1)S(1)}, bf16[192,384]{1,0:T(8,128)(2,1)S(1)}, u32[]{:S(2)}, u32[]{:S(2)}) collective-permute-start(bf16[192,384]{1,0:T(8,128)(2,1)S(1)} %get-tuple-element.40.own_ref), channel_id=1, source_target_pairs={{0,16},{1,17},{2,18},{3,19},{4,20},{5,21},{6,22},{7,23},{8,24},{9,... | collective-permute-start | bytes 442376 | tf_op jit(solution)/shard_map/ppermute | solution.py:352
